TPU v7x, 256 devices: a whole 4x4x8 slice. The times are simulated.
256 devices in a mesh: seq: 64 (over z, x, core), tp: 4 (over y).
Axes of the slice: x: 4, y: 4, z: 8, core: 2. Of those that a mesh axis runs over, the one named last changes fastest.
Arguments:
- hidden: bfloat16 [32768, 4096], P(('seq', 'tp')), may hold values from -640 to 640
- norm_gain: float32 [4096], replicated, may hold values from 0.5 to 1.5
- w_query: bfloat16 [4096, 2048], P(None, 'tp'), may hold values from -0.078125 to 0.078125
- w_key: bfloat16 [4096, 1024], P(None, 'tp'), may hold values from -2.421875 to 2.421875
- w_value: bfloat16 [4096, 1024], P(None, 'tp'), may hold values from -0.09375 to 0.09375
- doc_start: int32 [32768], P('seq'), may hold values from 0 to 32767, as said below
- block_owner: int32 [1024], P('seq'), may hold values from 0 to 63, as said below
Outputs:
- context_rows: bfloat16 [32768, 2048], P(('seq', 'tp'))
- key_cache: bfloat16 [49152, 1024], P('seq', 'tp')
- value_cache: bfloat16 [49152, 1024], P('seq', 'tp')
Inputs may be any that keep to these rules, and one draw needn't show every extreme that they name: `doc_start`: rows with equal values form one document: consecutive rows beginning at the row whose number is that value. Every document has at most 256 rows and one has exactly 256; all but the last have at least 64. `block_owner`: owner numbers never fall along the blocks. Owner o holds the blocks from o * 16 + e(o) up to (o + 1) * 16 + e(o + 1) - 1, where -4 <= e <= 4 and e is 0 at both ends of the axis; so an owner holds between 8 and 24 blocks, and some owner holds exactly 24.
All inputs are finite; a program needn't handle non-finite values.
Results may differ from a plain program's by a relative error of at most 0.0078.
Values may be sent and summed in bfloat16 or wider, within the bound.
No kernel may reach another device: no remote copies, remote signals or barrier semaphores. Data moves between devices by JAX's collectives and lax.ppermute only.
A program may use at most 128 MiB of HBM per device.

v0:
```python
import jax
import jax.numpy as jnp
from jax import lax
from jax.experimental import pallas as pl
from jax.experimental.pallas import tpu as pltpu
from jax.sharding import PartitionSpec as P


HD = 128
EPS = 1e-05
ROPE_BASE = 500000.0
CH = 128
VM = pltpu.MemorySpace.VMEM
HB = pltpu.MemorySpace.HBM


def ring(array, by):
    n = lax.axis_size("tp")
    return lax.ppermute(array, "tp", [(i, (i + by) % n) for i in range(n)])


def across(array, moves):
    homes, n = lax.axis_size("seq"), lax.axis_size("tp")
    pairs = [(h * n + t, (h + by) * n + t) for h in range(homes) for t, by in moves.items() if 0 <= h + by < homes]
    return lax.ppermute(array, ("seq", "tp"), pairs)


def swap(array, first):
    homes = lax.axis_size("seq")
    pairs = [p for h in range(first, homes - 1, 2) for p in ((h, h + 1), (h + 1, h))]
    return lax.ppermute(array, "seq", pairs)


def spots():
    me, home = lax.axis_index("tp"), lax.axis_index("seq")
    return [lax.rem(me + k, 4) for k in (0, 3, 1, 2)] + [home]


def vmem(x):
    return pltpu.with_memory_space_constraint(x, VM)


def call(body, outs, arrays, flops=0, owner=None, alias=None, scratch=()):
    smem = pl.BlockSpec(memory_space=pltpu.SMEM)
    inside = pl.BlockSpec(memory_space=VM)
    lead = [] if owner is None else [owner]
    moved = sum(x.size * x.dtype.itemsize for x in arrays)
    return pl.pallas_call(
        body,
        out_shape=[o if isinstance(o, jax.ShapeDtypeStruct) else VM(o, jnp.bfloat16) for o in outs],
        in_specs=[smem] * len(lead) + [inside] * len(arrays),
        out_specs=[
            pl.BlockSpec(memory_space=HB) if isinstance(o, jax.ShapeDtypeStruct) else inside for o in outs
        ],
        scratch_shapes=list(scratch),
        input_output_aliases={} if alias is None else {len(lead) + alias: 0},
        compiler_params=pltpu.CompilerParams(vmem_limit_bytes=12 << 20),
        cost_estimate=pl.CostEstimate(flops=flops, bytes_accessed=moved, transcendentals=0),
    )(*lead, *[vmem(x) for x in arrays])


def normalize(x, gain):
    wide = x.astype(jnp.float32)
    inverse = lax.rsqrt(jnp.mean(wide * wide, axis=1, keepdims=True) + EPS)
    return (wide * inverse * gain).astype(jnp.bfloat16)


def rotate(x, cosine, sine):
    heads = x.shape[1] // HD
    parts = []
    for i in range(heads):
        one = x[:, i * HD : (i + 1) * HD]
        parts.append((one * cosine + pltpu.roll(one, HD // 2, 1) * sine).astype(jnp.bfloat16))
    return parts


def dot(a, b):
    return jnp.dot(a, b, preferred_element_type=jnp.float32)


def project_kv(normed, wk, wv, cosine, sine):
    keys = rotate(dot(normed, wk[...]), cosine, sine)
    values = dot(normed, wv[...]).astype(jnp.bfloat16)
    return keys, values


def project_q(normed, wq, cosine, sine):
    parts = []
    for i in range(wq.shape[1] // 256):
        parts += rotate(dot(normed, wq[:, i * 256 : (i + 1) * 256]), cosine, sine)
    return parts


def run(copies):
    for copy in copies:
        copy.start()
    for copy in copies:
        copy.wait()


def weights_body(wq, wk, wv, after, wq_out, wk_out, wv_out, sems):
    run([pltpu.make_async_copy(w, out, sems.at[i]) for i, (w, out) in enumerate(((wq, wq_out), (wk, wk_out), (wv, wv_out)))])


def chunk_rows(at):
    return pl.ds(pl.multiple_of(at * CH, CH), CH)


def half_rows(at, offset):
    return pl.ds(pl.multiple_of(at * CH + offset, CH // 2), CH // 2)


def normalize_all(pieces, gain):
    return jnp.concatenate([normalize(piece[...], gain[...]) for piece in pieces], axis=0)


def put(ref, index, rows, parts):
    for i, part in enumerate(parts):
        ref[index, :, i * HD : (i + 1) * HD] = part[rows]


def kv_parts(normed, wk, wv, cosine, sine):
    keys, values = project_kv(normed, wk, wv, cosine, sine)
    return [*keys, values[:, :HD], values[:, HD:]]


def own_body(xa, xb, gain, wq, wk, wv, cosines, sines, ext, q_out):
    own = spots()[0]
    rows = chunk_rows(own)
    normed = normalize_all((xa, xb), gain)
    put(ext, 2 + own, slice(None), kv_parts(normed, wk, wv, cosines[rows], sines[rows]))
    for i, part in enumerate(project_q(normed, wq, cosines[rows], sines[rows])):
        q_out[:, i * HD : (i + 1) * HD] = part


def owned_part(part, live):
    return jnp.where(live, part, jnp.zeros_like(part))


def near_body(ext_in, la, rb, gain, wq, wk, wv, cosines, sines, ext, q_out):
    _, left, right, _, _ = spots()
    half = CH // 2
    first, second = half_rows(left, 0), half_rows(right, half)
    cosine = jnp.concatenate([cosines[first], cosines[second]], axis=0)
    sine = jnp.concatenate([sines[first], sines[second]], axis=0)
    normed = normalize_all((la, rb), gain)
    for i, part in enumerate(kv_parts(normed, wk, wv, cosine, sine)):
        ext[2 + left, 0:half, i * HD : (i + 1) * HD] = part[:half]
        ext[2 + right, half:CH, i * HD : (i + 1) * HD] = part[half:]
    for i, part in enumerate(project_q(normed, wq, cosine, sine)):
        q_out[:, i * HD : (i + 1) * HD] = part


def rest_turns(cosines, sines):
    _, left, right, _, _ = spots()
    half = CH // 2
    first, second = half_rows(right, 0), half_rows(left, half)
    cosine = jnp.concatenate([cosines[first], cosines[second]], axis=0)
    sine = jnp.concatenate([sines[first], sines[second]], axis=0)
    return cosine, sine


def rest_body(owner, ext_in, ra, lb, gain, wk, wv, cosines, sines, ext, normed_out, inside_out, outside_out):
    _, left, right, _, home = spots()
    half = CH // 2
    normed = normalize_all((ra, lb), gain)
    normed_out[...] = normed
    for i, part in enumerate(kv_parts(normed, wk, wv, *rest_turns(cosines, sines))):
        ext[2 + right, 0:half, i * HD : (i + 1) * HD] = part[:half]
        ext[2 + left, half:CH, i * HD : (i + 1) * HD] = part[half:]
    count = jnp.int32(0)
    for j in range(4):
        count += (owner[12 + j] == home + 1).astype(jnp.int32)

    def fill(to_right, to_left):
        to_right[0:CH] = ext[4]
        to_right[CH : 2 * CH] = ext[5]
        to_right[2 * CH :] = jnp.full((16, 512), count.astype(jnp.float32), jnp.float32).astype(jnp.bfloat16)
        for j in range(4):
            to_left[j * 32 : (j + 1) * 32] = owned_part(ext[2, j * 32 : (j + 1) * 32], owner[j] == home - 1)

    @pl.when(lax.rem(home, 2) == 0)
    def _():
        fill(inside_out, outside_out)

    @pl.when(lax.rem(home, 2) == 1)
    def _():
        fill(outside_out, inside_out)


def rest_q_body(normed, wq, cosines, sines, q_out):
    for i, part in enumerate(project_q(normed[...], wq, *rest_turns(cosines, sines))):
        q_out[:, i * HD : (i + 1) * HD] = part


def attend(tile, q, ext, docs):
    window = 3 * CH
    doc = docs[chunk_rows(tile), 0:1]
    key_row = lax.broadcasted_iota(jnp.int32, (CH, window), 1) + (tile - 2) * CH
    row = lax.broadcasted_iota(jnp.int32, (CH, window), 0) + tile * CH
    allowed = (key_row >= doc) & (key_row <= row)
    allowed = jnp.concatenate([allowed, allowed], axis=0)
    near = ext[pl.ds(tile, 3)].reshape(window, 512)
    outs = []
    for g in range(2):
        pair = jnp.concatenate(q[2 * g : 2 * g + 2], axis=0)
        keys, values = near[:, g * HD : (g + 1) * HD], near[:, (2 + g) * HD : (3 + g) * HD]
        scores = lax.dot_general(pair, keys, (((1,), (1,)), ((), ())), preferred_element_type=jnp.float32) * HD ** (-0.5)
        scores = jnp.where(allowed, scores, -jnp.inf)
        highest = jnp.max(scores, axis=1, keepdims=True)
        weights = jnp.exp(scores - highest)
        weights = (weights * (1.0 / jnp.sum(weights, axis=1, keepdims=True))).astype(jnp.bfloat16)
        blended = dot(weights, values).astype(jnp.bfloat16)
        outs += [blended[:CH], blended[CH:]]
    return outs


def heads(q):
    return [q[:, i * HD : (i + 1) * HD] for i in range(4)]


def emit(out, parts):
    for i, part in enumerate(parts):
        out[:, i * HD : (i + 1) * HD] = part


def first_body(ext_in, inner, outer, q_near, q_rest, docs, ext, out):
    _, _, right, _, home = spots()
    half = CH // 2

    @pl.when(lax.rem(home, 2) == 1)
    def _():
        ext[0] = inner[0:CH]
        ext[1] = inner[CH : 2 * CH]

    @pl.when(lax.rem(home, 2) == 0)
    def _():
        ext[0] = outer[0:CH]
        ext[1] = outer[CH : 2 * CH]

    q = jnp.concatenate([q_rest[0:half], q_near[half:CH]], axis=0)
    emit(out, attend(right, heads(q), ext, docs))


def last_body(owner, ext_in, xa, xb, gain, wk, wv, cosines, sines, ext, normed_out, late_out):
    _, _, _, far, home = spots()
    rows = chunk_rows(far)
    normed = normalize_all((xa, xb), gain)
    normed_out[...] = normed
    parts = kv_parts(normed, wk, wv, cosines[rows], sines[rows])
    put(ext, 2 + far, slice(None), parts)
    for j in range(4):
        live = (far > 0) | (owner[j] == home - 1)
        for i, part in enumerate(parts):
            late_out[j * 32 : (j + 1) * 32, i * HD : (i + 1) * HD] = owned_part(part[j * 32 : (j + 1) * 32], live)


def far_body(ext_in, normed, wq, cosines, sines, docs, ext, out):
    far = spots()[3]
    rows = chunk_rows(far)
    q = project_q(normed[...], wq, cosines[rows], sines[rows])
    emit(out, attend(far, q, ext, docs))


def left_body(ext_in, late, q_near, q_rest, docs, ext, out):
    own, left, _, _, _ = spots()
    half = CH // 2

    @pl.when(own < 2)
    def _():
        ext[own] = late[...]

    q = jnp.concatenate([q_near[0:half], q_rest[half:CH]], axis=0)
    emit(out, attend(left, heads(q), ext, docs))


def own_tile_body(owner, ext, late, inner, outer, q, docs, out, key_out, value_out, keys, values, sems):
    own, _, _, _, home = spots()

    def put_cache(row, part):
        keys[row : row + part.shape[0]] = part[:, 0:256]
        values[row : row + part.shape[0]] = part[:, 256:512]

    count = jnp.where(lax.rem(home, 2) == 1, inner[2 * CH : 2 * CH + 1, :], outer[2 * CH : 2 * CH + 1, :]).astype(jnp.float32)
    for j in range(4):
        part = ext[1, j * 32 : (j + 1) * 32]
        put_cache(j * 32, jnp.where(count > 3.5 - j, part.astype(jnp.float32), 0.0).astype(jnp.bfloat16))
    for j in range(16):
        part = ext[2 + j // 4, (j % 4) * 32 : (j % 4 + 1) * 32]
        put_cache(CH + j * 32, owned_part(part, owner[j] == home))

    @pl.when(own == 2)
    def _():
        put_cache(5 * CH, late[...])

    @pl.when((own != 2) & (lax.rem(home, 2) == 0))
    def _():
        put_cache(5 * CH, inner[0:CH])

    @pl.when((own != 2) & (lax.rem(home, 2) == 1))
    def _():
        put_cache(5 * CH, outer[0:CH])

    copies = [
        pltpu.make_async_copy(keys, key_out, sems.at[0]),
        pltpu.make_async_copy(values, value_out, sems.at[1]),
    ]
    for copy in copies:
        copy.start()
    emit(out, attend(own, heads(q), ext, docs))
    for copy in copies:
        copy.wait()


def join_body(s0, r1, r2, r3, out, sems):
    own, left, right, far, _ = spots()
    copies = []
    for i, (piece, at) in enumerate(((s0, own), (r1, left), (r2, far), (r3, right))):
        columns = pl.ds(pl.multiple_of(at * 512, 512), 512)
        copies.append(pltpu.make_async_copy(piece, out.at[:, columns], sems.at[i]))
    run(copies)


def layer(hidden, norm_gain, w_query, w_key, w_value, doc_start, block_owner):
    home = lax.axis_index("seq")
    rows = doc_start.shape[0]
    bf = jnp.bfloat16
    inside = pl.BlockSpec(memory_space=VM)
    outside = pl.BlockSpec(memory_space=pltpu.MemorySpace.HBM)
    wide = hidden.shape[1]

    def mover(body, outs, arrays, size):
        return pl.pallas_call(
            body,
            out_shape=[VM(s, bf) for s in outs],
            in_specs=[outside if x.size > CH * wide // 2 else pl.BlockSpec(memory_space=pl.ANY) for x in arrays],
            out_specs=[inside] * len(outs),
            scratch_shapes=[pltpu.SemaphoreType.DMA((len(outs),))],
            compiler_params=pltpu.CompilerParams(vmem_limit_bytes=2 << 20),
            cost_estimate=pl.CostEstimate(flops=0, bytes_accessed=size, transcendentals=0),
        )(*[pltpu.with_memory_space_constraint(x, HB) if x.size > CH * wide // 2 else x for x in arrays])

    own_a, own_b = hidden[: CH // 2], hidden[CH // 2 :]
    left_a = ring(own_a, 1)
    right_b = ring(own_b, -1)
    left_b = ring(own_b, 1)
    right_a = ring(own_a, -1)
    far_a = ring(left_a, 1)
    far_b = ring(right_b, -1)
    row_number = home * rows + jnp.arange(rows, dtype=jnp.int32)
    lane = jnp.arange(HD, dtype=jnp.float32)
    lane_half = jnp.where(lane < HD // 2, lane, lane - HD // 2)
    frequency = jnp.power(ROPE_BASE, -lane_half * (2.0 / HD))
    angles = (row_number - doc_start).astype(jnp.float32)[:, None] * frequency[None, :]
    cosines, sines = jnp.cos(angles), jnp.where(lane < HD // 2, -1.0, 1.0)[None, :] * jnp.sin(angles)
    docs = jnp.broadcast_to((doc_start - home * rows)[:, None], (rows, HD))

    w_query, w_key, w_value = mover(
        weights_body, [w.shape for w in (w_query, w_key, w_value)], [w_query, w_key, w_value, docs], 16 << 20
    )
    gain = norm_gain[None, :]
    flops = 2 * CH * wide * 1024
    scores = 8 * 2 * CH * 3 * CH * HD
    slots = (6, CH, 512)
    piece = (CH, 512)
    ext, q_own = call(own_body, [slots, piece], [own_a, own_b, gain, w_query, w_key, w_value, cosines, sines], flops)
    ext, q_near = call(
        near_body,
        [slots, piece],
        [ext, left_a, right_b, gain, w_query, w_key, w_value, cosines, sines],
        flops,
        alias=0,
    )
    ext, normed, inside_out, outside_out = call(
        rest_body,
        [slots, (CH, wide), (2 * CH + 16, 512), (2 * CH + 16, 512)],
        [ext, right_a, left_b, gain, w_key, w_value, cosines, sines],
        flops // 2,
        owner=block_owner,
        alias=0,
    )
    outer = swap(outside_out, 1)
    inner = swap(inside_out, 0)
    (q_rest,) = call(rest_q_body, [piece], [normed, w_query, cosines, sines], flops // 2)
    ext, normed, far = call(
        last_body,
        [slots, (CH, wide), piece],
        [ext, far_a, far_b, gain, w_key, w_value, cosines, sines],
        flops // 2,
        owner=block_owner,
        alias=0,
    )
    late = across(far, {0: 1, 1: 1, 2: -1})
    ext, s1 = call(first_body, [slots, piece], [ext, inner, outer, q_near, q_rest, docs], scores, alias=0)
    r1 = ring(s1, 1)
    ext, s2 = call(far_body, [slots, piece], [ext, normed, w_query, cosines, sines, docs], flops, alias=0)
    r2 = ring(s2, 2)
    ext, s3 = call(left_body, [slots, piece], [ext, late, q_near, q_rest, docs], scores, alias=0)
    r3 = ring(s3, 3)
    cache = jax.ShapeDtypeStruct((rows + 2 * CH, 256), bf)
    s0, key_cache, value_cache = call(
        own_tile_body,
        [piece, cache, cache],
        [ext, late, inner, outer, q_own, docs],
        scores,
        owner=block_owner,
        scratch=[VM((rows + 2 * CH, 256), bf)] * 2 + [pltpu.SemaphoreType.DMA((2,))],
    )
    (context,) = call(
        join_body,
        [jax.ShapeDtypeStruct((CH, 2048), bf)],
        [s0, r1, r2, r3],
        scratch=[pltpu.SemaphoreType.DMA((4,))],
    )
    return (context, key_cache, value_cache)


def solution(mesh):
    return jax.shard_map(
        layer,
        mesh=mesh,
        in_specs=(
            P(("seq", "tp"), None),
            P(),
            P(None, "tp"),
            P(None, "tp"),
            P(None, "tp"),
            P("seq"),
            P("seq"),
        ),
        out_specs=(P(("seq", "tp"), None), P("seq", "tp"), P("seq", "tp")),
        check_vma=False,
    )
```

profile of v0, /device:TPU:127, one launch (start us, length us, event | category | flops | bytes accessed | tf_op | source)
XLA Modules:
  0.0 59.9 jit_solution(15211211374448551640)
XLA Ops:
  0.6 1.3 %fusion.4 = (bf16[64,4096]{1,0:T(8,128)(2,1)S(1)}, bf16[64,4096]{1,0:T(8,128)(2,1)S(1)}) fusion(bf16[128,4096]{1,0:T(8,128)(2,1)} %param.7), kind=kLoop, calls=%fused_computation.11 | loop fusion | bytes 2097152 | tf_op jit(solution)/shard_map/slice | solution.py:343
  1.9 0.1 collective-permute-start
  2.0 1.5 %collective-permute-start.1 = (bf16[64,4096]{1,0:T(8,128)(2,1)S(1)}, bf16[64,4096]{1,0:T(8,128)(2,1)S(1)}, u32[]{:S(2)}, u32[]{:S(2)}) collective-permute-start(bf16[64,4096]{1,0:T(8,128)(2,1)S(1)} %get-tuple-element.49.xb), channel_id=1, source_target_pairs={{0,3},{1,0},{2,1},{3,2},{4,7},{5,4},{6,5},{7,6},{8,11},{9,8},{10,9... | collective-permute-start | bytes 1572872 | tf_op jit(solution)/shard_map/ppermute | solution.py:19
  3.5 0.5 collective-permute-start.2
  3.9 2.2 %collective-permute-start.3 = (bf16[64,4096]{1,0:T(8,128)(2,1)S(1)}, bf16[64,4096]{1,0:T(8,128)(2,1)S(1)}, u32[]{:S(2)}, u32[]{:S(2)}) collective-permute-start(bf16[64,4096]{1,0:T(8,128)(2,1)S(1)} %get-tuple-element.49.xb), channel_id=1, source_target_pairs={{0,1},{1,2},{2,3},{3,0},{4,5},{5,6},{6,7},{7,4},{8,9},{9,10},{10,1... | collective-permute-start | bytes 1572872 | tf_op jit(solution)/shard_map/ppermute | solution.py:19
  6.2 8.6 %collective-permute-done.la = bf16[64,4096]{1,0:T(8,128)(2,1)S(1)} collective-permute-done((bf16[64,4096]{1,0:T(8,128)(2,1)S(1)}, bf16[64,4096]{1,0:T(8,128)(2,1)S(1)}, u32[]{:S(2)}, u32[]{:S(2)}) %collective-permute-start) | collective-permute-done | bytes 524320 | tf_op jit(solution)/shard_map/ppermute | solution.py:19
  14.8 1.3 %collective-permute-start.4 = (bf16[64,4096]{1,0:T(8,128)(2,1)S(1)}, bf16[64,4096]{1,0:T(8,128)(2,1)S(1)}, u32[]{:S(2)}, u32[]{:S(2)}) collective-permute-start(bf16[64,4096]{1,0:T(8,128)(2,1)S(1)} %collective-permute-done.la), channel_id=1, source_target_pairs={{0,1},{1,2},{2,3},{3,0},{4,5},{5,6},{6,7},{7,4},{8,9},{9,10},{10,1... | collective-permute-start | bytes 1572872 | tf_op jit(solution)/shard_map/ppermute | solution.py:19
  16.1 0.2 collective-permute-start.5
  16.3 1.0 %fusion = (f32[512,128]{1,0:T(8,128)S(1)}, f32[512,128]{1,0:T(8,128)S(1)}) fusion(f32[128]{0:T(128)S(1)} %get-tuple-element.55, f32[128]{0:T(128)S(1)} %get-tuple-element.56, f32[512]{0:T(512)S(1)} %get-tuple-element.53), kind=kLoop, calls=%fused_computation.2 | loop fusion | flops 131072 | bytes 527360 | tf_op jit(solution)/shard_map/mul | solution.py:355
  17.3 0.1 broadcast_in_dim.21.after.docs
  17.4 3.5 %shard_map.94 = (bf16[4096,512]{1,0:T(8,128)(2,1)S(1)}, bf16[4096,256]{1,0:T(8,128)(2,1)S(1)}, bf16[4096,256]{1,0:T(8,128)(2,1)S(1)}) custom-call(bf16[4096,512]{1,0:T(8,128)(2,1)} %wq.1, bf16[4096,256]{1,0:T(8,128)(2,1)} %wk.1, bf16[4096,256]{1,0:T(8,128)(2,1)} %wv.1, s32[512,128]{1,0:T(8,128)S(1)} %broadcast_in_dim.21.after.docs), custom_call_target="tpu_custom_call" | custom-call | bytes 16777216 | tf_op jit(solution)/shard_map/pallas_call | solution.py:333
  20.9 1.6 %shard_map.95 = (bf16[6,128,512]{2,1,0:T(8,128)(2,1)S(1)}, bf16[128,512]{1,0:T(8,128)(2,1)S(1)}) custom-call(bf16[64,4096]{1,0:T(8,128)(2,1)S(1)} %get-tuple-element.50.xa, bf16[64,4096]{1,0:T(8,128)(2,1)S(1)} %get-tuple-element.49.xb, f32[1,4096]{1,0:T(1,128)S(1)} %bitcast.1, bf16[4096,512]{1,0:T(8,128)(2,1)S(1)} %get-tuple-element.26.wq, ...), custom_call_target="tpu_custom_call" | custom-call | flops 1073741824 | bytes 9977856 | tf_op jit(solution)/shard_map/pallas_call | solution.py:48
  22.6 1.6 %shard_map.96 = (bf16[6,128,512]{2,1,0:T(8,128)(2,1)S(1)}, bf16[128,512]{1,0:T(8,128)(2,1)S(1)}) custom-call(bf16[6,128,512]{2,1,0:T(8,128)(2,1)S(1)} %get-tuple-element.29.ext_in, bf16[64,4096]{1,0:T(8,128)(2,1)S(1)} %collective-permute-done.la, bf16[64,4096]{1,0:T(8,128)(2,1)S(1)} %collective-permute-done.1.rb, ...), custom_call_target="tpu_custom_call", output_to_operand_aliasing={{0}: (0, {})} | custom-call | flops 1073741824 | bytes 10764288 | tf_op jit(solution)/shard_map/pallas_call | solution.py:48
  24.2 3.0 %collective-permute-done.2.ra = bf16[64,4096]{1,0:T(8,128)(2,1)S(1)} collective-permute-done((bf16[64,4096]{1,0:T(8,128)(2,1)S(1)}, bf16[64,4096]{1,0:T(8,128)(2,1)S(1)}, u32[]{:S(2)}, u32[]{:S(2)}) %collective-permute-start.2) | collective-permute-done | bytes 524320 | tf_op jit(solution)/shard_map/ppermute | solution.py:19
  27.2 1.7 %shard_map.97 = (bf16[6,128,512]{2,1,0:T(8,128)(2,1)S(1)}, bf16[128,4096]{1,0:T(8,128)(2,1)S(1)}, bf16[272,512]{1,0:T(8,128)(2,1)S(1)}, bf16[272,512]{1,0:T(8,128)(2,1)S(1)}) custom-call(s32[16]{0:T(128)S(1)} %copy-done.1, bf16[6,128,512]{2,1,0:T(8,128)(2,1)S(1)} %get-tuple-element.30.ext_in, ...), custom_call_target="tpu_custom_call", output_to_operand_aliasing={{0}: (1, {})} | custom-call | flops 536870912 | bytes 6569984 | tf_op jit(solution)/shard_map/pallas_call | solution.py:48
  28.9 3.0 %collective-permute-start.6 = (bf16[272,512]{1,0:T(8,128)(2,1)S(1)}, bf16[272,512]{1,0:T(8,128)(2,1)S(1)}, u32[]{:S(2)}, u32[]{:S(2)}) collective-permute-start(bf16[272,512]{1,0:T(8,128)(2,1)S(1)} %get-tuple-element.33), channel_id=1, source_target_pairs={{0,4},{4,0},{8,12},{12,8},{16,20},{20,16},{24,28},{28,24},{32,36},... | collective-permute-start | bytes 835592 | tf_op jit(solution)/shard_map/ppermute | solution.py:31
  31.9 4.6 %collective-permute-start.7 = (bf16[272,512]{1,0:T(8,128)(2,1)S(1)}, bf16[272,512]{1,0:T(8,128)(2,1)S(1)}, u32[]{:S(2)}, u32[]{:S(2)}) collective-permute-start(bf16[272,512]{1,0:T(8,128)(2,1)S(1)} %get-tuple-element.34), channel_id=1, source_target_pairs={{4,8},{8,4},{12,16},{16,12},{20,24},{24,20},{28,32},{32,28},{36,40... | collective-permute-start | bytes 835592 | tf_op jit(solution)/shard_map/ppermute | solution.py:31
  36.5 0.8 %collective-permute-done.4.xa = bf16[64,4096]{1,0:T(8,128)(2,1)S(1)} collective-permute-done((bf16[64,4096]{1,0:T(8,128)(2,1)S(1)}, bf16[64,4096]{1,0:T(8,128)(2,1)S(1)}, u32[]{:S(2)}, u32[]{:S(2)}) %collective-permute-start.4) | collective-permute-done | bytes 524320 | tf_op jit(solution)/shard_map/ppermute | solution.py:19
  37.3 1.2 %collective-permute-done.5.xb = bf16[64,4096]{1,0:T(8,128)(2,1)S(1)} collective-permute-done((bf16[64,4096]{1,0:T(8,128)(2,1)S(1)}, bf16[64,4096]{1,0:T(8,128)(2,1)S(1)}, u32[]{:S(2)}, u32[]{:S(2)}) %collective-permute-start.5) | collective-permute-done | bytes 524320 | tf_op jit(solution)/shard_map/ppermute | solution.py:19
  38.4 1.6 %shard_map.98 = (bf16[6,128,512]{2,1,0:T(8,128)(2,1)S(1)}, bf16[128,4096]{1,0:T(8,128)(2,1)S(1)}, bf16[128,512]{1,0:T(8,128)(2,1)S(1)}) custom-call(s32[16]{0:T(128)S(1)} %copy-done.1, bf16[6,128,512]{2,1,0:T(8,128)(2,1)S(1)} %get-tuple-element.31.ext_in, bf16[64,4096]{1,0:T(8,128)(2,1)S(1)} %collective-permute-done.4.xa, ...), custom_call_target="tpu_custom_call", output_to_operand_aliasing={{0}: (1, {})} | custom-call | flops 536870912 | bytes 6569984 | tf_op jit(solution)/shard_map/pallas_call | solution.py:48
  40.1 0.8 %collective-permute-start.8 = (bf16[128,512]{1,0:T(8,128)(2,1)S(1)}, bf16[128,512]{1,0:T(8,128)(2,1)S(1)}, u32[]{:S(2)}, u32[]{:S(2)}) collective-permute-start(bf16[128,512]{1,0:T(8,128)(2,1)S(1)} %get-tuple-element.40), channel_id=1, source_target_pairs={{0,4},{1,5},{4,8},{5,9},{6,2},{8,12},{9,13},{10,6},{12,16},{13,17}... | collective-permute-start | bytes 393224 | tf_op jit(solution)/shard_map/ppermute | solution.py:25
  40.9 0.9 %shard_map.99.q_rest = bf16[128,512]{1,0:T(8,128)(2,1)S(1)} custom-call(bf16[128,4096]{1,0:T(8,128)(2,1)S(1)} %get-tuple-element.36.normed, bf16[4096,512]{1,0:T(8,128)(2,1)S(1)} %get-tuple-element.26.wq, f32[512,128]{1,0:T(8,128)S(1)} %get-tuple-element.52.cosines, f32[512,128]{1,0:T(8,128)S(1)} %get-tuple-element.51.sines), custom_call_target="tpu_custom_call" | custom-call | flops 536870912 | bytes 5767168 | tf_op jit(solution)/shard_map/pallas_call | solution.py:48
  41.8 1.2 %collective-permute-done.7.outer = bf16[272,512]{1,0:T(8,128)(2,1)S(1)} collective-permute-done((bf16[272,512]{1,0:T(8,128)(2,1)S(1)}, bf16[272,512]{1,0:T(8,128)(2,1)S(1)}, u32[]{:S(2)}, u32[]{:S(2)}) %collective-permute-start.7) | collective-permute-done | bytes 278560 | tf_op jit(solution)/shard_map/ppermute | solution.py:31
  43.1 1.0 %shard_map.100 = (bf16[6,128,512]{2,1,0:T(8,128)(2,1)S(1)}, bf16[128,512]{1,0:T(8,128)(2,1)S(1)}) custom-call(bf16[6,128,512]{2,1,0:T(8,128)(2,1)S(1)} %get-tuple-element.32.ext_in, bf16[272,512]{1,0:T(8,128)(2,1)S(1)} %collective-permute-done.6.inner, bf16[272,512]{1,0:T(8,128)(2,1)S(1)} %collective-permute-done.7.outer, ...), custom_call_target="tpu_custom_call", output_to_operand_aliasing={{0}: (0, {})} | custom-call | flops 100663296 | bytes 1867776 | tf_op jit(solution)/shard_map/pallas_call | solution.py:48
  44.1 1.7 %shard_map.101 = (bf16[6,128,512]{2,1,0:T(8,128)(2,1)S(1)}, bf16[128,512]{1,0:T(8,128)(2,1)S(1)}) custom-call(bf16[6,128,512]{2,1,0:T(8,128)(2,1)S(1)} %get-tuple-element.37.ext_in, bf16[128,4096]{1,0:T(8,128)(2,1)S(1)} %get-tuple-element.38.normed, bf16[4096,512]{1,0:T(8,128)(2,1)S(1)} %get-tuple-element.26.wq, ...), custom_call_target="tpu_custom_call", output_to_operand_aliasing={{0}: (0, {})} | custom-call | flops 1073741824 | bytes 6815744 | tf_op jit(solution)/shard_map/pallas_call | solution.py:48
  45.8 5.4 %collective-permute-start.10 = (bf16[128,512]{1,0:T(8,128)(2,1)S(1)}, bf16[128,512]{1,0:T(8,128)(2,1)S(1)}, u32[]{:S(2)}, u32[]{:S(2)}) collective-permute-start(bf16[128,512]{1,0:T(8,128)(2,1)S(1)} %get-tuple-element.45), channel_id=1, source_target_pairs={{0,2},{1,3},{2,0},{3,1},{4,6},{5,7},{6,4},{7,5},{8,10},{9,11},{10,... | collective-permute-start | bytes 393224 | tf_op jit(solution)/shard_map/ppermute | solution.py:19
  51.2 1.0 %shard_map.102 = (bf16[6,128,512]{2,1,0:T(8,128)(2,1)S(1)}, bf16[128,512]{1,0:T(8,128)(2,1)S(1)}) custom-call(bf16[6,128,512]{2,1,0:T(8,128)(2,1)S(1)} %get-tuple-element.39.ext_in, bf16[128,512]{1,0:T(8,128)(2,1)S(1)} %collective-permute-done.8.late, bf16[128,512]{1,0:T(8,128)(2,1)S(1)} %get-tuple-element.35.q_near, ...), custom_call_target="tpu_custom_call", output_to_operand_aliasing={{0}: (0, {})} | custom-call | flops 100663296 | bytes 1441792 | tf_op jit(solution)/shard_map/pallas_call | solution.py:48
  52.1 1.5 %collective-permute-start.11 = (bf16[128,512]{1,0:T(8,128)(2,1)S(1)}, bf16[128,512]{1,0:T(8,128)(2,1)S(1)}, u32[]{:S(2)}, u32[]{:S(2)}) collective-permute-start(bf16[128,512]{1,0:T(8,128)(2,1)S(1)} %get-tuple-element.46), channel_id=1, source_target_pairs={{0,3},{1,0},{2,1},{3,2},{4,7},{5,4},{6,5},{7,6},{8,11},{9,8},{10,9... | collective-permute-start | bytes 393224 | tf_op jit(solution)/shard_map/ppermute | solution.py:19
  53.7 1.6 %shard_map.103 = (bf16[128,512]{1,0:T(8,128)(2,1)S(1)}, bf16[768,256]{1,0:T(8,128)(2,1)}, bf16[768,256]{1,0:T(8,128)(2,1)}) custom-call(s32[16]{0:T(128)S(1)} %copy-done.1, bf16[6,128,512]{2,1,0:T(8,128)(2,1)S(1)} %get-tuple-element.41.ext, bf16[128,512]{1,0:T(8,128)(2,1)S(1)} %collective-permute-done.8.late, ...), custom_call_target="tpu_custom_call" | custom-call | flops 100663296 | bytes 1867776 | tf_op jit(solution)/shard_map/pallas_call | solution.py:48
  55.3 0.9 %collective-permute-done.9.r1 = bf16[128,512]{1,0:T(8,128)(2,1)S(1)} collective-permute-done((bf16[128,512]{1,0:T(8,128)(2,1)S(1)}, bf16[128,512]{1,0:T(8,128)(2,1)S(1)}, u32[]{:S(2)}, u32[]{:S(2)}) %collective-permute-start.9) | collective-permute-done | bytes 131104 | tf_op jit(solution)/shard_map/ppermute | solution.py:19
  56.2 2.7 %collective-permute-done.11.r3 = bf16[128,512]{1,0:T(8,128)(2,1)S(1)} collective-permute-done((bf16[128,512]{1,0:T(8,128)(2,1)S(1)}, bf16[128,512]{1,0:T(8,128)(2,1)S(1)}, u32[]{:S(2)}, u32[]{:S(2)}) %collective-permute-start.11) | collective-permute-done | bytes 131104 | tf_op jit(solution)/shard_map/ppermute | solution.py:19
  58.9 0.8 %shard_map.104 = bf16[128,2048]{1,0:T(8,128)(2,1)} custom-call(bf16[128,512]{1,0:T(8,128)(2,1)S(1)} %get-tuple-element.43.s0, bf16[128,512]{1,0:T(8,128)(2,1)S(1)} %collective-permute-done.9.r1, bf16[128,512]{1,0:T(8,128)(2,1)S(1)} %collective-permute-done.10.r2, bf16[128,512]{1,0:T(8,128)(2,1)S(1)} %collective-permute-done.11.r3), custom_call_target="tpu_custom_call" | custom-call | bytes 524288 | tf_op jit(solution)/shard_map/pallas_call | solution.py:48
  (14 shorter events, 0.0 us)
Async XLA Ops:
  0.6 5.5 %copy-start.2 = (s32[512]{0:T(512)S(1)}, s32[512]{0:T(512)}, u32[]{:S(2)}) copy-start(s32[512]{0:T(512)} %param.12) | copy-start | bytes 6148
  1.9 12.9 %collective-permute-start = (bf16[64,4096]{1,0:T(8,128)(2,1)S(1)}, bf16[64,4096]{1,0:T(8,128)(2,1)S(1)}, u32[]{:S(2)}, u32[]{:S(2)}) collective-permute-start(bf16[64,4096]{1,0:T(8,128)(2,1)S(1)} %get-tuple-element.50.xa), channel_id=1, source_target_pairs={{0,1},{1,2},{2,3},{3,0},{4,5},{5,6},{6,7},{7,4},{8,9},{9,10},{10,1... | collective-permute-start | bytes 1572872 | tf_op jit(solution)/shard_map/ppermute | solution.py:19
  2.0 14.1 %collective-permute-start.1 = (bf16[64,4096]{1,0:T(8,128)(2,1)S(1)}, bf16[64,4096]{1,0:T(8,128)(2,1)S(1)}, u32[]{:S(2)}, u32[]{:S(2)}) collective-permute-start(bf16[64,4096]{1,0:T(8,128)(2,1)S(1)} %get-tuple-element.49.xb), channel_id=1, source_target_pairs={{0,3},{1,0},{2,1},{3,2},{4,7},{5,4},{6,5},{7,6},{8,11},{9,8},{10,9... | collective-permute-start | bytes 1572872 | tf_op jit(solution)/shard_map/ppermute | solution.py:19
  3.5 23.7 %collective-permute-start.2 = (bf16[64,4096]{1,0:T(8,128)(2,1)S(1)}, bf16[64,4096]{1,0:T(8,128)(2,1)S(1)}, u32[]{:S(2)}, u32[]{:S(2)}) collective-permute-start(bf16[64,4096]{1,0:T(8,128)(2,1)S(1)} %get-tuple-element.50.xa), channel_id=1, source_target_pairs={{0,3},{1,0},{2,1},{3,2},{4,7},{5,4},{6,5},{7,6},{8,11},{9,8},{10,9... | collective-permute-start | bytes 1572872 | tf_op jit(solution)/shard_map/ppermute | solution.py:19
  3.9 23.3 %collective-permute-start.3 = (bf16[64,4096]{1,0:T(8,128)(2,1)S(1)}, bf16[64,4096]{1,0:T(8,128)(2,1)S(1)}, u32[]{:S(2)}, u32[]{:S(2)}) collective-permute-start(bf16[64,4096]{1,0:T(8,128)(2,1)S(1)} %get-tuple-element.49.xb), channel_id=1, source_target_pairs={{0,1},{1,2},{2,3},{3,0},{4,5},{5,6},{6,7},{7,4},{8,9},{9,10},{10,1... | collective-permute-start | bytes 1572872 | tf_op jit(solution)/shard_map/ppermute | solution.py:19
  14.8 22.5 %collective-permute-start.4 = (bf16[64,4096]{1,0:T(8,128)(2,1)S(1)}, bf16[64,4096]{1,0:T(8,128)(2,1)S(1)}, u32[]{:S(2)}, u32[]{:S(2)}) collective-permute-start(bf16[64,4096]{1,0:T(8,128)(2,1)S(1)} %collective-permute-done.la), channel_id=1, source_target_pairs={{0,1},{1,2},{2,3},{3,0},{4,5},{5,6},{6,7},{7,4},{8,9},{9,10},{10,1... | collective-permute-start | bytes 1572872 | tf_op jit(solution)/shard_map/ppermute | solution.py:19
  16.1 22.4 %collective-permute-start.5 = (bf16[64,4096]{1,0:T(8,128)(2,1)S(1)}, bf16[64,4096]{1,0:T(8,128)(2,1)S(1)}, u32[]{:S(2)}, u32[]{:S(2)}) collective-permute-start(bf16[64,4096]{1,0:T(8,128)(2,1)S(1)} %collective-permute-done.1.rb), channel_id=1, source_target_pairs={{0,3},{1,0},{2,1},{3,2},{4,7},{5,4},{6,5},{7,6},{8,11},{9,8},{10,9... | collective-permute-start | bytes 1572872 | tf_op jit(solution)/shard_map/ppermute | solution.py:19
  17.4 3.5 %copy-start = (f32[4096]{0:T(1024)S(1)}, f32[4096]{0:T(1024)}, u32[]{:S(2)}) copy-start(f32[4096]{0:T(1024)} %param.8) | copy-start | bytes 49156
  22.6 4.6 %copy-start.1 = (s32[16]{0:T(128)S(1)}, s32[16]{0:T(128)}, u32[]{:S(2)}) copy-start(s32[16]{0:T(128)} %owner.5) | copy-start | bytes 196
  28.9 13.0 %collective-permute-start.6 = (bf16[272,512]{1,0:T(8,128)(2,1)S(1)}, bf16[272,512]{1,0:T(8,128)(2,1)S(1)}, u32[]{:S(2)}, u32[]{:S(2)}) collective-permute-start(bf16[272,512]{1,0:T(8,128)(2,1)S(1)} %get-tuple-element.33), channel_id=1, source_target_pairs={{0,4},{4,0},{8,12},{12,8},{16,20},{20,16},{24,28},{28,24},{32,36},... | collective-permute-start | bytes 835592 | tf_op jit(solution)/shard_map/ppermute | solution.py:31
  31.9 11.2 %collective-permute-start.7 = (bf16[272,512]{1,0:T(8,128)(2,1)S(1)}, bf16[272,512]{1,0:T(8,128)(2,1)S(1)}, u32[]{:S(2)}, u32[]{:S(2)}) collective-permute-start(bf16[272,512]{1,0:T(8,128)(2,1)S(1)} %get-tuple-element.34), channel_id=1, source_target_pairs={{4,8},{8,4},{12,16},{16,12},{20,24},{24,20},{28,32},{32,28},{36,40... | collective-permute-start | bytes 835592 | tf_op jit(solution)/shard_map/ppermute | solution.py:31
  40.1 11.1 %collective-permute-start.8 = (bf16[128,512]{1,0:T(8,128)(2,1)S(1)}, bf16[128,512]{1,0:T(8,128)(2,1)S(1)}, u32[]{:S(2)}, u32[]{:S(2)}) collective-permute-start(bf16[128,512]{1,0:T(8,128)(2,1)S(1)} %get-tuple-element.40), channel_id=1, source_target_pairs={{0,4},{1,5},{4,8},{5,9},{6,2},{8,12},{9,13},{10,6},{12,16},{13,17}... | collective-permute-start | bytes 393224 | tf_op jit(solution)/shard_map/ppermute | solution.py:25
  45.8 9.5 %collective-permute-start.10 = (bf16[128,512]{1,0:T(8,128)(2,1)S(1)}, bf16[128,512]{1,0:T(8,128)(2,1)S(1)}, u32[]{:S(2)}, u32[]{:S(2)}) collective-permute-start(bf16[128,512]{1,0:T(8,128)(2,1)S(1)} %get-tuple-element.45), channel_id=1, source_target_pairs={{0,2},{1,3},{2,0},{3,1},{4,6},{5,7},{6,4},{7,5},{8,10},{9,11},{10,... | collective-permute-start | bytes 393224 | tf_op jit(solution)/shard_map/ppermute | solution.py:19
  51.1 5.0 %collective-permute-start.9 = (bf16[128,512]{1,0:T(8,128)(2,1)S(1)}, bf16[128,512]{1,0:T(8,128)(2,1)S(1)}, u32[]{:S(2)}, u32[]{:S(2)}) collective-permute-start(bf16[128,512]{1,0:T(8,128)(2,1)S(1)} %get-tuple-element.44), channel_id=1, source_target_pairs={{0,1},{1,2},{2,3},{3,0},{4,5},{5,6},{6,7},{7,4},{8,9},{9,10},{10,1... | collective-permute-start | bytes 393224 | tf_op jit(solution)/shard_map/ppermute | solution.py:19
  52.1 6.8 %collective-permute-start.11 = (bf16[128,512]{1,0:T(8,128)(2,1)S(1)}, bf16[128,512]{1,0:T(8,128)(2,1)S(1)}, u32[]{:S(2)}, u32[]{:S(2)}) collective-permute-start(bf16[128,512]{1,0:T(8,128)(2,1)S(1)} %get-tuple-element.46), channel_id=1, source_target_pairs={{0,3},{1,0},{2,1},{3,2},{4,7},{5,4},{6,5},{7,6},{8,11},{9,8},{10,9... | collective-permute-start | bytes 393224 | tf_op jit(solution)/shard_map/ppermute | solution.py:19
where the time goes:
time: 60 us; the launch traced here: 59.9 us
  starting transfers between devices  21.1 us (35%)
  waiting for transfers between devices  18.5 us (31%)
  Pallas kernels  17 us (28%)
  local copies, waits for them, and re-layouts  1.41 us (2%)
  other arithmetic  1.01 us (2%)
  between operations  0.96 us (2%)
    ppermute x9, waiting for transfers between devices, ring(): return lax.ppermute(array, 'tp', [(i, (i + by) % n) for i in range(n)])  17.2 us
    pallas_call x10, Pallas kernels, call(): pl.pallas_call(body, out_shape=[o if isinstance(o, jax.ShapeDtypeStruct)...  13.5 us
    ppermute x9, starting transfers between devices, ring(): return lax.ppermute(array, 'tp', [(i, (i + by) % n) for i in range(n)])  12.6 us
    ppermute x2, starting transfers between devices, swap(): return lax.ppermute(array, 'seq', pairs)  7.6 us
    pallas_call x1, Pallas kernels, mover(): pl.pallas_call(body, out_shape=[VM(s, bf) for s in outs], in_specs=[outsi...  3.51 us
    slice x1, local copies, waits for them, and re-layouts, layer(): own_a, own_b = (hidden[:CH // 2], hidden[CH // 2:])  1.27 us
    ppermute x2, waiting for transfers between devices, swap(): return lax.ppermute(array, 'seq', pairs)  1.24 us
  transfers between devices with their start and end apart: 12, of which 7 were waited for; matrix products, arithmetic and copies ran while one was open for 2% of the time, Pallas kernels for 27%

commit v1 on v0

--- a/solution.py
+++ b/solution.py
@@ -10,6 +10,7 @@
 EPS = 1e-05
 ROPE_BASE = 500000.0
 CH = 128
+BLK = 32
 VM = pltpu.MemorySpace.VMEM
 HB = pltpu.MemorySpace.HBM
 
@@ -40,23 +41,21 @@
     return pltpu.with_memory_space_constraint(x, VM)
 
 
-def call(body, outs, arrays, flops=0, owner=None, alias=None, scratch=()):
-    smem = pl.BlockSpec(memory_space=pltpu.SMEM)
+def call(body, outs, arrays, flops=0, alias=None, scratch=()):
     inside = pl.BlockSpec(memory_space=VM)
-    lead = [] if owner is None else [owner]
     moved = sum(x.size * x.dtype.itemsize for x in arrays)
     return pl.pallas_call(
         body,
         out_shape=[o if isinstance(o, jax.ShapeDtypeStruct) else VM(o, jnp.bfloat16) for o in outs],
-        in_specs=[smem] * len(lead) + [inside] * len(arrays),
+        in_specs=[inside] * len(arrays),
         out_specs=[
             pl.BlockSpec(memory_space=HB) if isinstance(o, jax.ShapeDtypeStruct) else inside for o in outs
         ],
         scratch_shapes=list(scratch),
-        input_output_aliases={} if alias is None else {len(lead) + alias: 0},
+        input_output_aliases={} if alias is None else {alias: 0},
         compiler_params=pltpu.CompilerParams(vmem_limit_bytes=12 << 20),
         cost_estimate=pl.CostEstimate(flops=flops, bytes_accessed=moved, transcendentals=0),
-    )(*lead, *[vmem(x) for x in arrays])
+    )(*[vmem(x) for x in arrays])
 
 
 def normalize(x, gain):
@@ -98,7 +97,7 @@
         copy.wait()
 
 
-def weights_body(wq, wk, wv, after, wq_out, wk_out, wv_out, sems):
+def weights_body(wq, wk, wv, after, after_too, wq_out, wk_out, wv_out, sems):
     run([pltpu.make_async_copy(w, out, sems.at[i]) for i, (w, out) in enumerate(((wq, wq_out), (wk, wk_out), (wv, wv_out)))])
 
 
@@ -134,7 +133,8 @@
 
 
 def owned_part(part, live):
-    return jnp.where(live, part, jnp.zeros_like(part))
+    live = jnp.concatenate([live] * (part.shape[1] // HD), axis=1)
+    return jnp.where(live, part.astype(jnp.float32), 0.0).astype(jnp.bfloat16)
 
 
 def near_body(ext_in, la, rb, gain, wq, wk, wv, cosines, sines, ext, q_out):
@@ -160,7 +160,7 @@
     return cosine, sine
 
 
-def rest_body(owner, ext_in, ra, lb, gain, wk, wv, cosines, sines, ext, normed_out, inside_out, outside_out):
+def rest_body(ext_in, owners, ra, lb, gain, wk, wv, cosines, sines, ext, normed_out, inside_out, outside_out):
     _, left, right, _, home = spots()
     half = CH // 2
     normed = normalize_all((ra, lb), gain)
@@ -168,16 +168,14 @@
     for i, part in enumerate(kv_parts(normed, wk, wv, *rest_turns(cosines, sines))):
         ext[2 + right, 0:half, i * HD : (i + 1) * HD] = part[:half]
         ext[2 + left, half:CH, i * HD : (i + 1) * HD] = part[half:]
-    count = jnp.int32(0)
-    for j in range(4):
-        count += (owner[12 + j] == home + 1).astype(jnp.int32)
+    count = jnp.sum(jnp.where(owners[3 * CH :] == home + 1, 1.0 / 32, 0.0), axis=0, keepdims=True)
+    count = jnp.broadcast_to(jnp.concatenate([count] * 4, axis=1), (16, 512)).astype(jnp.bfloat16)
 
     def fill(to_right, to_left):
         to_right[0:CH] = ext[4]
         to_right[CH : 2 * CH] = ext[5]
-        to_right[2 * CH :] = jnp.full((16, 512), count.astype(jnp.float32), jnp.float32).astype(jnp.bfloat16)
-        for j in range(4):
-            to_left[j * 32 : (j + 1) * 32] = owned_part(ext[2, j * 32 : (j + 1) * 32], owner[j] == home - 1)
+        to_right[2 * CH :] = count
+        to_left[0:CH] = owned_part(ext[2], owners[0:CH] == home - 1)
 
     @pl.when(lax.rem(home, 2) == 0)
     def _():
@@ -224,9 +222,9 @@
         out[:, i * HD : (i + 1) * HD] = part
 
 
-def first_body(ext_in, inner, outer, q_near, q_rest, docs, ext, out):
-    _, _, right, _, home = spots()
-    half = CH // 2
+def far_body(ext_in, inner, outer, normed, wq, cosines, sines, docs, ext, out):
+    _, _, _, far, home = spots()
+    rows = chunk_rows(far)
 
     @pl.when(lax.rem(home, 2) == 1)
     def _():
@@ -238,28 +236,27 @@
         ext[0] = outer[0:CH]
         ext[1] = outer[CH : 2 * CH]
 
-    q = jnp.concatenate([q_rest[0:half], q_near[half:CH]], axis=0)
-    emit(out, attend(right, heads(q), ext, docs))
-
-
-def last_body(owner, ext_in, xa, xb, gain, wk, wv, cosines, sines, ext, normed_out, late_out):
+    q = project_q(normed[...], wq, cosines[rows], sines[rows])
+    emit(out, attend(far, q, ext, docs))
+
+
+def last_body(ext_in, owners, xa, xb, gain, wk, wv, cosines, sines, ext, normed_out, late_out):
     _, _, _, far, home = spots()
     rows = chunk_rows(far)
     normed = normalize_all((xa, xb), gain)
     normed_out[...] = normed
     parts = kv_parts(normed, wk, wv, cosines[rows], sines[rows])
     put(ext, 2 + far, slice(None), parts)
-    for j in range(4):
-        live = (far > 0) | (owner[j] == home - 1)
-        for i, part in enumerate(parts):
-            late_out[j * 32 : (j + 1) * 32, i * HD : (i + 1) * HD] = owned_part(part[j * 32 : (j + 1) * 32], live)
-
-
-def far_body(ext_in, normed, wq, cosines, sines, docs, ext, out):
-    far = spots()[3]
-    rows = chunk_rows(far)
-    q = project_q(normed[...], wq, cosines[rows], sines[rows])
-    emit(out, attend(far, q, ext, docs))
+    live = (owners[0:CH] == home - 1) | (far > 0)
+    for i, part in enumerate(parts):
+        late_out[:, i * HD : (i + 1) * HD] = owned_part(part, live)
+
+
+def first_body(ext_in, q_near, q_rest, docs, ext, out):
+    right = spots()[2]
+    half = CH // 2
+    q = jnp.concatenate([q_rest[0:half], q_near[half:CH]], axis=0)
+    emit(out, attend(right, heads(q), ext, docs))
 
 
 def left_body(ext_in, late, q_near, q_rest, docs, ext, out):
@@ -274,7 +271,7 @@
     emit(out, attend(left, heads(q), ext, docs))
 
 
-def own_tile_body(owner, ext, late, inner, outer, q, docs, out, key_out, value_out, keys, values, sems):
+def own_tile_body(ext, owners, late, inner, outer, q, docs, out, key_out, value_out, keys, values, sems):
     own, _, _, _, home = spots()
 
     def put_cache(row, part):
@@ -285,9 +282,8 @@
     for j in range(4):
         part = ext[1, j * 32 : (j + 1) * 32]
         put_cache(j * 32, jnp.where(count > 3.5 - j, part.astype(jnp.float32), 0.0).astype(jnp.bfloat16))
-    for j in range(16):
-        part = ext[2 + j // 4, (j % 4) * 32 : (j % 4 + 1) * 32]
-        put_cache(CH + j * 32, owned_part(part, owner[j] == home))
+    for j in range(4):
+        put_cache(CH + j * CH, owned_part(ext[2 + j], owners[j * CH : (j + 1) * CH] == home))
 
     @pl.when(own == 2)
     def _():
@@ -354,9 +350,10 @@
     angles = (row_number - doc_start).astype(jnp.float32)[:, None] * frequency[None, :]
     cosines, sines = jnp.cos(angles), jnp.where(lane < HD // 2, -1.0, 1.0)[None, :] * jnp.sin(angles)
     docs = jnp.broadcast_to((doc_start - home * rows)[:, None], (rows, HD))
+    owners = jnp.broadcast_to(block_owner[:, None, None], (block_owner.shape[0], BLK, HD)).reshape(rows, HD)
 
     w_query, w_key, w_value = mover(
-        weights_body, [w.shape for w in (w_query, w_key, w_value)], [w_query, w_key, w_value, docs], 16 << 20
+        weights_body, [w.shape for w in (w_query, w_key, w_value)], [w_query, w_key, w_value, docs, owners], 16 << 20
     )
     gain = norm_gain[None, :]
     flops = 2 * CH * wide * 1024
@@ -374,9 +371,8 @@
     ext, normed, inside_out, outside_out = call(
         rest_body,
         [slots, (CH, wide), (2 * CH + 16, 512), (2 * CH + 16, 512)],
-        [ext, right_a, left_b, gain, w_key, w_value, cosines, sines],
+        [ext, owners, right_a, left_b, gain, w_key, w_value, cosines, sines],
         flops // 2,
-        owner=block_owner,
         alias=0,
     )
     outer = swap(outside_out, 1)
@@ -385,25 +381,23 @@
     ext, normed, far = call(
         last_body,
         [slots, (CH, wide), piece],
-        [ext, far_a, far_b, gain, w_key, w_value, cosines, sines],
+        [ext, owners, far_a, far_b, gain, w_key, w_value, cosines, sines],
         flops // 2,
-        owner=block_owner,
         alias=0,
     )
     late = across(far, {0: 1, 1: 1, 2: -1})
-    ext, s1 = call(first_body, [slots, piece], [ext, inner, outer, q_near, q_rest, docs], scores, alias=0)
+    ext, s2 = call(far_body, [slots, piece], [ext, inner, outer, normed, w_query, cosines, sines, docs], flops, alias=0)
+    r2 = ring(s2, 2)
+    ext, s1 = call(first_body, [slots, piece], [ext, q_near, q_rest, docs], scores, alias=0)
     r1 = ring(s1, 1)
-    ext, s2 = call(far_body, [slots, piece], [ext, normed, w_query, cosines, sines, docs], flops, alias=0)
-    r2 = ring(s2, 2)
     ext, s3 = call(left_body, [slots, piece], [ext, late, q_near, q_rest, docs], scores, alias=0)
     r3 = ring(s3, 3)
     cache = jax.ShapeDtypeStruct((rows + 2 * CH, 256), bf)
     s0, key_cache, value_cache = call(
         own_tile_body,
         [piece, cache, cache],
-        [ext, late, inner, outer, q_own, docs],
+        [ext, owners, late, inner, outer, q_own, docs],
         scores,
-        owner=block_owner,
         scratch=[VM((rows + 2 * CH, 256), bf)] * 2 + [pltpu.SemaphoreType.DMA((2,))],
     )
     (context,) = call(

time: 60 us -> 60.6 us (1.010)
  the two profiles are of different devices: /device:TPU:127 before, /device:TPU:128 now
where the time goes in v1:
time: 60.6 us; the launch traced here: 59.7 us
  starting transfers between devices  21.1 us (35%)
  Pallas kernels  17.7 us (29%)
  waiting for transfers between devices  17.2 us (28%)
  local copies, waits for them, and re-layouts  1.69 us (3%)
  other arithmetic  1.01 us (2%)
  between operations  1 us (2%)
    ppermute x9, waiting for transfers between devices, ring(): return lax.ppermute(array, 'tp', [(i, (i + by) % n) for i in range(n)])  16.9 us
    ppermute x9, starting transfers between devices, ring(): return lax.ppermute(array, 'tp', [(i, (i + by) % n) for i in range(n)])  14.6 us
    pallas_call x10, Pallas kernels, call(): pl.pallas_call(body, out_shape=[o if isinstance(o, jax.ShapeDtypeStruct)...  14.2 us
    ppermute x2, starting transfers between devices, swap(): return lax.ppermute(array, 'seq', pairs)  4.39 us
    pallas_call x1, Pallas kernels, mover(): pl.pallas_call(body, out_shape=[VM(s, bf) for s in outs], in_specs=[outsi...  3.51 us
    ppermute x1, starting transfers between devices, across(): return lax.ppermute(array, ('seq', 'tp'), pairs)  2.1 us
    slice x1, local copies, waits for them, and re-layouts, layer(): own_a, own_b = (hidden[:CH // 2], hidden[CH // 2:])  1.28 us
  transfers between devices with their start and end apart: 12, of which 6 were waited for; matrix products, arithmetic and copies ran while one was open for 2% of the time, Pallas kernels for 28%

profile of v1, /device:TPU:128, one launch (start us, length us, event | category | flops | bytes accessed | tf_op | source)
XLA Modules:
  0.0 59.7 jit_solution(17054444034973783530)
XLA Ops:
  0.7 1.3 %fusion.4 = (bf16[64,4096]{1,0:T(8,128)(2,1)S(1)}, bf16[64,4096]{1,0:T(8,128)(2,1)S(1)}) fusion(bf16[128,4096]{1,0:T(8,128)(2,1)} %param.7), kind=kLoop, calls=%fused_computation.11 | loop fusion | bytes 2097152 | tf_op jit(solution)/shard_map/slice | solution.py:339
  1.9 1.7 %collective-permute-start = (bf16[64,4096]{1,0:T(8,128)(2,1)S(1)}, bf16[64,4096]{1,0:T(8,128)(2,1)}, u32[]{:S(2)}, u32[]{:S(2)}) collective-permute-start(bf16[64,4096]{1,0:T(8,128)(2,1)S(1)} %get-tuple-element.50.xa), channel_id=1, source_target_pairs={{0,1},{1,2},{2,3},{3,0},{4,5},{5,6},{6,7},{7,4},{8,9},{9,10},{10,1... | collective-permute-start | bytes 1572872 | tf_op jit(solution)/shard_map/ppermute | solution.py:20
  3.6 1.7 %collective-permute-start.1 = (bf16[64,4096]{1,0:T(8,128)(2,1)S(1)}, bf16[64,4096]{1,0:T(8,128)(2,1)}, u32[]{:S(2)}, u32[]{:S(2)}) collective-permute-start(bf16[64,4096]{1,0:T(8,128)(2,1)S(1)} %get-tuple-element.49.xb), channel_id=1, source_target_pairs={{0,3},{1,0},{2,1},{3,2},{4,7},{5,4},{6,5},{7,6},{8,11},{9,8},{10,9... | collective-permute-start | bytes 1572872 | tf_op jit(solution)/shard_map/ppermute | solution.py:20
  5.2 1.8 %collective-permute-start.2 = (bf16[64,4096]{1,0:T(8,128)(2,1)S(1)}, bf16[64,4096]{1,0:T(8,128)(2,1)S(1)}, u32[]{:S(2)}, u32[]{:S(2)}) collective-permute-start(bf16[64,4096]{1,0:T(8,128)(2,1)S(1)} %get-tuple-element.50.xa), channel_id=1, source_target_pairs={{0,3},{1,0},{2,1},{3,2},{4,7},{5,4},{6,5},{7,6},{8,11},{9,8},{10,9... | collective-permute-start | bytes 1572872 | tf_op jit(solution)/shard_map/ppermute | solution.py:20
  7.1 0.2 collective-permute-start.3
  7.3 10.8 %collective-permute-done.la = bf16[64,4096]{1,0:T(8,128)(2,1)} collective-permute-done((bf16[64,4096]{1,0:T(8,128)(2,1)S(1)}, bf16[64,4096]{1,0:T(8,128)(2,1)}, u32[]{:S(2)}, u32[]{:S(2)}) %collective-permute-start) | collective-permute-done | bytes 524320 | tf_op jit(solution)/shard_map/ppermute | solution.py:20
  18.1 0.4 collective-permute-start.4
  18.5 2.9 %collective-permute-start.5 = (bf16[64,4096]{1,0:T(8,128)(2,1)}, bf16[64,4096]{1,0:T(8,128)(2,1)}, u32[]{:S(2)}, u32[]{:S(2)}) collective-permute-start(bf16[64,4096]{1,0:T(8,128)(2,1)} %collective-permute-done.1.rb), channel_id=1, source_target_pairs={{0,3},{1,0},{2,1},{3,2},{4,7},{5,4},{6,5},{7,6},{8,11},{9,8},{10,9... | collective-permute-start | bytes 1572872 | tf_op jit(solution)/shard_map/ppermute | solution.py:20
  21.4 1.0 %fusion = (f32[512,128]{1,0:T(8,128)S(1)}, f32[512,128]{1,0:T(8,128)S(1)}) fusion(f32[128]{0:T(128)S(1)} %get-tuple-element.55, f32[128]{0:T(128)S(1)} %get-tuple-element.56, f32[512]{0:T(512)S(1)} %get-tuple-element.53), kind=kLoop, calls=%fused_computation.2 | loop fusion | flops 131072 | bytes 527360 | tf_op jit(solution)/shard_map/mul | solution.py:351
  22.5 0.1 broadcast_in_dim.31.after.docs
  22.7 0.1 broadcast_in_dim.34.after_too.owners
  22.8 3.5 %shard_map.94 = (bf16[4096,512]{1,0:T(8,128)(2,1)S(1)}, bf16[4096,256]{1,0:T(8,128)(2,1)S(1)}, bf16[4096,256]{1,0:T(8,128)(2,1)S(1)}) custom-call(bf16[4096,512]{1,0:T(8,128)(2,1)} %wq.1, bf16[4096,256]{1,0:T(8,128)(2,1)} %wk.1, bf16[4096,256]{1,0:T(8,128)(2,1)} %wv.1, s32[512,128]{1,0:T(8,128)S(1)} %broadcast_in_dim.31.after.docs, ...), custom_call_target="tpu_custom_call" | custom-call | bytes 16777216 | tf_op jit(solution)/shard_map/pallas_call | solution.py:329
  26.3 1.6 %shard_map.95 = (bf16[6,128,512]{2,1,0:T(8,128)(2,1)S(1)}, bf16[128,512]{1,0:T(8,128)(2,1)S(1)}) custom-call(bf16[64,4096]{1,0:T(8,128)(2,1)S(1)} %get-tuple-element.50.xa, bf16[64,4096]{1,0:T(8,128)(2,1)S(1)} %get-tuple-element.49.xb, f32[1,4096]{1,0:T(1,128)S(1)} %bitcast.1, bf16[4096,512]{1,0:T(8,128)(2,1)S(1)} %get-tuple-element.26.wq, ...), custom_call_target="tpu_custom_call" | custom-call | flops 1073741824 | bytes 9977856 | tf_op jit(solution)/shard_map/pallas_call | solution.py:47
  28.0 2.8 %shard_map.96 = (bf16[6,128,512]{2,1,0:T(8,128)(2,1)S(1)}, bf16[128,512]{1,0:T(8,128)(2,1)S(1)}) custom-call(bf16[6,128,512]{2,1,0:T(8,128)(2,1)S(1)} %get-tuple-element.29.ext_in, bf16[64,4096]{1,0:T(8,128)(2,1)} %collective-permute-done.la, bf16[64,4096]{1,0:T(8,128)(2,1)} %collective-permute-done.1.rb, ...), custom_call_target="tpu_custom_call", output_to_operand_aliasing={{0}: (0, {})} | custom-call | flops 1073741824 | bytes 10764288 | tf_op jit(solution)/shard_map/pallas_call | solution.py:47
  30.8 1.1 %shard_map.97 = (bf16[6,128,512]{2,1,0:T(8,128)(2,1)S(1)}, bf16[128,4096]{1,0:T(8,128)(2,1)S(1)}, bf16[272,512]{1,0:T(8,128)(2,1)S(1)}, bf16[272,512]{1,0:T(8,128)(2,1)S(1)}) custom-call(bf16[6,128,512]{2,1,0:T(8,128)(2,1)S(1)} %get-tuple-element.30.ext_in, s32[512,128]{1,0:T(8,128)S(1)} %broadcast_in_dim.34.after_too.owners, ...), custom_call_target="tpu_custom_call", output_to_operand_aliasing={{0}: (0, {})} | custom-call | flops 536870912 | bytes 6832128 | tf_op jit(solution)/shard_map/pallas_call | solution.py:47
  32.0 4.3 %collective-permute-start.7 = (bf16[272,512]{1,0:T(8,128)(2,1)S(1)}, bf16[272,512]{1,0:T(8,128)(2,1)S(1)}, u32[]{:S(2)}, u32[]{:S(2)}) collective-permute-start(bf16[272,512]{1,0:T(8,128)(2,1)S(1)} %get-tuple-element.34), channel_id=1, source_target_pairs={{4,8},{8,4},{12,16},{16,12},{20,24},{24,20},{28,32},{32,28},{36,40... | collective-permute-start | bytes 835592 | tf_op jit(solution)/shard_map/ppermute | solution.py:32
  36.3 3.1 %collective-permute-done.4.xa = bf16[64,4096]{1,0:T(8,128)(2,1)S(1)} collective-permute-done((bf16[64,4096]{1,0:T(8,128)(2,1)}, bf16[64,4096]{1,0:T(8,128)(2,1)S(1)}, u32[]{:S(2)}, u32[]{:S(2)}) %collective-permute-start.4) | collective-permute-done | bytes 524320 | tf_op jit(solution)/shard_map/ppermute | solution.py:20
  39.4 0.1 collective-permute-done.5.xb
  39.5 2.1 %shard_map.98 = (bf16[6,128,512]{2,1,0:T(8,128)(2,1)S(1)}, bf16[128,4096]{1,0:T(8,128)(2,1)S(1)}, bf16[128,512]{1,0:T(8,128)(2,1)S(1)}) custom-call(bf16[6,128,512]{2,1,0:T(8,128)(2,1)S(1)} %get-tuple-element.31.ext_in, s32[512,128]{1,0:T(8,128)S(1)} %broadcast_in_dim.34.after_too.owners, ...), custom_call_target="tpu_custom_call", output_to_operand_aliasing={{0}: (0, {})} | custom-call | flops 536870912 | bytes 6832128 | tf_op jit(solution)/shard_map/pallas_call | solution.py:47
  41.7 2.1 %collective-permute-start.8 = (bf16[128,512]{1,0:T(8,128)(2,1)S(1)}, bf16[128,512]{1,0:T(8,128)(2,1)S(1)}, u32[]{:S(2)}, u32[]{:S(2)}) collective-permute-start(bf16[128,512]{1,0:T(8,128)(2,1)S(1)} %get-tuple-element.40), channel_id=1, source_target_pairs={{0,4},{1,5},{4,8},{5,9},{6,2},{8,12},{9,13},{10,6},{12,16},{13,17}... | collective-permute-start | bytes 393224 | tf_op jit(solution)/shard_map/ppermute | solution.py:26
  43.8 0.8 %shard_map.100.q_rest = bf16[128,512]{1,0:T(8,128)(2,1)S(1)} custom-call(bf16[128,4096]{1,0:T(8,128)(2,1)S(1)} %get-tuple-element.38.normed, bf16[4096,512]{1,0:T(8,128)(2,1)S(1)} %get-tuple-element.26.wq, f32[512,128]{1,0:T(8,128)S(1)} %get-tuple-element.52.cosines, f32[512,128]{1,0:T(8,128)S(1)} %get-tuple-element.51.sines), custom_call_target="tpu_custom_call" | custom-call | flops 536870912 | bytes 5767168 | tf_op jit(solution)/shard_map/pallas_call | solution.py:47
  44.6 1.7 %shard_map.99 = (bf16[6,128,512]{2,1,0:T(8,128)(2,1)S(1)}, bf16[128,512]{1,0:T(8,128)(2,1)S(1)}) custom-call(bf16[6,128,512]{2,1,0:T(8,128)(2,1)S(1)} %get-tuple-element.32.ext_in, bf16[272,512]{1,0:T(8,128)(2,1)S(1)} %collective-permute-done.6.inner, bf16[272,512]{1,0:T(8,128)(2,1)S(1)} %collective-permute-done.7.outer, ...), custom_call_target="tpu_custom_call", output_to_operand_aliasing={{0}: (0, {})} | custom-call | flops 1073741824 | bytes 7372800 | tf_op jit(solution)/shard_map/pallas_call | solution.py:47
  46.4 1.0 %shard_map.101 = (bf16[6,128,512]{2,1,0:T(8,128)(2,1)S(1)}, bf16[128,512]{1,0:T(8,128)(2,1)S(1)}) custom-call(bf16[6,128,512]{2,1,0:T(8,128)(2,1)S(1)} %get-tuple-element.36.ext_in, bf16[128,512]{1,0:T(8,128)(2,1)S(1)} %get-tuple-element.37.q_near, bf16[128,512]{1,0:T(8,128)(2,1)S(1)} %shard_map.100.q_rest, ...), custom_call_target="tpu_custom_call", output_to_operand_aliasing={{0}: (0, {})} | custom-call | flops 100663296 | bytes 1310720 | tf_op jit(solution)/shard_map/pallas_call | solution.py:47
  47.4 1.7 %collective-permute-start.9 = (bf16[128,512]{1,0:T(8,128)(2,1)S(1)}, bf16[128,512]{1,0:T(8,128)(2,1)S(1)}, u32[]{:S(2)}, u32[]{:S(2)}) collective-permute-start(bf16[128,512]{1,0:T(8,128)(2,1)S(1)} %get-tuple-element.44), channel_id=1, source_target_pairs={{0,1},{1,2},{2,3},{3,0},{4,5},{5,6},{6,7},{7,4},{8,9},{9,10},{10,1... | collective-permute-start | bytes 393224 | tf_op jit(solution)/shard_map/ppermute | solution.py:20
  49.0 2.0 %collective-permute-start.10 = (bf16[128,512]{1,0:T(8,128)(2,1)S(1)}, bf16[128,512]{1,0:T(8,128)(2,1)S(1)}, u32[]{:S(2)}, u32[]{:S(2)}) collective-permute-start(bf16[128,512]{1,0:T(8,128)(2,1)S(1)} %get-tuple-element.45), channel_id=1, source_target_pairs={{0,2},{1,3},{2,0},{3,1},{4,6},{5,7},{6,4},{7,5},{8,10},{9,11},{10,... | collective-permute-start | bytes 393224 | tf_op jit(solution)/shard_map/ppermute | solution.py:20
  51.0 0.2 collective-permute-done.8.late
  51.3 1.0 %shard_map.102 = (bf16[6,128,512]{2,1,0:T(8,128)(2,1)S(1)}, bf16[128,512]{1,0:T(8,128)(2,1)S(1)}) custom-call(bf16[6,128,512]{2,1,0:T(8,128)(2,1)S(1)} %get-tuple-element.39.ext_in, bf16[128,512]{1,0:T(8,128)(2,1)S(1)} %collective-permute-done.8.late, bf16[128,512]{1,0:T(8,128)(2,1)S(1)} %get-tuple-element.37.q_near, ...), custom_call_target="tpu_custom_call", output_to_operand_aliasing={{0}: (0, {})} | custom-call | flops 100663296 | bytes 1441792 | tf_op jit(solution)/shard_map/pallas_call | solution.py:47
  52.3 2.4 %collective-permute-start.11 = (bf16[128,512]{1,0:T(8,128)(2,1)S(1)}, bf16[128,512]{1,0:T(8,128)(2,1)S(1)}, u32[]{:S(2)}, u32[]{:S(2)}) collective-permute-start(bf16[128,512]{1,0:T(8,128)(2,1)S(1)} %get-tuple-element.46), channel_id=1, source_target_pairs={{0,3},{1,0},{2,1},{3,2},{4,7},{5,4},{6,5},{7,6},{8,11},{9,8},{10,9... | collective-permute-start | bytes 393224 | tf_op jit(solution)/shard_map/ppermute | solution.py:20
  54.6 1.1 %shard_map.103 = (bf16[128,512]{1,0:T(8,128)(2,1)S(1)}, bf16[768,256]{1,0:T(8,128)(2,1)}, bf16[768,256]{1,0:T(8,128)(2,1)}) custom-call(bf16[6,128,512]{2,1,0:T(8,128)(2,1)S(1)} %get-tuple-element.41.ext, s32[512,128]{1,0:T(8,128)S(1)} %broadcast_in_dim.34.after_too.owners, bf16[128,512]{1,0:T(8,128)(2,1)S(1)} %collective-permute-done.8.late, ...), custom_call_target="tpu_custom_call" | custom-call | flops 100663296 | bytes 2129920 | tf_op jit(solution)/shard_map/pallas_call | solution.py:47
  55.8 1.6 %collective-permute-done.10.r2 = bf16[128,512]{1,0:T(8,128)(2,1)S(1)} collective-permute-done((bf16[128,512]{1,0:T(8,128)(2,1)S(1)}, bf16[128,512]{1,0:T(8,128)(2,1)S(1)}, u32[]{:S(2)}, u32[]{:S(2)}) %collective-permute-start.10) | collective-permute-done | bytes 131104 | tf_op jit(solution)/shard_map/ppermute | solution.py:20
  57.4 1.3 %collective-permute-done.11.r3 = bf16[128,512]{1,0:T(8,128)(2,1)S(1)} collective-permute-done((bf16[128,512]{1,0:T(8,128)(2,1)S(1)}, bf16[128,512]{1,0:T(8,128)(2,1)S(1)}, u32[]{:S(2)}, u32[]{:S(2)}) %collective-permute-start.11) | collective-permute-done | bytes 131104 | tf_op jit(solution)/shard_map/ppermute | solution.py:20
  58.7 0.8 %shard_map.104 = bf16[128,2048]{1,0:T(8,128)(2,1)} custom-call(bf16[128,512]{1,0:T(8,128)(2,1)S(1)} %get-tuple-element.43.s0, bf16[128,512]{1,0:T(8,128)(2,1)S(1)} %collective-permute-done.9.r1, bf16[128,512]{1,0:T(8,128)(2,1)S(1)} %collective-permute-done.10.r2, bf16[128,512]{1,0:T(8,128)(2,1)S(1)} %collective-permute-done.11.r3), custom_call_target="tpu_custom_call" | custom-call | bytes 524288 | tf_op jit(solution)/shard_map/pallas_call | solution.py:47
  (17 shorter events, 0.3 us)
Async XLA Ops:
  0.6 6.6 %copy-start.1 = (s32[512]{0:T(512)S(1)}, s32[512]{0:T(512)}, u32[]{:S(2)}) copy-start(s32[512]{0:T(512)} %param.12) | copy-start | bytes 6148
  0.6 21.7 %copy-start.2 = (s32[16]{0:T(128)S(1)}, s32[16]{0:T(128)}, u32[]{:S(2)}) copy-start(s32[16]{0:T(128)} %param.13) | copy-start | bytes 196
  1.9 16.2 %collective-permute-start = (bf16[64,4096]{1,0:T(8,128)(2,1)S(1)}, bf16[64,4096]{1,0:T(8,128)(2,1)}, u32[]{:S(2)}, u32[]{:S(2)}) collective-permute-start(bf16[64,4096]{1,0:T(8,128)(2,1)S(1)} %get-tuple-element.50.xa), channel_id=1, source_target_pairs={{0,1},{1,2},{2,3},{3,0},{4,5},{5,6},{6,7},{7,4},{8,9},{9,10},{10,1... | collective-permute-start | bytes 1572872 | tf_op jit(solution)/shard_map/ppermute | solution.py:20
  3.6 14.9 %collective-permute-start.1 = (bf16[64,4096]{1,0:T(8,128)(2,1)S(1)}, bf16[64,4096]{1,0:T(8,128)(2,1)}, u32[]{:S(2)}, u32[]{:S(2)}) collective-permute-start(bf16[64,4096]{1,0:T(8,128)(2,1)S(1)} %get-tuple-element.49.xb), channel_id=1, source_target_pairs={{0,3},{1,0},{2,1},{3,2},{4,7},{5,4},{6,5},{7,6},{8,11},{9,8},{10,9... | collective-permute-start | bytes 1572872 | tf_op jit(solution)/shard_map/ppermute | solution.py:20
  5.2 25.5 %collective-permute-start.2 = (bf16[64,4096]{1,0:T(8,128)(2,1)S(1)}, bf16[64,4096]{1,0:T(8,128)(2,1)S(1)}, u32[]{:S(2)}, u32[]{:S(2)}) collective-permute-start(bf16[64,4096]{1,0:T(8,128)(2,1)S(1)} %get-tuple-element.50.xa), channel_id=1, source_target_pairs={{0,3},{1,0},{2,1},{3,2},{4,7},{5,4},{6,5},{7,6},{8,11},{9,8},{10,9... | collective-permute-start | bytes 1572872 | tf_op jit(solution)/shard_map/ppermute | solution.py:20
  7.1 23.7 %collective-permute-start.3 = (bf16[64,4096]{1,0:T(8,128)(2,1)S(1)}, bf16[64,4096]{1,0:T(8,128)(2,1)S(1)}, u32[]{:S(2)}, u32[]{:S(2)}) collective-permute-start(bf16[64,4096]{1,0:T(8,128)(2,1)S(1)} %get-tuple-element.49.xb), channel_id=1, source_target_pairs={{0,1},{1,2},{2,3},{3,0},{4,5},{5,6},{6,7},{7,4},{8,9},{9,10},{10,1... | collective-permute-start | bytes 1572872 | tf_op jit(solution)/shard_map/ppermute | solution.py:20
  18.1 21.3 %collective-permute-start.4 = (bf16[64,4096]{1,0:T(8,128)(2,1)}, bf16[64,4096]{1,0:T(8,128)(2,1)S(1)}, u32[]{:S(2)}, u32[]{:S(2)}) collective-permute-start(bf16[64,4096]{1,0:T(8,128)(2,1)} %collective-permute-done.la), channel_id=1, source_target_pairs={{0,1},{1,2},{2,3},{3,0},{4,5},{5,6},{6,7},{7,4},{8,9},{9,10},{10,1... | collective-permute-start | bytes 1572872 | tf_op jit(solution)/shard_map/ppermute | solution.py:20
  18.5 21.1 %collective-permute-start.5 = (bf16[64,4096]{1,0:T(8,128)(2,1)}, bf16[64,4096]{1,0:T(8,128)(2,1)}, u32[]{:S(2)}, u32[]{:S(2)}) collective-permute-start(bf16[64,4096]{1,0:T(8,128)(2,1)} %collective-permute-done.1.rb), channel_id=1, source_target_pairs={{0,3},{1,0},{2,1},{3,2},{4,7},{5,4},{6,5},{7,6},{8,11},{9,8},{10,9... | collective-permute-start | bytes 1572872 | tf_op jit(solution)/shard_map/ppermute | solution.py:20
  22.8 3.5 %copy-start = (f32[4096]{0:T(1024)S(1)}, f32[4096]{0:T(1024)}, u32[]{:S(2)}) copy-start(f32[4096]{0:T(1024)} %param.8) | copy-start | bytes 49156
  31.9 12.7 %collective-permute-start.6 = (bf16[272,512]{1,0:T(8,128)(2,1)S(1)}, bf16[272,512]{1,0:T(8,128)(2,1)S(1)}, u32[]{:S(2)}, u32[]{:S(2)}) collective-permute-start(bf16[272,512]{1,0:T(8,128)(2,1)S(1)} %get-tuple-element.33), channel_id=1, source_target_pairs={{0,4},{4,0},{8,12},{12,8},{16,20},{20,16},{24,28},{28,24},{32,36},... | collective-permute-start | bytes 835592 | tf_op jit(solution)/shard_map/ppermute | solution.py:32
  32.0 12.6 %collective-permute-start.7 = (bf16[272,512]{1,0:T(8,128)(2,1)S(1)}, bf16[272,512]{1,0:T(8,128)(2,1)S(1)}, u32[]{:S(2)}, u32[]{:S(2)}) collective-permute-start(bf16[272,512]{1,0:T(8,128)(2,1)S(1)} %get-tuple-element.34), channel_id=1, source_target_pairs={{4,8},{8,4},{12,16},{16,12},{20,24},{24,20},{28,32},{32,28},{36,40... | collective-permute-start | bytes 835592 | tf_op jit(solution)/shard_map/ppermute | solution.py:32
  41.7 9.6 %collective-permute-start.8 = (bf16[128,512]{1,0:T(8,128)(2,1)S(1)}, bf16[128,512]{1,0:T(8,128)(2,1)S(1)}, u32[]{:S(2)}, u32[]{:S(2)}) collective-permute-start(bf16[128,512]{1,0:T(8,128)(2,1)S(1)} %get-tuple-element.40), channel_id=1, source_target_pairs={{0,4},{1,5},{4,8},{5,9},{6,2},{8,12},{9,13},{10,6},{12,16},{13,17}... | collective-permute-start | bytes 393224 | tf_op jit(solution)/shard_map/ppermute | solution.py:26
  47.4 8.4 %collective-permute-start.9 = (bf16[128,512]{1,0:T(8,128)(2,1)S(1)}, bf16[128,512]{1,0:T(8,128)(2,1)S(1)}, u32[]{:S(2)}, u32[]{:S(2)}) collective-permute-start(bf16[128,512]{1,0:T(8,128)(2,1)S(1)} %get-tuple-element.44), channel_id=1, source_target_pairs={{0,1},{1,2},{2,3},{3,0},{4,5},{5,6},{6,7},{7,4},{8,9},{9,10},{10,1... | collective-permute-start | bytes 393224 | tf_op jit(solution)/shard_map/ppermute | solution.py:20
  49.0 8.4 %collective-permute-start.10 = (bf16[128,512]{1,0:T(8,128)(2,1)S(1)}, bf16[128,512]{1,0:T(8,128)(2,1)S(1)}, u32[]{:S(2)}, u32[]{:S(2)}) collective-permute-start(bf16[128,512]{1,0:T(8,128)(2,1)S(1)} %get-tuple-element.45), channel_id=1, source_target_pairs={{0,2},{1,3},{2,0},{3,1},{4,6},{5,7},{6,4},{7,5},{8,10},{9,11},{10,... | collective-permute-start | bytes 393224 | tf_op jit(solution)/shard_map/ppermute | solution.py:20
  52.3 6.4 %collective-permute-start.11 = (bf16[128,512]{1,0:T(8,128)(2,1)S(1)}, bf16[128,512]{1,0:T(8,128)(2,1)S(1)}, u32[]{:S(2)}, u32[]{:S(2)}) collective-permute-start(bf16[128,512]{1,0:T(8,128)(2,1)S(1)} %get-tuple-element.46), channel_id=1, source_target_pairs={{0,3},{1,0},{2,1},{3,2},{4,7},{5,4},{6,5},{7,6},{8,11},{9,8},{10,9... | collective-permute-start | bytes 393224 | tf_op jit(solution)/shard_map/ppermute | solution.py:20

commit v2 on v1

--- a/solution.py
+++ b/solution.py
@@ -26,6 +26,12 @@
     return lax.ppermute(array, ("seq", "tp"), pairs)
 
 
+def turn_of(array, parity):
+    homes, n = lax.axis_size("seq"), lax.axis_size("tp")
+    pairs = [(h * n + t, h * n + (t + 1) % n) for h in range(parity, homes, 2) for t in range(n)]
+    return lax.ppermute(array, ("seq", "tp"), pairs)
+
+
 def swap(array, first):
     homes = lax.axis_size("seq")
     pairs = [p for h in range(first, homes - 1, 2) for p in ((h, h + 1), (h + 1, h))]
@@ -41,7 +47,7 @@
     return pltpu.with_memory_space_constraint(x, VM)
 
 
-def call(body, outs, arrays, flops=0, alias=None, scratch=()):
+def call(body, outs, arrays, flops=0, alias=None, aliases=1, scratch=()):
     inside = pl.BlockSpec(memory_space=VM)
     moved = sum(x.size * x.dtype.itemsize for x in arrays)
     return pl.pallas_call(
@@ -52,7 +58,7 @@
             pl.BlockSpec(memory_space=HB) if isinstance(o, jax.ShapeDtypeStruct) else inside for o in outs
         ],
         scratch_shapes=list(scratch),
-        input_output_aliases={} if alias is None else {alias: 0},
+        input_output_aliases={} if alias is None else {alias + i: i for i in range(aliases)},
         compiler_params=pltpu.CompilerParams(vmem_limit_bytes=12 << 20),
         cost_estimate=pl.CostEstimate(flops=flops, bytes_accessed=moved, transcendentals=0),
     )(*[vmem(x) for x in arrays])
@@ -95,6 +101,11 @@
         copy.start()
     for copy in copies:
         copy.wait()
+
+
+def halves_body(hidden, a, b, sems):
+    size = CH // 2
+    run([pltpu.make_async_copy(hidden.at[i * size : (i + 1) * size], out, sems.at[i]) for i, out in enumerate((a, b))])
 
 
 def weights_body(wq, wk, wv, after, after_too, wq_out, wk_out, wv_out, sems):
@@ -222,14 +233,9 @@
         out[:, i * HD : (i + 1) * HD] = part
 
 
-def far_body(ext_in, inner, outer, normed, wq, cosines, sines, docs, ext, out):
+def far_body(ext_in, outer, normed, wq, cosines, sines, docs, ext, out):
     _, _, _, far, home = spots()
     rows = chunk_rows(far)
-
-    @pl.when(lax.rem(home, 2) == 1)
-    def _():
-        ext[0] = inner[0:CH]
-        ext[1] = inner[CH : 2 * CH]
 
     @pl.when(lax.rem(home, 2) == 0)
     def _():
@@ -252,11 +258,32 @@
         late_out[:, i * HD : (i + 1) * HD] = owned_part(part, live)
 
 
-def first_body(ext_in, q_near, q_rest, docs, ext, out):
-    right = spots()[2]
+def first_tile(ext, q_near, q_rest, docs, out):
     half = CH // 2
     q = jnp.concatenate([q_rest[0:half], q_near[half:CH]], axis=0)
-    emit(out, attend(right, heads(q), ext, docs))
+    emit(out, attend(spots()[2], heads(q), ext, docs))
+
+
+def first_is_early():
+    own, _, _, _, home = spots()
+    return (lax.rem(home, 2) == 1) | (own == 1) | (own == 2)
+
+
+def first_body(ext_in, inner, q_near, q_rest, docs, ext, out):
+    @pl.when(lax.rem(spots()[4], 2) == 1)
+    def _():
+        ext[0] = inner[0:CH]
+        ext[1] = inner[CH : 2 * CH]
+
+    @pl.when(first_is_early())
+    def _():
+        first_tile(ext, q_near, q_rest, docs, out)
+
+
+def second_body(out_in, far_in, ext, q_near, q_rest, docs, out, far_out):
+    @pl.when(jnp.logical_not(first_is_early()))
+    def _():
+        first_tile(ext, q_near, q_rest, docs, out)
 
 
 def left_body(ext_in, late, q_near, q_rest, docs, ext, out):
@@ -308,13 +335,26 @@
         copy.wait()
 
 
-def join_body(s0, r1, r2, r3, out, sems):
-    own, left, right, far, _ = spots()
-    copies = []
-    for i, (piece, at) in enumerate(((s0, own), (r1, left), (r2, far), (r3, right))):
+def join_body(s0, r1_odd, r1_even, r2, r3, out, sems):
+    own, left, right, far, home = spots()
+
+    def place(piece, at, i):
         columns = pl.ds(pl.multiple_of(at * 512, 512), 512)
-        copies.append(pltpu.make_async_copy(piece, out.at[:, columns], sems.at[i]))
-    run(copies)
+        return pltpu.make_async_copy(piece, out.at[:, columns], sems.at[i])
+
+    copies = [place(s0, own, 0), place(r2, far, 2), place(r3, right, 3)]
+    for copy in copies:
+        copy.start()
+    for parity, piece in ((1, r1_odd), (0, r1_even)):
+
+        @pl.when(lax.rem(home, 2) == parity)
+        def _():
+            copy = place(piece, left, 1)
+            copy.start()
+            copy.wait()
+
+    for copy in copies:
+        copy.wait()
 
 
 def layer(hidden, norm_gain, w_query, w_key, w_value, doc_start, block_owner):
@@ -336,7 +376,7 @@
             cost_estimate=pl.CostEstimate(flops=0, bytes_accessed=size, transcendentals=0),
         )(*[pltpu.with_memory_space_constraint(x, HB) if x.size > CH * wide // 2 else x for x in arrays])
 
-    own_a, own_b = hidden[: CH // 2], hidden[CH // 2 :]
+    own_a, own_b = mover(halves_body, [(CH // 2, wide)] * 2, [hidden], 2 << 20)
     left_a = ring(own_a, 1)
     right_b = ring(own_b, -1)
     left_b = ring(own_b, 1)
@@ -378,6 +418,8 @@
     outer = swap(outside_out, 1)
     inner = swap(inside_out, 0)
     (q_rest,) = call(rest_q_body, [piece], [normed, w_query, cosines, sines], flops // 2)
+    ext, s1 = call(first_body, [slots, piece], [ext, inner, q_near, q_rest, docs], scores, alias=0)
+    r1_odd = turn_of(s1, 1)
     ext, normed, far = call(
         last_body,
         [slots, (CH, wide), piece],
@@ -386,10 +428,12 @@
         alias=0,
     )
     late = across(far, {0: 1, 1: 1, 2: -1})
-    ext, s2 = call(far_body, [slots, piece], [ext, inner, outer, normed, w_query, cosines, sines, docs], flops, alias=0)
+    ext, s2 = call(
+        far_body, [slots, piece], [ext, outer, normed, w_query, cosines, sines, docs], flops, alias=0
+    )
+    s1, s2 = call(second_body, [piece, piece], [s1, s2, ext, q_near, q_rest, docs], scores, alias=0, aliases=2)
     r2 = ring(s2, 2)
-    ext, s1 = call(first_body, [slots, piece], [ext, q_near, q_rest, docs], scores, alias=0)
-    r1 = ring(s1, 1)
+    r1_even = turn_of(s1, 0)
     ext, s3 = call(left_body, [slots, piece], [ext, late, q_near, q_rest, docs], scores, alias=0)
     r3 = ring(s3, 3)
     cache = jax.ShapeDtypeStruct((rows + 2 * CH, 256), bf)
@@ -403,7 +447,7 @@
     (context,) = call(
         join_body,
         [jax.ShapeDtypeStruct((CH, 2048), bf)],
-        [s0, r1, r2, r3],
+        [s0, r1_odd, r1_even, r2, r3],
         scratch=[pltpu.SemaphoreType.DMA((4,))],
     )
     return (context, key_cache, value_cache)

time: 60.6 us -> 62.5 us (1.031)
  starting transfers between devices: 21.1 us -> 26 us
  waiting for transfers between devices: 17.2 us -> 15.3 us
  Pallas kernels: 17.7 us -> 16.6 us
  other arithmetic: 1.01 us -> 1.69 us
  local copies, waits for them, and re-layouts: 1.69 us -> 1.06 us
    ppermute x0 -> x2, starting transfers between devices: none -> 2.77 us  [turn_of(): return lax.ppermute(array, ('seq', 'tp'), pairs)]
    ppermute x9 -> x8, waiting for transfers between devices: 16.9 us -> 14.6 us  [ring(): return lax.ppermute(array, 'tp', [(i, (i + by) % n) for i in range(n)])]
    pallas_call x10 -> x11, Pallas kernels: 14.2 us -> 11.9 us  [call(): pl.pallas_call(body, out_shape=[o if isinstance(o, jax.ShapeDtypeStruct)...]
    slice x1 -> x0, local copies, waits for them, and re-layouts: 1.28 us -> none  [layer(): own_a, own_b = (hidden[:CH // 2], hidden[CH // 2:])]
    ppermute x9 -> x8, starting transfers between devices: 14.6 us -> 15.8 us  [ring(): return lax.ppermute(array, 'tp', [(i, (i + by) % n) for i in range(n)])]
    pallas_call x1 -> x2, Pallas kernels: 3.51 us -> 4.73 us  [mover(): pl.pallas_call(body, out_shape=[VM(s, bf) for s in outs], in_specs=[outsi...]
    ppermute x1, starting transfers between devices: 2.1 us -> 2.96 us  [across(): return lax.ppermute(array, ('seq', 'tp'), pairs)]
    convert_element_type x1, other arithmetic: 0.01 us -> 0.69 us  [layer(): (row_number - doc_start).astype(jnp.float32)[:, None] * frequency[None, :]]
  transfers between devices with their start and end apart: 12 -> 13, of which waited for: 6 -> 5; matrix products, arithmetic and copies ran while one was open for 2% -> 4% of each run, Pallas kernels for 28% -> 24%
where the time goes in v2:
time: 62.5 us; the launch traced here: 61.7 us
  starting transfers between devices  26 us (42%)
  Pallas kernels  16.6 us (27%)
  waiting for transfers between devices  15.3 us (24%)
  other arithmetic  1.69 us (3%)
  local copies, waits for them, and re-layouts  1.06 us (2%)
  between operations  1.01 us (2%)
    ppermute x8, starting transfers between devices, ring(): return lax.ppermute(array, 'tp', [(i, (i + by) % n) for i in range(n)])  15.8 us
    ppermute x8, waiting for transfers between devices, ring(): return lax.ppermute(array, 'tp', [(i, (i + by) % n) for i in range(n)])  14.6 us
    pallas_call x11, Pallas kernels, call(): pl.pallas_call(body, out_shape=[o if isinstance(o, jax.ShapeDtypeStruct)...  11.9 us
    pallas_call x2, Pallas kernels, mover(): pl.pallas_call(body, out_shape=[VM(s, bf) for s in outs], in_specs=[outsi...  4.73 us
    ppermute x2, starting transfers between devices, swap(): return lax.ppermute(array, 'seq', pairs)  4.39 us
    ppermute x1, starting transfers between devices, across(): return lax.ppermute(array, ('seq', 'tp'), pairs)  2.96 us
    ppermute x2, starting transfers between devices, turn_of(): return lax.ppermute(array, ('seq', 'tp'), pairs)  2.77 us
  transfers between devices with their start and end apart: 13, of which 5 were waited for; matrix products, arithmetic and copies ran while one was open for 4% of the time, Pallas kernels for 24%

profile of v2, /device:TPU:128, one launch (start us, length us, event | category | flops | bytes accessed | tf_op | source)
XLA Modules:
  0.0 61.7 jit_solution(8247384923723828891)
XLA Ops:
  0.6 1.2 %shard_map.94 = (bf16[64,4096]{1,0:T(8,128)(2,1)S(1)}, bf16[64,4096]{1,0:T(8,128)(2,1)S(1)}) custom-call(bf16[128,4096]{1,0:T(8,128)(2,1)} %hidden.1), custom_call_target="tpu_custom_call" | custom-call | bytes 2097152 | tf_op jit(solution)/shard_map/pallas_call | solution.py:369
  1.9 3.1 %collective-permute-start.2 = (bf16[64,4096]{1,0:T(8,128)(2,1)S(1)}, bf16[64,4096]{1,0:T(8,128)(2,1)S(1)}, u32[]{:S(2)}, u32[]{:S(2)}) collective-permute-start(bf16[64,4096]{1,0:T(8,128)(2,1)S(1)} %get-tuple-element.30.xa), channel_id=1, source_target_pairs={{0,3},{1,0},{2,1},{3,2},{4,7},{5,4},{6,5},{7,6},{8,11},{9,8},{10,9... | collective-permute-start | bytes 1572872 | tf_op jit(solution)/shard_map/ppermute | solution.py:20
  5.0 0.6 collective-permute-start.3
  5.5 2.7 %collective-permute-start.1 = (bf16[64,4096]{1,0:T(8,128)(2,1)S(1)}, bf16[64,4096]{1,0:T(8,128)(2,1)S(1)}, u32[]{:S(2)}, u32[]{:S(2)}) collective-permute-start(bf16[64,4096]{1,0:T(8,128)(2,1)S(1)} %get-tuple-element.31.xb), channel_id=1, source_target_pairs={{0,3},{1,0},{2,1},{3,2},{4,7},{5,4},{6,5},{7,6},{8,11},{9,8},{10,9... | collective-permute-start | bytes 1572872 | tf_op jit(solution)/shard_map/ppermute | solution.py:20
  8.2 0.7 %broadcast_in_dim.32 = s32[16,32]{1,0:T(8,128)S(1)} broadcast(s32[16]{0:T(128)} %param.13), dimensions={0} | broadcast | bytes 2112 | tf_op jit(solution)/shard_map/broadcast_in_dim | solution.py:393
  9.0 0.7 %subtract_convert_fusion = (f32[512]{0:T(512)S(1)}, s32[512]{0:T(512)S(1)}) fusion(s32[512]{0:T(512)} %param.12, s32[]{:T(128)S(6)} %mul.35), kind=kLoop, calls=%fused_computation.5 | loop fusion | flops 2048 | bytes 6148 | tf_op jit(solution)/shard_map/convert_element_type | solution.py:390
  9.7 0.1 broadcast_in_dim.34.after_too.owners
  9.8 0.1 broadcast_in_dim.31.after.docs
  10.0 3.5 %shard_map.95 = (bf16[4096,512]{1,0:T(8,128)(2,1)S(1)}, bf16[4096,256]{1,0:T(8,128)(2,1)S(1)}, bf16[4096,256]{1,0:T(8,128)(2,1)S(1)}) custom-call(bf16[4096,512]{1,0:T(8,128)(2,1)} %wq.1, bf16[4096,256]{1,0:T(8,128)(2,1)} %wk.1, bf16[4096,256]{1,0:T(8,128)(2,1)} %wv.1, s32[512,128]{1,0:T(8,128)S(1)} %broadcast_in_dim.31.after.docs, ...), custom_call_target="tpu_custom_call" | custom-call | bytes 16777216 | tf_op jit(solution)/shard_map/pallas_call | solution.py:369
  13.5 1.0 %fusion = (f32[512,128]{1,0:T(8,128)S(1)}, f32[512,128]{1,0:T(8,128)S(1)}) fusion(f32[128]{0:T(128)S(1)} %get-tuple-element.61, f32[128]{0:T(128)S(1)} %get-tuple-element.62, f32[512]{0:T(512)S(1)} %get-tuple-element.59), kind=kLoop, calls=%fused_computation.2 | loop fusion | flops 131072 | bytes 527360 | tf_op jit(solution)/shard_map/mul | solution.py:391
  14.5 6.4 %collective-permute-done.la = bf16[64,4096]{1,0:T(8,128)(2,1)S(1)} collective-permute-done((bf16[64,4096]{1,0:T(8,128)(2,1)S(1)}, bf16[64,4096]{1,0:T(8,128)(2,1)S(1)}, u32[]{:S(2)}, u32[]{:S(2)}) %collective-permute-start) | collective-permute-done | bytes 524320 | tf_op jit(solution)/shard_map/ppermute | solution.py:20
  21.0 6.4 %collective-permute-done.1.rb = bf16[64,4096]{1,0:T(8,128)(2,1)S(1)} collective-permute-done((bf16[64,4096]{1,0:T(8,128)(2,1)S(1)}, bf16[64,4096]{1,0:T(8,128)(2,1)S(1)}, u32[]{:S(2)}, u32[]{:S(2)}) %collective-permute-start.1) | collective-permute-done | bytes 524320 | tf_op jit(solution)/shard_map/ppermute | solution.py:20
  27.4 3.7 %collective-permute-start.6 = (bf16[64,4096]{1,0:T(8,128)(2,1)S(1)}, bf16[64,4096]{1,0:T(8,128)(2,1)S(1)}, u32[]{:S(2)}, u32[]{:S(2)}) collective-permute-start(bf16[64,4096]{1,0:T(8,128)(2,1)S(1)} %collective-permute-done.1.rb), channel_id=1, source_target_pairs={{0,3},{1,0},{2,1},{3,2},{4,7},{5,4},{6,5},{7,6},{8,11},{9,8},{10,9... | collective-permute-start | bytes 1572872 | tf_op jit(solution)/shard_map/ppermute | solution.py:20
  31.1 1.6 %shard_map.96 = (bf16[6,128,512]{2,1,0:T(8,128)(2,1)S(1)}, bf16[128,512]{1,0:T(8,128)(2,1)S(1)}) custom-call(bf16[64,4096]{1,0:T(8,128)(2,1)S(1)} %get-tuple-element.30.xa, bf16[64,4096]{1,0:T(8,128)(2,1)S(1)} %get-tuple-element.31.xb, f32[1,4096]{1,0:T(1,128)S(1)} %bitcast.1, bf16[4096,512]{1,0:T(8,128)(2,1)S(1)} %get-tuple-element.32.wq, ...), custom_call_target="tpu_custom_call" | custom-call | flops 1073741824 | bytes 9977856 | tf_op jit(solution)/shard_map/pallas_call | solution.py:53
  32.7 1.6 %shard_map.97 = (bf16[6,128,512]{2,1,0:T(8,128)(2,1)S(1)}, bf16[128,512]{1,0:T(8,128)(2,1)S(1)}) custom-call(bf16[6,128,512]{2,1,0:T(8,128)(2,1)S(1)} %get-tuple-element.35.ext_in, bf16[64,4096]{1,0:T(8,128)(2,1)S(1)} %collective-permute-done.la, bf16[64,4096]{1,0:T(8,128)(2,1)S(1)} %collective-permute-done.1.rb, ...), custom_call_target="tpu_custom_call", output_to_operand_aliasing={{0}: (0, {})} | custom-call | flops 1073741824 | bytes 10764288 | tf_op jit(solution)/shard_map/pallas_call | solution.py:53
  34.3 1.1 %shard_map.98 = (bf16[6,128,512]{2,1,0:T(8,128)(2,1)S(1)}, bf16[128,4096]{1,0:T(8,128)(2,1)S(1)}, bf16[272,512]{1,0:T(8,128)(2,1)S(1)}, bf16[272,512]{1,0:T(8,128)(2,1)S(1)}) custom-call(bf16[6,128,512]{2,1,0:T(8,128)(2,1)S(1)} %get-tuple-element.36.ext_in, s32[512,128]{1,0:T(8,128)S(1)} %broadcast_in_dim.34.after_too.owners, ...), custom_call_target="tpu_custom_call", output_to_operand_aliasing={{0}: (0, {})} | custom-call | flops 536870912 | bytes 6832128 | tf_op jit(solution)/shard_map/pallas_call | solution.py:53
  35.6 4.3 %collective-permute-start.7 = (bf16[272,512]{1,0:T(8,128)(2,1)S(1)}, bf16[272,512]{1,0:T(8,128)(2,1)S(1)}, u32[]{:S(2)}, u32[]{:S(2)}) collective-permute-start(bf16[272,512]{1,0:T(8,128)(2,1)S(1)} %get-tuple-element.43), channel_id=1, source_target_pairs={{4,8},{8,4},{12,16},{16,12},{20,24},{24,20},{28,32},{32,28},{36,40... | collective-permute-start | bytes 835592 | tf_op jit(solution)/shard_map/ppermute | solution.py:38
  39.9 0.8 %shard_map.99.q_rest = bf16[128,512]{1,0:T(8,128)(2,1)S(1)} custom-call(bf16[128,4096]{1,0:T(8,128)(2,1)S(1)} %get-tuple-element.40.normed, bf16[4096,512]{1,0:T(8,128)(2,1)S(1)} %get-tuple-element.32.wq, f32[512,128]{1,0:T(8,128)S(1)} %get-tuple-element.58.cosines, f32[512,128]{1,0:T(8,128)S(1)} %get-tuple-element.57.sines), custom_call_target="tpu_custom_call" | custom-call | flops 536870912 | bytes 5767168 | tf_op jit(solution)/shard_map/pallas_call | solution.py:53
  40.7 0.8 %collective-permute-start.9 = (bf16[128,512]{1,0:T(8,128)(2,1)S(1)}, bf16[128,512]{1,0:T(8,128)(2,1)S(1)}, u32[]{:S(2)}, u32[]{:S(2)}) collective-permute-start(bf16[128,512]{1,0:T(8,128)(2,1)S(1)} %get-tuple-element.50.out_in), channel_id=1, source_target_pairs={{4,5},{5,6},{6,7},{7,4},{12,13},{13,14},{14,15},{15,12},{20,21},{2... | collective-permute-start | bytes 393224 | tf_op jit(solution)/shard_map/ppermute | solution.py:32
  41.6 0.4 collective-permute-done.5.xa
  42.0 1.1 %shard_map.101 = (bf16[6,128,512]{2,1,0:T(8,128)(2,1)S(1)}, bf16[128,4096]{1,0:T(8,128)(2,1)S(1)}, bf16[128,512]{1,0:T(8,128)(2,1)S(1)}) custom-call(bf16[6,128,512]{2,1,0:T(8,128)(2,1)S(1)} %get-tuple-element.41.ext_in, s32[512,128]{1,0:T(8,128)S(1)} %broadcast_in_dim.34.after_too.owners, ...), custom_call_target="tpu_custom_call", output_to_operand_aliasing={{0}: (0, {})} | custom-call | flops 536870912 | bytes 6832128 | tf_op jit(solution)/shard_map/pallas_call | solution.py:53
  43.1 3.0 %collective-permute-start.8 = (bf16[128,512]{1,0:T(8,128)(2,1)S(1)}, bf16[128,512]{1,0:T(8,128)(2,1)S(1)}, u32[]{:S(2)}, u32[]{:S(2)}) collective-permute-start(bf16[128,512]{1,0:T(8,128)(2,1)S(1)} %get-tuple-element.46), channel_id=1, source_target_pairs={{0,4},{1,5},{4,8},{5,9},{6,2},{8,12},{9,13},{10,6},{12,16},{13,17}... | collective-permute-start | bytes 393224 | tf_op jit(solution)/shard_map/ppermute | solution.py:26
  46.1 0.7 %collective-permute-done.7.outer = bf16[272,512]{1,0:T(8,128)(2,1)S(1)} collective-permute-done((bf16[272,512]{1,0:T(8,128)(2,1)S(1)}, bf16[272,512]{1,0:T(8,128)(2,1)S(1)}, u32[]{:S(2)}, u32[]{:S(2)}) %collective-permute-start.7) | collective-permute-done | bytes 278560 | tf_op jit(solution)/shard_map/ppermute | solution.py:38
  46.7 1.7 %shard_map.102 = (bf16[6,128,512]{2,1,0:T(8,128)(2,1)S(1)}, bf16[128,512]{1,0:T(8,128)(2,1)S(1)}) custom-call(bf16[6,128,512]{2,1,0:T(8,128)(2,1)S(1)} %get-tuple-element.42.ext_in, bf16[272,512]{1,0:T(8,128)(2,1)S(1)} %collective-permute-done.7.outer, bf16[128,4096]{1,0:T(8,128)(2,1)S(1)} %get-tuple-element.44.normed, ...), custom_call_target="tpu_custom_call", output_to_operand_aliasing={{0}: (0, {})} | custom-call | flops 1073741824 | bytes 7094272 | tf_op jit(solution)/shard_map/pallas_call | solution.py:53
  48.5 1.0 %shard_map.105 = (bf16[128,512]{1,0:T(8,128)(2,1)S(1)}, bf16[128,512]{1,0:T(8,128)(2,1)S(1)}) custom-call(bf16[128,512]{1,0:T(8,128)(2,1)S(1)} %get-tuple-element.50.out_in, bf16[128,512]{1,0:T(8,128)(2,1)S(1)} %get-tuple-element.51.far_in, bf16[6,128,512]{2,1,0:T(8,128)(2,1)S(1)} %get-tuple-element.45.ext_in.ext, ...), custom_call_target="tpu_custom_call", output_to_operand_aliasing={{0}: (0, {}), {1}: (1, {})} | custom-call | flops 100663296 | bytes 1572864 | tf_op jit(solution)/shard_map/pallas_call | solution.py:53
  49.5 1.9 %collective-permute-start.10 = (bf16[128,512]{1,0:T(8,128)(2,1)S(1)}, bf16[128,512]{1,0:T(8,128)(2,1)S(1)}, u32[]{:S(2)}, u32[]{:S(2)}) collective-permute-start(bf16[128,512]{1,0:T(8,128)(2,1)S(1)} %get-tuple-element.52), channel_id=1, source_target_pairs={{0,1},{1,2},{2,3},{3,0},{8,9},{9,10},{10,11},{11,8},{16,17},{17,18... | collective-permute-start | bytes 393224 | tf_op jit(solution)/shard_map/ppermute | solution.py:32
  51.4 3.1 %collective-permute-start.11 = (bf16[128,512]{1,0:T(8,128)(2,1)S(1)}, bf16[128,512]{1,0:T(8,128)(2,1)S(1)}, u32[]{:S(2)}, u32[]{:S(2)}) collective-permute-start(bf16[128,512]{1,0:T(8,128)(2,1)S(1)} %get-tuple-element.53), channel_id=1, source_target_pairs={{0,2},{1,3},{2,0},{3,1},{4,6},{5,7},{6,4},{7,5},{8,10},{9,11},{10,... | collective-permute-start | bytes 393224 | tf_op jit(solution)/shard_map/ppermute | solution.py:20
  54.5 1.0 %shard_map.103 = (bf16[6,128,512]{2,1,0:T(8,128)(2,1)S(1)}, bf16[128,512]{1,0:T(8,128)(2,1)S(1)}) custom-call(bf16[6,128,512]{2,1,0:T(8,128)(2,1)S(1)} %get-tuple-element.45.ext_in.ext, bf16[128,512]{1,0:T(8,128)(2,1)S(1)} %collective-permute-done.8.late, bf16[128,512]{1,0:T(8,128)(2,1)S(1)} %get-tuple-element.39.q_near, ...), custom_call_target="tpu_custom_call", output_to_operand_aliasing={{0}: (0, {})} | custom-call | flops 100663296 | bytes 1441792 | tf_op jit(solution)/shard_map/pallas_call | solution.py:53
  55.5 2.7 %collective-permute-start.12 = (bf16[128,512]{1,0:T(8,128)(2,1)S(1)}, bf16[128,512]{1,0:T(8,128)(2,1)S(1)}, u32[]{:S(2)}, u32[]{:S(2)}) collective-permute-start(bf16[128,512]{1,0:T(8,128)(2,1)S(1)} %get-tuple-element.54), channel_id=1, source_target_pairs={{0,3},{1,0},{2,1},{3,2},{4,7},{5,4},{6,5},{7,6},{8,11},{9,8},{10,9... | collective-permute-start | bytes 393224 | tf_op jit(solution)/shard_map/ppermute | solution.py:20
  58.2 1.1 %shard_map.104 = (bf16[128,512]{1,0:T(8,128)(2,1)S(1)}, bf16[768,256]{1,0:T(8,128)(2,1)}, bf16[768,256]{1,0:T(8,128)(2,1)}) custom-call(bf16[6,128,512]{2,1,0:T(8,128)(2,1)S(1)} %get-tuple-element.47.ext, s32[512,128]{1,0:T(8,128)S(1)} %broadcast_in_dim.34.after_too.owners, bf16[128,512]{1,0:T(8,128)(2,1)S(1)} %collective-permute-done.8.late, ...), custom_call_target="tpu_custom_call" | custom-call | flops 100663296 | bytes 2129920 | tf_op jit(solution)/shard_map/pallas_call | solution.py:53
  59.4 1.3 %collective-permute-done.12.r3 = bf16[128,512]{1,0:T(8,128)(2,1)S(1)} collective-permute-done((bf16[128,512]{1,0:T(8,128)(2,1)S(1)}, bf16[128,512]{1,0:T(8,128)(2,1)S(1)}, u32[]{:S(2)}, u32[]{:S(2)}) %collective-permute-start.12) | collective-permute-done | bytes 131104 | tf_op jit(solution)/shard_map/ppermute | solution.py:20
  60.7 0.8 %shard_map.106 = bf16[128,2048]{1,0:T(8,128)(2,1)} custom-call(bf16[128,512]{1,0:T(8,128)(2,1)S(1)} %get-tuple-element.49.s0, bf16[128,512]{1,0:T(8,128)(2,1)S(1)} %collective-permute-done.9.r1_odd, bf16[128,512]{1,0:T(8,128)(2,1)S(1)} %collective-permute-done.10.r1_even, bf16[128,512]{1,0:T(8,128)(2,1)S(1)} %collective-permute-done.11.r2, ...), custom_call_target="tpu_custom_call" | custom-call | bytes 655360 | tf_op jit(solution)/shard_map/pallas_call | solution.py:53
  (16 shorter events, 0.2 us)
Async XLA Ops:
  1.9 32.5 %collective-permute-start.2 = (bf16[64,4096]{1,0:T(8,128)(2,1)S(1)}, bf16[64,4096]{1,0:T(8,128)(2,1)S(1)}, u32[]{:S(2)}, u32[]{:S(2)}) collective-permute-start(bf16[64,4096]{1,0:T(8,128)(2,1)S(1)} %get-tuple-element.30.xa), channel_id=1, source_target_pairs={{0,3},{1,0},{2,1},{3,2},{4,7},{5,4},{6,5},{7,6},{8,11},{9,8},{10,9... | collective-permute-start | bytes 1572872 | tf_op jit(solution)/shard_map/ppermute | solution.py:20
  4.9 16.0 %collective-permute-start = (bf16[64,4096]{1,0:T(8,128)(2,1)S(1)}, bf16[64,4096]{1,0:T(8,128)(2,1)S(1)}, u32[]{:S(2)}, u32[]{:S(2)}) collective-permute-start(bf16[64,4096]{1,0:T(8,128)(2,1)S(1)} %get-tuple-element.30.xa), channel_id=1, source_target_pairs={{0,1},{1,2},{2,3},{3,0},{4,5},{5,6},{6,7},{7,4},{8,9},{9,10},{10,1... | collective-permute-start | bytes 1572872 | tf_op jit(solution)/shard_map/ppermute | solution.py:20
  5.0 29.4 %collective-permute-start.3 = (bf16[64,4096]{1,0:T(8,128)(2,1)S(1)}, bf16[64,4096]{1,0:T(8,128)(2,1)S(1)}, u32[]{:S(2)}, u32[]{:S(2)}) collective-permute-start(bf16[64,4096]{1,0:T(8,128)(2,1)S(1)} %get-tuple-element.31.xb), channel_id=1, source_target_pairs={{0,1},{1,2},{2,3},{3,0},{4,5},{5,6},{6,7},{7,4},{8,9},{9,10},{10,1... | collective-permute-start | bytes 1572872 | tf_op jit(solution)/shard_map/ppermute | solution.py:20
  5.5 21.8 %collective-permute-start.1 = (bf16[64,4096]{1,0:T(8,128)(2,1)S(1)}, bf16[64,4096]{1,0:T(8,128)(2,1)S(1)}, u32[]{:S(2)}, u32[]{:S(2)}) collective-permute-start(bf16[64,4096]{1,0:T(8,128)(2,1)S(1)} %get-tuple-element.31.xb), channel_id=1, source_target_pairs={{0,3},{1,0},{2,1},{3,2},{4,7},{5,4},{6,5},{7,6},{8,11},{9,8},{10,9... | collective-permute-start | bytes 1572872 | tf_op jit(solution)/shard_map/ppermute | solution.py:20
  10.0 21.1 %copy-start = (f32[4096]{0:T(1024)S(1)}, f32[4096]{0:T(1024)}, u32[]{:S(2)}) copy-start(f32[4096]{0:T(1024)} %param.8) | copy-start | bytes 49156
  21.0 21.1 %collective-permute-start.5 = (bf16[64,4096]{1,0:T(8,128)(2,1)S(1)}, bf16[64,4096]{1,0:T(8,128)(2,1)S(1)}, u32[]{:S(2)}, u32[]{:S(2)}) collective-permute-start(bf16[64,4096]{1,0:T(8,128)(2,1)S(1)} %collective-permute-done.la), channel_id=1, source_target_pairs={{0,1},{1,2},{2,3},{3,0},{4,5},{5,6},{6,7},{7,4},{8,9},{9,10},{10,1... | collective-permute-start | bytes 1572872 | tf_op jit(solution)/shard_map/ppermute | solution.py:20
  27.4 14.7 %collective-permute-start.6 = (bf16[64,4096]{1,0:T(8,128)(2,1)S(1)}, bf16[64,4096]{1,0:T(8,128)(2,1)S(1)}, u32[]{:S(2)}, u32[]{:S(2)}) collective-permute-start(bf16[64,4096]{1,0:T(8,128)(2,1)S(1)} %collective-permute-done.1.rb), channel_id=1, source_target_pairs={{0,3},{1,0},{2,1},{3,2},{4,7},{5,4},{6,5},{7,6},{8,11},{9,8},{10,9... | collective-permute-start | bytes 1572872 | tf_op jit(solution)/shard_map/ppermute | solution.py:20
  35.5 5.2 %collective-permute-start.4 = (bf16[272,512]{1,0:T(8,128)(2,1)S(1)}, bf16[272,512]{1,0:T(8,128)(2,1)S(1)}, u32[]{:S(2)}, u32[]{:S(2)}) collective-permute-start(bf16[272,512]{1,0:T(8,128)(2,1)S(1)} %get-tuple-element.38), channel_id=1, source_target_pairs={{0,4},{4,0},{8,12},{12,8},{16,20},{20,16},{24,28},{28,24},{32,36},... | collective-permute-start | bytes 835592 | tf_op jit(solution)/shard_map/ppermute | solution.py:38
  35.6 11.2 %collective-permute-start.7 = (bf16[272,512]{1,0:T(8,128)(2,1)S(1)}, bf16[272,512]{1,0:T(8,128)(2,1)S(1)}, u32[]{:S(2)}, u32[]{:S(2)}) collective-permute-start(bf16[272,512]{1,0:T(8,128)(2,1)S(1)} %get-tuple-element.43), channel_id=1, source_target_pairs={{4,8},{8,4},{12,16},{16,12},{20,24},{24,20},{28,32},{32,28},{36,40... | collective-permute-start | bytes 835592 | tf_op jit(solution)/shard_map/ppermute | solution.py:38
  40.7 7.7 %collective-permute-start.9 = (bf16[128,512]{1,0:T(8,128)(2,1)S(1)}, bf16[128,512]{1,0:T(8,128)(2,1)S(1)}, u32[]{:S(2)}, u32[]{:S(2)}) collective-permute-start(bf16[128,512]{1,0:T(8,128)(2,1)S(1)} %get-tuple-element.50.out_in), channel_id=1, source_target_pairs={{4,5},{5,6},{6,7},{7,4},{12,13},{13,14},{14,15},{15,12},{20,21},{2... | collective-permute-start | bytes 393224 | tf_op jit(solution)/shard_map/ppermute | solution.py:32
  43.1 11.4 %collective-permute-start.8 = (bf16[128,512]{1,0:T(8,128)(2,1)S(1)}, bf16[128,512]{1,0:T(8,128)(2,1)S(1)}, u32[]{:S(2)}, u32[]{:S(2)}) collective-permute-start(bf16[128,512]{1,0:T(8,128)(2,1)S(1)} %get-tuple-element.46), channel_id=1, source_target_pairs={{0,4},{1,5},{4,8},{5,9},{6,2},{8,12},{9,13},{10,6},{12,16},{13,17}... | collective-permute-start | bytes 393224 | tf_op jit(solution)/shard_map/ppermute | solution.py:26
  49.5 9.9 %collective-permute-start.10 = (bf16[128,512]{1,0:T(8,128)(2,1)S(1)}, bf16[128,512]{1,0:T(8,128)(2,1)S(1)}, u32[]{:S(2)}, u32[]{:S(2)}) collective-permute-start(bf16[128,512]{1,0:T(8,128)(2,1)S(1)} %get-tuple-element.52), channel_id=1, source_target_pairs={{0,1},{1,2},{2,3},{3,0},{8,9},{9,10},{10,11},{11,8},{16,17},{17,18... | collective-permute-start | bytes 393224 | tf_op jit(solution)/shard_map/ppermute | solution.py:32
  51.4 7.9 %collective-permute-start.11 = (bf16[128,512]{1,0:T(8,128)(2,1)S(1)}, bf16[128,512]{1,0:T(8,128)(2,1)S(1)}, u32[]{:S(2)}, u32[]{:S(2)}) collective-permute-start(bf16[128,512]{1,0:T(8,128)(2,1)S(1)} %get-tuple-element.53), channel_id=1, source_target_pairs={{0,2},{1,3},{2,0},{3,1},{4,6},{5,7},{6,4},{7,5},{8,10},{9,11},{10,... | collective-permute-start | bytes 393224 | tf_op jit(solution)/shard_map/ppermute | solution.py:20
  55.5 5.2 %collective-permute-start.12 = (bf16[128,512]{1,0:T(8,128)(2,1)S(1)}, bf16[128,512]{1,0:T(8,128)(2,1)S(1)}, u32[]{:S(2)}, u32[]{:S(2)}) collective-permute-start(bf16[128,512]{1,0:T(8,128)(2,1)S(1)} %get-tuple-element.54), channel_id=1, source_target_pairs={{0,3},{1,0},{2,1},{3,2},{4,7},{5,4},{6,5},{7,6},{8,11},{9,8},{10,9... | collective-permute-start | bytes 393224 | tf_op jit(solution)/shard_map/ppermute | solution.py:20

commit v3 on v2

--- a/solution.py
+++ b/solution.py
@@ -23,12 +23,6 @@
 def across(array, moves):
     homes, n = lax.axis_size("seq"), lax.axis_size("tp")
     pairs = [(h * n + t, (h + by) * n + t) for h in range(homes) for t, by in moves.items() if 0 <= h + by < homes]
-    return lax.ppermute(array, ("seq", "tp"), pairs)
-
-
-def turn_of(array, parity):
-    homes, n = lax.axis_size("seq"), lax.axis_size("tp")
-    pairs = [(h * n + t, h * n + (t + 1) % n) for h in range(parity, homes, 2) for t in range(n)]
     return lax.ppermute(array, ("seq", "tp"), pairs)
 
 
@@ -335,26 +329,13 @@
         copy.wait()
 
 
-def join_body(s0, r1_odd, r1_even, r2, r3, out, sems):
-    own, left, right, far, home = spots()
-
-    def place(piece, at, i):
+def join_body(s0, r1, r2, r3, out, sems):
+    own, left, right, far, _ = spots()
+    copies = []
+    for i, (piece, at) in enumerate(((s0, own), (r1, left), (r2, far), (r3, right))):
         columns = pl.ds(pl.multiple_of(at * 512, 512), 512)
-        return pltpu.make_async_copy(piece, out.at[:, columns], sems.at[i])
-
-    copies = [place(s0, own, 0), place(r2, far, 2), place(r3, right, 3)]
-    for copy in copies:
-        copy.start()
-    for parity, piece in ((1, r1_odd), (0, r1_even)):
-
-        @pl.when(lax.rem(home, 2) == parity)
-        def _():
-            copy = place(piece, left, 1)
-            copy.start()
-            copy.wait()
-
-    for copy in copies:
-        copy.wait()
+        copies.append(pltpu.make_async_copy(piece, out.at[:, columns], sems.at[i]))
+    run(copies)
 
 
 def layer(hidden, norm_gain, w_query, w_key, w_value, doc_start, block_owner):
@@ -419,7 +400,6 @@
     inner = swap(inside_out, 0)
     (q_rest,) = call(rest_q_body, [piece], [normed, w_query, cosines, sines], flops // 2)
     ext, s1 = call(first_body, [slots, piece], [ext, inner, q_near, q_rest, docs], scores, alias=0)
-    r1_odd = turn_of(s1, 1)
     ext, normed, far = call(
         last_body,
         [slots, (CH, wide), piece],
@@ -433,7 +413,7 @@
     )
     s1, s2 = call(second_body, [piece, piece], [s1, s2, ext, q_near, q_rest, docs], scores, alias=0, aliases=2)
     r2 = ring(s2, 2)
-    r1_even = turn_of(s1, 0)
+    r1 = ring(s1, 1)
     ext, s3 = call(left_body, [slots, piece], [ext, late, q_near, q_rest, docs], scores, alias=0)
     r3 = ring(s3, 3)
     cache = jax.ShapeDtypeStruct((rows + 2 * CH, 256), bf)
@@ -447,7 +427,7 @@
     (context,) = call(
         join_body,
         [jax.ShapeDtypeStruct((CH, 2048), bf)],
-        [s0, r1_odd, r1_even, r2, r3],
+        [s0, r1, r2, r3],
         scratch=[pltpu.SemaphoreType.DMA((4,))],
     )
     return (context, key_cache, value_cache)

time: 62.5 us -> 61 us (0.976)
  the two profiles are of different devices: /device:TPU:128 before, /device:TPU:103 now
where the time goes in v3:
time: 61 us; the launch traced here: 60.8 us
  starting transfers between devices  22.6 us (37%)
  waiting for transfers between devices  17.6 us (29%)
  Pallas kernels  16.9 us (28%)
  other arithmetic  1.69 us (3%)
  local copies, waits for them, and re-layouts  1.06 us (2%)
  between operations  1.01 us (2%)
    ppermute x9, waiting for transfers between devices, ring(): return lax.ppermute(array, 'tp', [(i, (i + by) % n) for i in range(n)])  17.6 us
    pallas_call x11, Pallas kernels, call(): pl.pallas_call(body, out_shape=[o if isinstance(o, jax.ShapeDtypeStruct)...  12.1 us
    ppermute x9, starting transfers between devices, ring(): return lax.ppermute(array, 'tp', [(i, (i + by) % n) for i in range(n)])  11.7 us
    ppermute x2, starting transfers between devices, swap(): return lax.ppermute(array, 'seq', pairs)  6.47 us
    pallas_call x2, Pallas kernels, mover(): pl.pallas_call(body, out_shape=[VM(s, bf) for s in outs], in_specs=[outsi...  4.73 us
    ppermute x1, starting transfers between devices, across(): return lax.ppermute(array, ('seq', 'tp'), pairs)  4.39 us
  transfers between devices with their start and end apart: 12, of which 4 were waited for; matrix products, arithmetic and copies ran while one was open for 5% of the time, Pallas kernels for 24%

profile of v3, /device:TPU:103, one launch (start us, length us, event | category | flops | bytes accessed | tf_op | source)
XLA Modules:
  0.0 60.8 jit_solution(9966052170518137578)
XLA Ops:
  0.6 1.2 %shard_map.94 = (bf16[64,4096]{1,0:T(8,128)(2,1)S(1)}, bf16[64,4096]{1,0:T(8,128)(2,1)S(1)}) custom-call(bf16[128,4096]{1,0:T(8,128)(2,1)} %hidden.1), custom_call_target="tpu_custom_call" | custom-call | bytes 2097152 | tf_op jit(solution)/shard_map/pallas_call | solution.py:350
  1.9 2.8 %collective-permute-start.2 = (bf16[64,4096]{1,0:T(8,128)(2,1)S(1)}, bf16[64,4096]{1,0:T(8,128)(2,1)S(1)}, u32[]{:S(2)}, u32[]{:S(2)}) collective-permute-start(bf16[64,4096]{1,0:T(8,128)(2,1)S(1)} %get-tuple-element.30.xa), channel_id=1, source_target_pairs={{0,3},{1,0},{2,1},{3,2},{4,7},{5,4},{6,5},{7,6},{8,11},{9,8},{10,9... | collective-permute-start | bytes 1572872 | tf_op jit(solution)/shard_map/ppermute | solution.py:20
  4.7 0.0 collective-permute-start.3
  4.7 2.7 %collective-permute-start.1 = (bf16[64,4096]{1,0:T(8,128)(2,1)S(1)}, bf16[64,4096]{1,0:T(8,128)(2,1)S(1)}, u32[]{:S(2)}, u32[]{:S(2)}) collective-permute-start(bf16[64,4096]{1,0:T(8,128)(2,1)S(1)} %get-tuple-element.31.xb), channel_id=1, source_target_pairs={{0,3},{1,0},{2,1},{3,2},{4,7},{5,4},{6,5},{7,6},{8,11},{9,8},{10,9... | collective-permute-start | bytes 1572872 | tf_op jit(solution)/shard_map/ppermute | solution.py:20
  7.4 0.7 %broadcast_in_dim.32 = s32[16,32]{1,0:T(8,128)S(1)} broadcast(s32[16]{0:T(128)} %param.13), dimensions={0} | broadcast | bytes 2112 | tf_op jit(solution)/shard_map/broadcast_in_dim | solution.py:374
  8.1 0.1 broadcast_in_dim.33
  8.2 0.7 %subtract_convert_fusion = (f32[512]{0:T(512)S(1)}, s32[512]{0:T(512)S(1)}) fusion(s32[512]{0:T(512)} %param.12, s32[]{:T(128)S(6)} %mul.35), kind=kLoop, calls=%fused_computation.5 | loop fusion | flops 2048 | bytes 6148 | tf_op jit(solution)/shard_map/convert_element_type | solution.py:371
  8.9 0.1 broadcast_in_dim.34.after_too.owners
  9.0 0.1 broadcast_in_dim.31.after.docs
  9.1 3.5 %shard_map.95 = (bf16[4096,512]{1,0:T(8,128)(2,1)S(1)}, bf16[4096,256]{1,0:T(8,128)(2,1)S(1)}, bf16[4096,256]{1,0:T(8,128)(2,1)S(1)}) custom-call(bf16[4096,512]{1,0:T(8,128)(2,1)} %wq.1, bf16[4096,256]{1,0:T(8,128)(2,1)} %wk.1, bf16[4096,256]{1,0:T(8,128)(2,1)} %wv.1, s32[512,128]{1,0:T(8,128)S(1)} %broadcast_in_dim.31.after.docs, ...), custom_call_target="tpu_custom_call" | custom-call | bytes 16777216 | tf_op jit(solution)/shard_map/pallas_call | solution.py:350
  12.7 1.0 %fusion = (f32[512,128]{1,0:T(8,128)S(1)}, f32[512,128]{1,0:T(8,128)S(1)}) fusion(f32[128]{0:T(128)S(1)} %get-tuple-element.61, f32[128]{0:T(128)S(1)} %get-tuple-element.62, f32[512]{0:T(512)S(1)} %get-tuple-element.59), kind=kLoop, calls=%fused_computation.2 | loop fusion | flops 131072 | bytes 527360 | tf_op jit(solution)/shard_map/mul | solution.py:372
  13.7 4.7 %collective-permute-done.la = bf16[64,4096]{1,0:T(8,128)(2,1)S(1)} collective-permute-done((bf16[64,4096]{1,0:T(8,128)(2,1)S(1)}, bf16[64,4096]{1,0:T(8,128)(2,1)S(1)}, u32[]{:S(2)}, u32[]{:S(2)}) %collective-permute-start) | collective-permute-done | bytes 524320 | tf_op jit(solution)/shard_map/ppermute | solution.py:20
  18.4 8.1 %collective-permute-done.1.rb = bf16[64,4096]{1,0:T(8,128)(2,1)S(1)} collective-permute-done((bf16[64,4096]{1,0:T(8,128)(2,1)S(1)}, bf16[64,4096]{1,0:T(8,128)(2,1)S(1)}, u32[]{:S(2)}, u32[]{:S(2)}) %collective-permute-start.1) | collective-permute-done | bytes 524320 | tf_op jit(solution)/shard_map/ppermute | solution.py:20
  26.5 3.4 %collective-permute-start.6 = (bf16[64,4096]{1,0:T(8,128)(2,1)S(1)}, bf16[64,4096]{1,0:T(8,128)(2,1)S(1)}, u32[]{:S(2)}, u32[]{:S(2)}) collective-permute-start(bf16[64,4096]{1,0:T(8,128)(2,1)S(1)} %collective-permute-done.1.rb), channel_id=1, source_target_pairs={{0,3},{1,0},{2,1},{3,2},{4,7},{5,4},{6,5},{7,6},{8,11},{9,8},{10,9... | collective-permute-start | bytes 1572872 | tf_op jit(solution)/shard_map/ppermute | solution.py:20
  29.9 1.6 %shard_map.96 = (bf16[6,128,512]{2,1,0:T(8,128)(2,1)S(1)}, bf16[128,512]{1,0:T(8,128)(2,1)S(1)}) custom-call(bf16[64,4096]{1,0:T(8,128)(2,1)S(1)} %get-tuple-element.30.xa, bf16[64,4096]{1,0:T(8,128)(2,1)S(1)} %get-tuple-element.31.xb, f32[1,4096]{1,0:T(1,128)S(1)} %bitcast.1, bf16[4096,512]{1,0:T(8,128)(2,1)S(1)} %get-tuple-element.32.wq, ...), custom_call_target="tpu_custom_call" | custom-call | flops 1073741824 | bytes 9977856 | tf_op jit(solution)/shard_map/pallas_call | solution.py:47
  31.5 1.6 %shard_map.97 = (bf16[6,128,512]{2,1,0:T(8,128)(2,1)S(1)}, bf16[128,512]{1,0:T(8,128)(2,1)S(1)}) custom-call(bf16[6,128,512]{2,1,0:T(8,128)(2,1)S(1)} %get-tuple-element.35.ext_in, bf16[64,4096]{1,0:T(8,128)(2,1)S(1)} %collective-permute-done.la, bf16[64,4096]{1,0:T(8,128)(2,1)S(1)} %collective-permute-done.1.rb, ...), custom_call_target="tpu_custom_call", output_to_operand_aliasing={{0}: (0, {})} | custom-call | flops 1073741824 | bytes 10764288 | tf_op jit(solution)/shard_map/pallas_call | solution.py:47
  33.2 1.1 %shard_map.98 = (bf16[6,128,512]{2,1,0:T(8,128)(2,1)S(1)}, bf16[128,4096]{1,0:T(8,128)(2,1)S(1)}, bf16[272,512]{1,0:T(8,128)(2,1)S(1)}, bf16[272,512]{1,0:T(8,128)(2,1)S(1)}) custom-call(bf16[6,128,512]{2,1,0:T(8,128)(2,1)S(1)} %get-tuple-element.36.ext_in, s32[512,128]{1,0:T(8,128)S(1)} %broadcast_in_dim.34.after_too.owners, ...), custom_call_target="tpu_custom_call", output_to_operand_aliasing={{0}: (0, {})} | custom-call | flops 536870912 | bytes 6832128 | tf_op jit(solution)/shard_map/pallas_call | solution.py:47
  34.3 1.9 %collective-permute-start.4 = (bf16[272,512]{1,0:T(8,128)(2,1)S(1)}, bf16[272,512]{1,0:T(8,128)(2,1)S(1)}, u32[]{:S(2)}, u32[]{:S(2)}) collective-permute-start(bf16[272,512]{1,0:T(8,128)(2,1)S(1)} %get-tuple-element.38), channel_id=1, source_target_pairs={{0,4},{4,0},{8,12},{12,8},{16,20},{20,16},{24,28},{28,24},{32,36},... | collective-permute-start | bytes 835592 | tf_op jit(solution)/shard_map/ppermute | solution.py:32
  36.2 4.6 %collective-permute-start.7 = (bf16[272,512]{1,0:T(8,128)(2,1)S(1)}, bf16[272,512]{1,0:T(8,128)(2,1)S(1)}, u32[]{:S(2)}, u32[]{:S(2)}) collective-permute-start(bf16[272,512]{1,0:T(8,128)(2,1)S(1)} %get-tuple-element.43), channel_id=1, source_target_pairs={{4,8},{8,4},{12,16},{16,12},{20,24},{24,20},{28,32},{32,28},{36,40... | collective-permute-start | bytes 835592 | tf_op jit(solution)/shard_map/ppermute | solution.py:32
  40.8 0.8 %shard_map.99.q_rest = bf16[128,512]{1,0:T(8,128)(2,1)S(1)} custom-call(bf16[128,4096]{1,0:T(8,128)(2,1)S(1)} %get-tuple-element.40.normed, bf16[4096,512]{1,0:T(8,128)(2,1)S(1)} %get-tuple-element.32.wq, f32[512,128]{1,0:T(8,128)S(1)} %get-tuple-element.58.cosines, f32[512,128]{1,0:T(8,128)S(1)} %get-tuple-element.57.sines), custom_call_target="tpu_custom_call" | custom-call | flops 536870912 | bytes 5767168 | tf_op jit(solution)/shard_map/pallas_call | solution.py:47
  41.6 1.2 %shard_map.100 = (bf16[6,128,512]{2,1,0:T(8,128)(2,1)S(1)}, bf16[128,512]{1,0:T(8,128)(2,1)S(1)}) custom-call(bf16[6,128,512]{2,1,0:T(8,128)(2,1)S(1)} %get-tuple-element.37.ext_in, bf16[272,512]{1,0:T(8,128)(2,1)S(1)} %collective-permute-done.4.inner, bf16[128,512]{1,0:T(8,128)(2,1)S(1)} %get-tuple-element.39.q_near, ...), custom_call_target="tpu_custom_call", output_to_operand_aliasing={{0}: (0, {})} | custom-call | flops 100663296 | bytes 1589248 | tf_op jit(solution)/shard_map/pallas_call | solution.py:47
  42.9 1.1 %shard_map.101 = (bf16[6,128,512]{2,1,0:T(8,128)(2,1)S(1)}, bf16[128,4096]{1,0:T(8,128)(2,1)S(1)}, bf16[128,512]{1,0:T(8,128)(2,1)S(1)}) custom-call(bf16[6,128,512]{2,1,0:T(8,128)(2,1)S(1)} %get-tuple-element.41.ext_in, s32[512,128]{1,0:T(8,128)S(1)} %broadcast_in_dim.34.after_too.owners, ...), custom_call_target="tpu_custom_call", output_to_operand_aliasing={{0}: (0, {})} | custom-call | flops 536870912 | bytes 6832128 | tf_op jit(solution)/shard_map/pallas_call | solution.py:47
  43.9 4.4 %collective-permute-start.8 = (bf16[128,512]{1,0:T(8,128)(2,1)S(1)}, bf16[128,512]{1,0:T(8,128)(2,1)S(1)}, u32[]{:S(2)}, u32[]{:S(2)}) collective-permute-start(bf16[128,512]{1,0:T(8,128)(2,1)S(1)} %get-tuple-element.46), channel_id=1, source_target_pairs={{0,4},{1,5},{4,8},{5,9},{6,2},{8,12},{9,13},{10,6},{12,16},{13,17}... | collective-permute-start | bytes 393224 | tf_op jit(solution)/shard_map/ppermute | solution.py:26
  48.3 1.7 %shard_map.102 = (bf16[6,128,512]{2,1,0:T(8,128)(2,1)S(1)}, bf16[128,512]{1,0:T(8,128)(2,1)S(1)}) custom-call(bf16[6,128,512]{2,1,0:T(8,128)(2,1)S(1)} %get-tuple-element.42.ext_in, bf16[272,512]{1,0:T(8,128)(2,1)S(1)} %collective-permute-done.7.outer, bf16[128,4096]{1,0:T(8,128)(2,1)S(1)} %get-tuple-element.44.normed, ...), custom_call_target="tpu_custom_call", output_to_operand_aliasing={{0}: (0, {})} | custom-call | flops 1073741824 | bytes 7094272 | tf_op jit(solution)/shard_map/pallas_call | solution.py:47
  50.1 0.1 collective-permute-start.9
  50.2 0.1 collective-permute-start.10
  50.3 1.0 %shard_map.103 = (bf16[6,128,512]{2,1,0:T(8,128)(2,1)S(1)}, bf16[128,512]{1,0:T(8,128)(2,1)S(1)}) custom-call(bf16[6,128,512]{2,1,0:T(8,128)(2,1)S(1)} %get-tuple-element.45.ext_in.ext, bf16[128,512]{1,0:T(8,128)(2,1)S(1)} %collective-permute-done.8.late, bf16[128,512]{1,0:T(8,128)(2,1)S(1)} %get-tuple-element.39.q_near, ...), custom_call_target="tpu_custom_call", output_to_operand_aliasing={{0}: (0, {})} | custom-call | flops 100663296 | bytes 1441792 | tf_op jit(solution)/shard_map/pallas_call | solution.py:47
  51.3 2.6 %collective-permute-start.11 = (bf16[128,512]{1,0:T(8,128)(2,1)S(1)}, bf16[128,512]{1,0:T(8,128)(2,1)S(1)}, u32[]{:S(2)}, u32[]{:S(2)}) collective-permute-start(bf16[128,512]{1,0:T(8,128)(2,1)S(1)} %get-tuple-element.54), channel_id=1, source_target_pairs={{0,3},{1,0},{2,1},{3,2},{4,7},{5,4},{6,5},{7,6},{8,11},{9,8},{10,9... | collective-permute-start | bytes 393224 | tf_op jit(solution)/shard_map/ppermute | solution.py:20
  53.9 1.1 %shard_map.104 = (bf16[128,512]{1,0:T(8,128)(2,1)S(1)}, bf16[768,256]{1,0:T(8,128)(2,1)}, bf16[768,256]{1,0:T(8,128)(2,1)}) custom-call(bf16[6,128,512]{2,1,0:T(8,128)(2,1)S(1)} %get-tuple-element.47.ext, s32[512,128]{1,0:T(8,128)S(1)} %broadcast_in_dim.34.after_too.owners, bf16[128,512]{1,0:T(8,128)(2,1)S(1)} %collective-permute-done.8.late, ...), custom_call_target="tpu_custom_call" | custom-call | flops 100663296 | bytes 2129920 | tf_op jit(solution)/shard_map/pallas_call | solution.py:47
  55.1 3.8 %collective-permute-done.9.r1 = bf16[128,512]{1,0:T(8,128)(2,1)S(1)} collective-permute-done((bf16[128,512]{1,0:T(8,128)(2,1)S(1)}, bf16[128,512]{1,0:T(8,128)(2,1)S(1)}, u32[]{:S(2)}, u32[]{:S(2)}) %collective-permute-start.9) | collective-permute-done | bytes 131104 | tf_op jit(solution)/shard_map/ppermute | solution.py:20
  58.9 0.9 %collective-permute-done.11.r3 = bf16[128,512]{1,0:T(8,128)(2,1)S(1)} collective-permute-done((bf16[128,512]{1,0:T(8,128)(2,1)S(1)}, bf16[128,512]{1,0:T(8,128)(2,1)S(1)}, u32[]{:S(2)}, u32[]{:S(2)}) %collective-permute-start.11) | collective-permute-done | bytes 131104 | tf_op jit(solution)/shard_map/ppermute | solution.py:20
  59.8 0.8 %shard_map.106 = bf16[128,2048]{1,0:T(8,128)(2,1)} custom-call(bf16[128,512]{1,0:T(8,128)(2,1)S(1)} %get-tuple-element.49.s0, bf16[128,512]{1,0:T(8,128)(2,1)S(1)} %collective-permute-done.9.r1, bf16[128,512]{1,0:T(8,128)(2,1)S(1)} %collective-permute-done.10.r2, bf16[128,512]{1,0:T(8,128)(2,1)S(1)} %collective-permute-done.11.r3), custom_call_target="tpu_custom_call" | custom-call | bytes 524288 | tf_op jit(solution)/shard_map/pallas_call | solution.py:47
  (14 shorter events, 0.1 us)
Async XLA Ops:
  1.9 31.3 %collective-permute-start.2 = (bf16[64,4096]{1,0:T(8,128)(2,1)S(1)}, bf16[64,4096]{1,0:T(8,128)(2,1)S(1)}, u32[]{:S(2)}, u32[]{:S(2)}) collective-permute-start(bf16[64,4096]{1,0:T(8,128)(2,1)S(1)} %get-tuple-element.30.xa), channel_id=1, source_target_pairs={{0,3},{1,0},{2,1},{3,2},{4,7},{5,4},{6,5},{7,6},{8,11},{9,8},{10,9... | collective-permute-start | bytes 1572872 | tf_op jit(solution)/shard_map/ppermute | solution.py:20
  4.7 13.7 %collective-permute-start = (bf16[64,4096]{1,0:T(8,128)(2,1)S(1)}, bf16[64,4096]{1,0:T(8,128)(2,1)S(1)}, u32[]{:S(2)}, u32[]{:S(2)}) collective-permute-start(bf16[64,4096]{1,0:T(8,128)(2,1)S(1)} %get-tuple-element.30.xa), channel_id=1, source_target_pairs={{0,1},{1,2},{2,3},{3,0},{4,5},{5,6},{6,7},{7,4},{8,9},{9,10},{10,1... | collective-permute-start | bytes 1572872 | tf_op jit(solution)/shard_map/ppermute | solution.py:20
  4.7 28.5 %collective-permute-start.3 = (bf16[64,4096]{1,0:T(8,128)(2,1)S(1)}, bf16[64,4096]{1,0:T(8,128)(2,1)S(1)}, u32[]{:S(2)}, u32[]{:S(2)}) collective-permute-start(bf16[64,4096]{1,0:T(8,128)(2,1)S(1)} %get-tuple-element.31.xb), channel_id=1, source_target_pairs={{0,1},{1,2},{2,3},{3,0},{4,5},{5,6},{6,7},{7,4},{8,9},{9,10},{10,1... | collective-permute-start | bytes 1572872 | tf_op jit(solution)/shard_map/ppermute | solution.py:20
  4.7 21.8 %collective-permute-start.1 = (bf16[64,4096]{1,0:T(8,128)(2,1)S(1)}, bf16[64,4096]{1,0:T(8,128)(2,1)S(1)}, u32[]{:S(2)}, u32[]{:S(2)}) collective-permute-start(bf16[64,4096]{1,0:T(8,128)(2,1)S(1)} %get-tuple-element.31.xb), channel_id=1, source_target_pairs={{0,3},{1,0},{2,1},{3,2},{4,7},{5,4},{6,5},{7,6},{8,11},{9,8},{10,9... | collective-permute-start | bytes 1572872 | tf_op jit(solution)/shard_map/ppermute | solution.py:20
  9.1 20.8 %copy-start = (f32[4096]{0:T(1024)S(1)}, f32[4096]{0:T(1024)}, u32[]{:S(2)}) copy-start(f32[4096]{0:T(1024)} %param.8) | copy-start | bytes 49156
  18.4 24.4 %collective-permute-start.5 = (bf16[64,4096]{1,0:T(8,128)(2,1)S(1)}, bf16[64,4096]{1,0:T(8,128)(2,1)S(1)}, u32[]{:S(2)}, u32[]{:S(2)}) collective-permute-start(bf16[64,4096]{1,0:T(8,128)(2,1)S(1)} %collective-permute-done.la), channel_id=1, source_target_pairs={{0,1},{1,2},{2,3},{3,0},{4,5},{5,6},{6,7},{7,4},{8,9},{9,10},{10,1... | collective-permute-start | bytes 1572872 | tf_op jit(solution)/shard_map/ppermute | solution.py:20
  26.5 16.3 %collective-permute-start.6 = (bf16[64,4096]{1,0:T(8,128)(2,1)S(1)}, bf16[64,4096]{1,0:T(8,128)(2,1)S(1)}, u32[]{:S(2)}, u32[]{:S(2)}) collective-permute-start(bf16[64,4096]{1,0:T(8,128)(2,1)S(1)} %collective-permute-done.1.rb), channel_id=1, source_target_pairs={{0,3},{1,0},{2,1},{3,2},{4,7},{5,4},{6,5},{7,6},{8,11},{9,8},{10,9... | collective-permute-start | bytes 1572872 | tf_op jit(solution)/shard_map/ppermute | solution.py:20
  34.3 7.3 %collective-permute-start.4 = (bf16[272,512]{1,0:T(8,128)(2,1)S(1)}, bf16[272,512]{1,0:T(8,128)(2,1)S(1)}, u32[]{:S(2)}, u32[]{:S(2)}) collective-permute-start(bf16[272,512]{1,0:T(8,128)(2,1)S(1)} %get-tuple-element.38), channel_id=1, source_target_pairs={{0,4},{4,0},{8,12},{12,8},{16,20},{20,16},{24,28},{28,24},{32,36},... | collective-permute-start | bytes 835592 | tf_op jit(solution)/shard_map/ppermute | solution.py:32
  36.2 12.1 %collective-permute-start.7 = (bf16[272,512]{1,0:T(8,128)(2,1)S(1)}, bf16[272,512]{1,0:T(8,128)(2,1)S(1)}, u32[]{:S(2)}, u32[]{:S(2)}) collective-permute-start(bf16[272,512]{1,0:T(8,128)(2,1)S(1)} %get-tuple-element.43), channel_id=1, source_target_pairs={{4,8},{8,4},{12,16},{16,12},{20,24},{24,20},{28,32},{32,28},{36,40... | collective-permute-start | bytes 835592 | tf_op jit(solution)/shard_map/ppermute | solution.py:32
  43.9 6.4 %collective-permute-start.8 = (bf16[128,512]{1,0:T(8,128)(2,1)S(1)}, bf16[128,512]{1,0:T(8,128)(2,1)S(1)}, u32[]{:S(2)}, u32[]{:S(2)}) collective-permute-start(bf16[128,512]{1,0:T(8,128)(2,1)S(1)} %get-tuple-element.46), channel_id=1, source_target_pairs={{0,4},{1,5},{4,8},{5,9},{6,2},{8,12},{9,13},{10,6},{12,16},{13,17}... | collective-permute-start | bytes 393224 | tf_op jit(solution)/shard_map/ppermute | solution.py:26
  50.1 8.8 %collective-permute-start.9 = (bf16[128,512]{1,0:T(8,128)(2,1)S(1)}, bf16[128,512]{1,0:T(8,128)(2,1)S(1)}, u32[]{:S(2)}, u32[]{:S(2)}) collective-permute-start(bf16[128,512]{1,0:T(8,128)(2,1)S(1)} %get-tuple-element.52), channel_id=1, source_target_pairs={{0,1},{1,2},{2,3},{3,0},{4,5},{5,6},{6,7},{7,4},{8,9},{9,10},{10,1... | collective-permute-start | bytes 393224 | tf_op jit(solution)/shard_map/ppermute | solution.py:20
  50.2 8.7 %collective-permute-start.10 = (bf16[128,512]{1,0:T(8,128)(2,1)S(1)}, bf16[128,512]{1,0:T(8,128)(2,1)S(1)}, u32[]{:S(2)}, u32[]{:S(2)}) collective-permute-start(bf16[128,512]{1,0:T(8,128)(2,1)S(1)} %get-tuple-element.53), channel_id=1, source_target_pairs={{0,2},{1,3},{2,0},{3,1},{4,6},{5,7},{6,4},{7,5},{8,10},{9,11},{10,... | collective-permute-start | bytes 393224 | tf_op jit(solution)/shard_map/ppermute | solution.py:20
  51.3 8.5 %collective-permute-start.11 = (bf16[128,512]{1,0:T(8,128)(2,1)S(1)}, bf16[128,512]{1,0:T(8,128)(2,1)S(1)}, u32[]{:S(2)}, u32[]{:S(2)}) collective-permute-start(bf16[128,512]{1,0:T(8,128)(2,1)S(1)} %get-tuple-element.54), channel_id=1, source_target_pairs={{0,3},{1,0},{2,1},{3,2},{4,7},{5,4},{6,5},{7,6},{8,11},{9,8},{10,9... | collective-permute-start | bytes 393224 | tf_op jit(solution)/shard_map/ppermute | solution.py:20

commit v4 on v3

--- a/solution.py
+++ b/solution.py
@@ -227,17 +227,25 @@
         out[:, i * HD : (i + 1) * HD] = part
 
 
-def far_body(ext_in, outer, normed, wq, cosines, sines, docs, ext, out):
-    _, _, _, far, home = spots()
+def far_tile(ext, normed, wq, cosines, sines, docs, out):
+    far = spots()[3]
     rows = chunk_rows(far)
-
-    @pl.when(lax.rem(home, 2) == 0)
+    q = project_q(normed[...], wq, cosines[rows], sines[rows])
+    emit(out, attend(far, q, ext, docs))
+
+
+def ahead_body(ext_in, late_in, normed, wq, cosines, sines, docs, ext, late_out, out):
+    @pl.when(lax.rem(spots()[4], 2) == 1)
+    def _():
+        far_tile(ext, normed, wq, cosines, sines, docs, out)
+
+
+def far_body(ext_in, out_in, outer, normed, wq, cosines, sines, docs, ext, out):
+    @pl.when(lax.rem(spots()[4], 2) == 0)
     def _():
         ext[0] = outer[0:CH]
         ext[1] = outer[CH : 2 * CH]
-
-    q = project_q(normed[...], wq, cosines[rows], sines[rows])
-    emit(out, attend(far, q, ext, docs))
+        far_tile(ext, normed, wq, cosines, sines, docs, out)
 
 
 def last_body(ext_in, owners, xa, xb, gain, wk, wv, cosines, sines, ext, normed_out, late_out):
@@ -407,9 +415,22 @@
         flops // 2,
         alias=0,
     )
+    ext, far, s2 = call(
+        ahead_body,
+        [slots, piece, piece],
+        [ext, far, normed, w_query, cosines, sines, docs],
+        flops,
+        alias=0,
+        aliases=2,
+    )
     late = across(far, {0: 1, 1: 1, 2: -1})
     ext, s2 = call(
-        far_body, [slots, piece], [ext, outer, normed, w_query, cosines, sines, docs], flops, alias=0
+        far_body,
+        [slots, piece],
+        [ext, s2, outer, normed, w_query, cosines, sines, docs],
+        flops,
+        alias=0,
+        aliases=2,
     )
     s1, s2 = call(second_body, [piece, piece], [s1, s2, ext, q_near, q_rest, docs], scores, alias=0, aliases=2)
     r2 = ring(s2, 2)

time: 61 us -> 60 us (0.984)
  the two profiles are of different devices: /device:TPU:103 before, /device:TPU:128 now
where the time goes in v4:
time: 60 us; the launch traced here: 59.7 us
  waiting for transfers between devices  19.8 us (33%)
  starting transfers between devices  19.4 us (32%)
  Pallas kernels  16.8 us (28%)
  other arithmetic  1.69 us (3%)
  local copies, waits for them, and re-layouts  1.06 us (2%)
  between operations  0.99 us (2%)
    ppermute x9, waiting for transfers between devices, ring(): return lax.ppermute(array, 'tp', [(i, (i + by) % n) for i in range(n)])  17.3 us
    ppermute x9, starting transfers between devices, ring(): return lax.ppermute(array, 'tp', [(i, (i + by) % n) for i in range(n)])  12.3 us
    pallas_call x12, Pallas kernels, call(): pl.pallas_call(body, out_shape=[o if isinstance(o, jax.ShapeDtypeStruct)...  12.1 us
    pallas_call x2, Pallas kernels, mover(): pl.pallas_call(body, out_shape=[VM(s, bf) for s in outs], in_specs=[outsi...  4.73 us
    ppermute x2, starting transfers between devices, swap(): return lax.ppermute(array, 'seq', pairs)  4.39 us
    ppermute x1, starting transfers between devices, across(): return lax.ppermute(array, ('seq', 'tp'), pairs)  2.72 us
    ppermute x1, waiting for transfers between devices, across(): return lax.ppermute(array, ('seq', 'tp'), pairs)  1.6 us
  transfers between devices with their start and end apart: 12, of which 7 were waited for; matrix products, arithmetic and copies ran while one was open for 5% of the time, Pallas kernels for 25%

profile of v4, /device:TPU:128, one launch (start us, length us, event | category | flops | bytes accessed | tf_op | source)
XLA Modules:
  0.0 59.7 jit_solution(17791874192905614822)
XLA Ops:
  0.6 1.2 %shard_map.94 = (bf16[64,4096]{1,0:T(8,128)(2,1)S(1)}, bf16[64,4096]{1,0:T(8,128)(2,1)S(1)}) custom-call(bf16[128,4096]{1,0:T(8,128)(2,1)} %hidden.1), custom_call_target="tpu_custom_call" | custom-call | bytes 2097152 | tf_op jit(solution)/shard_map/pallas_call | solution.py:358
  1.9 3.1 %collective-permute-start.2 = (bf16[64,4096]{1,0:T(8,128)(2,1)S(1)}, bf16[64,4096]{1,0:T(8,128)(2,1)S(1)}, u32[]{:S(2)}, u32[]{:S(2)}) collective-permute-start(bf16[64,4096]{1,0:T(8,128)(2,1)S(1)} %get-tuple-element.33.xa), channel_id=1, source_target_pairs={{0,3},{1,0},{2,1},{3,2},{4,7},{5,4},{6,5},{7,6},{8,11},{9,8},{10,9... | collective-permute-start | bytes 1572872 | tf_op jit(solution)/shard_map/ppermute | solution.py:20
  5.0 0.6 collective-permute-start.3
  5.5 2.7 %collective-permute-start.1 = (bf16[64,4096]{1,0:T(8,128)(2,1)S(1)}, bf16[64,4096]{1,0:T(8,128)(2,1)S(1)}, u32[]{:S(2)}, u32[]{:S(2)}) collective-permute-start(bf16[64,4096]{1,0:T(8,128)(2,1)S(1)} %get-tuple-element.34.xb), channel_id=1, source_target_pairs={{0,3},{1,0},{2,1},{3,2},{4,7},{5,4},{6,5},{7,6},{8,11},{9,8},{10,9... | collective-permute-start | bytes 1572872 | tf_op jit(solution)/shard_map/ppermute | solution.py:20
  8.2 0.7 %broadcast_in_dim.32 = s32[16,32]{1,0:T(8,128)S(1)} broadcast(s32[16]{0:T(128)} %param.13), dimensions={0} | broadcast | bytes 2112 | tf_op jit(solution)/shard_map/broadcast_in_dim | solution.py:382
  9.0 0.7 %subtract_convert_fusion = (f32[512]{0:T(512)S(1)}, s32[512]{0:T(512)S(1)}) fusion(s32[512]{0:T(512)} %param.12, s32[]{:T(128)S(6)} %mul.35), kind=kLoop, calls=%fused_computation.5 | loop fusion | flops 2048 | bytes 6148 | tf_op jit(solution)/shard_map/convert_element_type | solution.py:379
  9.8 0.1 broadcast_in_dim.31.after.docs
  10.0 3.5 %shard_map.95 = (bf16[4096,512]{1,0:T(8,128)(2,1)S(1)}, bf16[4096,256]{1,0:T(8,128)(2,1)S(1)}, bf16[4096,256]{1,0:T(8,128)(2,1)S(1)}) custom-call(bf16[4096,512]{1,0:T(8,128)(2,1)} %wq.1, bf16[4096,256]{1,0:T(8,128)(2,1)} %wk.1, bf16[4096,256]{1,0:T(8,128)(2,1)} %wv.1, s32[512,128]{1,0:T(8,128)S(1)} %broadcast_in_dim.31.after.docs, ...), custom_call_target="tpu_custom_call" | custom-call | bytes 16777216 | tf_op jit(solution)/shard_map/pallas_call | solution.py:358
  13.5 1.0 %fusion = (f32[512,128]{1,0:T(8,128)S(1)}, f32[512,128]{1,0:T(8,128)S(1)}) fusion(f32[128]{0:T(128)S(1)} %get-tuple-element.67, f32[128]{0:T(128)S(1)} %get-tuple-element.68, f32[512]{0:T(512)S(1)} %get-tuple-element.65), kind=kLoop, calls=%fused_computation.2 | loop fusion | flops 131072 | bytes 527360 | tf_op jit(solution)/shard_map/mul | solution.py:380
  14.5 6.4 %collective-permute-done.la = bf16[64,4096]{1,0:T(8,128)(2,1)S(1)} collective-permute-done((bf16[64,4096]{1,0:T(8,128)(2,1)S(1)}, bf16[64,4096]{1,0:T(8,128)(2,1)S(1)}, u32[]{:S(2)}, u32[]{:S(2)}) %collective-permute-start) | collective-permute-done | bytes 524320 | tf_op jit(solution)/shard_map/ppermute | solution.py:20
  21.0 6.4 %collective-permute-done.1.rb = bf16[64,4096]{1,0:T(8,128)(2,1)S(1)} collective-permute-done((bf16[64,4096]{1,0:T(8,128)(2,1)S(1)}, bf16[64,4096]{1,0:T(8,128)(2,1)S(1)}, u32[]{:S(2)}, u32[]{:S(2)}) %collective-permute-start.1) | collective-permute-done | bytes 524320 | tf_op jit(solution)/shard_map/ppermute | solution.py:20
  27.4 3.7 %collective-permute-start.6 = (bf16[64,4096]{1,0:T(8,128)(2,1)S(1)}, bf16[64,4096]{1,0:T(8,128)(2,1)S(1)}, u32[]{:S(2)}, u32[]{:S(2)}) collective-permute-start(bf16[64,4096]{1,0:T(8,128)(2,1)S(1)} %collective-permute-done.1.rb), channel_id=1, source_target_pairs={{0,3},{1,0},{2,1},{3,2},{4,7},{5,4},{6,5},{7,6},{8,11},{9,8},{10,9... | collective-permute-start | bytes 1572872 | tf_op jit(solution)/shard_map/ppermute | solution.py:20
  31.1 1.6 %shard_map.96 = (bf16[6,128,512]{2,1,0:T(8,128)(2,1)S(1)}, bf16[128,512]{1,0:T(8,128)(2,1)S(1)}) custom-call(bf16[64,4096]{1,0:T(8,128)(2,1)S(1)} %get-tuple-element.33.xa, bf16[64,4096]{1,0:T(8,128)(2,1)S(1)} %get-tuple-element.34.xb, f32[1,4096]{1,0:T(1,128)S(1)} %bitcast.1, bf16[4096,512]{1,0:T(8,128)(2,1)S(1)} %get-tuple-element.35.wq, ...), custom_call_target="tpu_custom_call" | custom-call | flops 1073741824 | bytes 9977856 | tf_op jit(solution)/shard_map/pallas_call | solution.py:47
  32.7 1.6 %shard_map.97 = (bf16[6,128,512]{2,1,0:T(8,128)(2,1)S(1)}, bf16[128,512]{1,0:T(8,128)(2,1)S(1)}) custom-call(bf16[6,128,512]{2,1,0:T(8,128)(2,1)S(1)} %get-tuple-element.38.ext_in, bf16[64,4096]{1,0:T(8,128)(2,1)S(1)} %collective-permute-done.la, bf16[64,4096]{1,0:T(8,128)(2,1)S(1)} %collective-permute-done.1.rb, ...), custom_call_target="tpu_custom_call", output_to_operand_aliasing={{0}: (0, {})} | custom-call | flops 1073741824 | bytes 10764288 | tf_op jit(solution)/shard_map/pallas_call | solution.py:47
  34.3 1.1 %shard_map.98 = (bf16[6,128,512]{2,1,0:T(8,128)(2,1)S(1)}, bf16[128,4096]{1,0:T(8,128)(2,1)S(1)}, bf16[272,512]{1,0:T(8,128)(2,1)S(1)}, bf16[272,512]{1,0:T(8,128)(2,1)S(1)}) custom-call(bf16[6,128,512]{2,1,0:T(8,128)(2,1)S(1)} %get-tuple-element.39.ext_in, s32[512,128]{1,0:T(8,128)S(1)} %broadcast_in_dim.34.after_too.owners, ...), custom_call_target="tpu_custom_call", output_to_operand_aliasing={{0}: (0, {})} | custom-call | flops 536870912 | bytes 6832128 | tf_op jit(solution)/shard_map/pallas_call | solution.py:47
  35.6 4.3 %collective-permute-start.7 = (bf16[272,512]{1,0:T(8,128)(2,1)S(1)}, bf16[272,512]{1,0:T(8,128)(2,1)S(1)}, u32[]{:S(2)}, u32[]{:S(2)}) collective-permute-start(bf16[272,512]{1,0:T(8,128)(2,1)S(1)} %get-tuple-element.50), channel_id=1, source_target_pairs={{4,8},{8,4},{12,16},{16,12},{20,24},{24,20},{28,32},{32,28},{36,40... | collective-permute-start | bytes 835592 | tf_op jit(solution)/shard_map/ppermute | solution.py:32
  39.9 0.8 %shard_map.99.q_rest = bf16[128,512]{1,0:T(8,128)(2,1)S(1)} custom-call(bf16[128,4096]{1,0:T(8,128)(2,1)S(1)} %get-tuple-element.43.normed, bf16[4096,512]{1,0:T(8,128)(2,1)S(1)} %get-tuple-element.35.wq, f32[512,128]{1,0:T(8,128)S(1)} %get-tuple-element.64.cosines, f32[512,128]{1,0:T(8,128)S(1)} %get-tuple-element.63.sines), custom_call_target="tpu_custom_call" | custom-call | flops 536870912 | bytes 5767168 | tf_op jit(solution)/shard_map/pallas_call | solution.py:47
  40.7 0.2 shard_map.100
  40.9 1.1 %collective-permute-done.5.xa = bf16[64,4096]{1,0:T(8,128)(2,1)S(1)} collective-permute-done((bf16[64,4096]{1,0:T(8,128)(2,1)S(1)}, bf16[64,4096]{1,0:T(8,128)(2,1)S(1)}, u32[]{:S(2)}, u32[]{:S(2)}) %collective-permute-start.5) | collective-permute-done | bytes 524320 | tf_op jit(solution)/shard_map/ppermute | solution.py:20
  42.0 1.1 %shard_map.101 = (bf16[6,128,512]{2,1,0:T(8,128)(2,1)S(1)}, bf16[128,4096]{1,0:T(8,128)(2,1)S(1)}, bf16[128,512]{1,0:T(8,128)(2,1)S(1)}) custom-call(bf16[6,128,512]{2,1,0:T(8,128)(2,1)S(1)} %get-tuple-element.44.ext_in, s32[512,128]{1,0:T(8,128)S(1)} %broadcast_in_dim.34.after_too.owners, ...), custom_call_target="tpu_custom_call", output_to_operand_aliasing={{0}: (0, {})} | custom-call | flops 536870912 | bytes 6832128 | tf_op jit(solution)/shard_map/pallas_call | solution.py:47
  43.1 2.7 %collective-permute-start.8 = (bf16[128,512]{1,0:T(8,128)(2,1)S(1)}, bf16[128,512]{1,0:T(8,128)(2,1)S(1)}, u32[]{:S(2)}, u32[]{:S(2)}) collective-permute-start(bf16[128,512]{1,0:T(8,128)(2,1)S(1)} %get-tuple-element.52), channel_id=1, source_target_pairs={{0,4},{1,5},{4,8},{5,9},{6,2},{8,12},{9,13},{10,6},{12,16},{13,17}... | collective-permute-start | bytes 393224 | tf_op jit(solution)/shard_map/ppermute | solution.py:26
  45.9 0.9 %collective-permute-done.7.outer = bf16[272,512]{1,0:T(8,128)(2,1)S(1)} collective-permute-done((bf16[272,512]{1,0:T(8,128)(2,1)S(1)}, bf16[272,512]{1,0:T(8,128)(2,1)S(1)}, u32[]{:S(2)}, u32[]{:S(2)}) %collective-permute-start.7) | collective-permute-done | bytes 278560 | tf_op jit(solution)/shard_map/ppermute | solution.py:32
  46.7 1.7 %shard_map.103 = (bf16[6,128,512]{2,1,0:T(8,128)(2,1)S(1)}, bf16[128,512]{1,0:T(8,128)(2,1)S(1)}) custom-call(bf16[6,128,512]{2,1,0:T(8,128)(2,1)S(1)} %get-tuple-element.48.ext_in, bf16[128,512]{1,0:T(8,128)(2,1)S(1)} %get-tuple-element.49.out_in, bf16[272,512]{1,0:T(8,128)(2,1)S(1)} %collective-permute-done.7.outer, ...), custom_call_target="tpu_custom_call", output_to_operand_aliasing={{0}: (0, {}), {1}: (1, {})} | custom-call | flops 1073741824 | bytes 7225344 | tf_op jit(solution)/shard_map/pallas_call | solution.py:47
  48.4 1.0 %shard_map.106 = (bf16[128,512]{1,0:T(8,128)(2,1)S(1)}, bf16[128,512]{1,0:T(8,128)(2,1)S(1)}) custom-call(bf16[128,512]{1,0:T(8,128)(2,1)S(1)} %get-tuple-element.56.out_in, bf16[128,512]{1,0:T(8,128)(2,1)S(1)} %get-tuple-element.57.far_in, bf16[6,128,512]{2,1,0:T(8,128)(2,1)S(1)} %get-tuple-element.51.ext_in.ext, ...), custom_call_target="tpu_custom_call", output_to_operand_aliasing={{0}: (0, {}), {1}: (1, {})} | custom-call | flops 100663296 | bytes 1572864 | tf_op jit(solution)/shard_map/pallas_call | solution.py:47
  49.5 1.6 %collective-permute-start.10 = (bf16[128,512]{1,0:T(8,128)(2,1)S(1)}, bf16[128,512]{1,0:T(8,128)(2,1)S(1)}, u32[]{:S(2)}, u32[]{:S(2)}) collective-permute-start(bf16[128,512]{1,0:T(8,128)(2,1)S(1)} %get-tuple-element.59), channel_id=1, source_target_pairs={{0,2},{1,3},{2,0},{3,1},{4,6},{5,7},{6,4},{7,5},{8,10},{9,11},{10,... | collective-permute-start | bytes 393224 | tf_op jit(solution)/shard_map/ppermute | solution.py:20
  51.1 1.6 %collective-permute-done.8.late = bf16[128,512]{1,0:T(8,128)(2,1)S(1)} collective-permute-done((bf16[128,512]{1,0:T(8,128)(2,1)S(1)}, bf16[128,512]{1,0:T(8,128)(2,1)S(1)}, u32[]{:S(2)}, u32[]{:S(2)}) %collective-permute-start.8) | collective-permute-done | bytes 131104 | tf_op jit(solution)/shard_map/ppermute | solution.py:26
  52.7 1.0 %shard_map.104 = (bf16[6,128,512]{2,1,0:T(8,128)(2,1)S(1)}, bf16[128,512]{1,0:T(8,128)(2,1)S(1)}) custom-call(bf16[6,128,512]{2,1,0:T(8,128)(2,1)S(1)} %get-tuple-element.51.ext_in.ext, bf16[128,512]{1,0:T(8,128)(2,1)S(1)} %collective-permute-done.8.late, bf16[128,512]{1,0:T(8,128)(2,1)S(1)} %get-tuple-element.42.q_near, ...), custom_call_target="tpu_custom_call", output_to_operand_aliasing={{0}: (0, {})} | custom-call | flops 100663296 | bytes 1441792 | tf_op jit(solution)/shard_map/pallas_call | solution.py:47
  53.7 0.6 collective-permute-start.11
  54.3 1.1 %shard_map.105 = (bf16[128,512]{1,0:T(8,128)(2,1)S(1)}, bf16[768,256]{1,0:T(8,128)(2,1)}, bf16[768,256]{1,0:T(8,128)(2,1)}) custom-call(bf16[6,128,512]{2,1,0:T(8,128)(2,1)S(1)} %get-tuple-element.53.ext, s32[512,128]{1,0:T(8,128)S(1)} %broadcast_in_dim.34.after_too.owners, bf16[128,512]{1,0:T(8,128)(2,1)S(1)} %collective-permute-done.8.late, ...), custom_call_target="tpu_custom_call" | custom-call | flops 100663296 | bytes 2129920 | tf_op jit(solution)/shard_map/pallas_call | solution.py:47
  55.4 1.7 %collective-permute-done.9.r1 = bf16[128,512]{1,0:T(8,128)(2,1)S(1)} collective-permute-done((bf16[128,512]{1,0:T(8,128)(2,1)S(1)}, bf16[128,512]{1,0:T(8,128)(2,1)S(1)}, u32[]{:S(2)}, u32[]{:S(2)}) %collective-permute-start.9) | collective-permute-done | bytes 131104 | tf_op jit(solution)/shard_map/ppermute | solution.py:20
  57.1 1.7 %collective-permute-done.11.r3 = bf16[128,512]{1,0:T(8,128)(2,1)S(1)} collective-permute-done((bf16[128,512]{1,0:T(8,128)(2,1)S(1)}, bf16[128,512]{1,0:T(8,128)(2,1)S(1)}, u32[]{:S(2)}, u32[]{:S(2)}) %collective-permute-start.11) | collective-permute-done | bytes 131104 | tf_op jit(solution)/shard_map/ppermute | solution.py:20
  58.8 0.8 %shard_map.107 = bf16[128,2048]{1,0:T(8,128)(2,1)} custom-call(bf16[128,512]{1,0:T(8,128)(2,1)S(1)} %get-tuple-element.55.s0, bf16[128,512]{1,0:T(8,128)(2,1)S(1)} %collective-permute-done.9.r1, bf16[128,512]{1,0:T(8,128)(2,1)S(1)} %collective-permute-done.10.r2, bf16[128,512]{1,0:T(8,128)(2,1)S(1)} %collective-permute-done.11.r3), custom_call_target="tpu_custom_call" | custom-call | bytes 524288 | tf_op jit(solution)/shard_map/pallas_call | solution.py:47
  (15 shorter events, 0.4 us)
Async XLA Ops:
  1.9 32.5 %collective-permute-start.2 = (bf16[64,4096]{1,0:T(8,128)(2,1)S(1)}, bf16[64,4096]{1,0:T(8,128)(2,1)S(1)}, u32[]{:S(2)}, u32[]{:S(2)}) collective-permute-start(bf16[64,4096]{1,0:T(8,128)(2,1)S(1)} %get-tuple-element.33.xa), channel_id=1, source_target_pairs={{0,3},{1,0},{2,1},{3,2},{4,7},{5,4},{6,5},{7,6},{8,11},{9,8},{10,9... | collective-permute-start | bytes 1572872 | tf_op jit(solution)/shard_map/ppermute | solution.py:20
  4.9 16.0 %collective-permute-start = (bf16[64,4096]{1,0:T(8,128)(2,1)S(1)}, bf16[64,4096]{1,0:T(8,128)(2,1)S(1)}, u32[]{:S(2)}, u32[]{:S(2)}) collective-permute-start(bf16[64,4096]{1,0:T(8,128)(2,1)S(1)} %get-tuple-element.33.xa), channel_id=1, source_target_pairs={{0,1},{1,2},{2,3},{3,0},{4,5},{5,6},{6,7},{7,4},{8,9},{9,10},{10,1... | collective-permute-start | bytes 1572872 | tf_op jit(solution)/shard_map/ppermute | solution.py:20
  5.0 29.4 %collective-permute-start.3 = (bf16[64,4096]{1,0:T(8,128)(2,1)S(1)}, bf16[64,4096]{1,0:T(8,128)(2,1)S(1)}, u32[]{:S(2)}, u32[]{:S(2)}) collective-permute-start(bf16[64,4096]{1,0:T(8,128)(2,1)S(1)} %get-tuple-element.34.xb), channel_id=1, source_target_pairs={{0,1},{1,2},{2,3},{3,0},{4,5},{5,6},{6,7},{7,4},{8,9},{9,10},{10,1... | collective-permute-start | bytes 1572872 | tf_op jit(solution)/shard_map/ppermute | solution.py:20
  5.5 21.8 %collective-permute-start.1 = (bf16[64,4096]{1,0:T(8,128)(2,1)S(1)}, bf16[64,4096]{1,0:T(8,128)(2,1)S(1)}, u32[]{:S(2)}, u32[]{:S(2)}) collective-permute-start(bf16[64,4096]{1,0:T(8,128)(2,1)S(1)} %get-tuple-element.34.xb), channel_id=1, source_target_pairs={{0,3},{1,0},{2,1},{3,2},{4,7},{5,4},{6,5},{7,6},{8,11},{9,8},{10,9... | collective-permute-start | bytes 1572872 | tf_op jit(solution)/shard_map/ppermute | solution.py:20
  10.0 21.1 %copy-start = (f32[4096]{0:T(1024)S(1)}, f32[4096]{0:T(1024)}, u32[]{:S(2)}) copy-start(f32[4096]{0:T(1024)} %param.8) | copy-start | bytes 49156
  21.0 21.1 %collective-permute-start.5 = (bf16[64,4096]{1,0:T(8,128)(2,1)S(1)}, bf16[64,4096]{1,0:T(8,128)(2,1)S(1)}, u32[]{:S(2)}, u32[]{:S(2)}) collective-permute-start(bf16[64,4096]{1,0:T(8,128)(2,1)S(1)} %collective-permute-done.la), channel_id=1, source_target_pairs={{0,1},{1,2},{2,3},{3,0},{4,5},{5,6},{6,7},{7,4},{8,9},{9,10},{10,1... | collective-permute-start | bytes 1572872 | tf_op jit(solution)/shard_map/ppermute | solution.py:20
  27.4 14.7 %collective-permute-start.6 = (bf16[64,4096]{1,0:T(8,128)(2,1)S(1)}, bf16[64,4096]{1,0:T(8,128)(2,1)S(1)}, u32[]{:S(2)}, u32[]{:S(2)}) collective-permute-start(bf16[64,4096]{1,0:T(8,128)(2,1)S(1)} %collective-permute-done.1.rb), channel_id=1, source_target_pairs={{0,3},{1,0},{2,1},{3,2},{4,7},{5,4},{6,5},{7,6},{8,11},{9,8},{10,9... | collective-permute-start | bytes 1572872 | tf_op jit(solution)/shard_map/ppermute | solution.py:20
  35.5 5.2 %collective-permute-start.4 = (bf16[272,512]{1,0:T(8,128)(2,1)S(1)}, bf16[272,512]{1,0:T(8,128)(2,1)S(1)}, u32[]{:S(2)}, u32[]{:S(2)}) collective-permute-start(bf16[272,512]{1,0:T(8,128)(2,1)S(1)} %get-tuple-element.41), channel_id=1, source_target_pairs={{0,4},{4,0},{8,12},{12,8},{16,20},{20,16},{24,28},{28,24},{32,36},... | collective-permute-start | bytes 835592 | tf_op jit(solution)/shard_map/ppermute | solution.py:32
  35.6 11.2 %collective-permute-start.7 = (bf16[272,512]{1,0:T(8,128)(2,1)S(1)}, bf16[272,512]{1,0:T(8,128)(2,1)S(1)}, u32[]{:S(2)}, u32[]{:S(2)}) collective-permute-start(bf16[272,512]{1,0:T(8,128)(2,1)S(1)} %get-tuple-element.50), channel_id=1, source_target_pairs={{4,8},{8,4},{12,16},{16,12},{20,24},{24,20},{28,32},{32,28},{36,40... | collective-permute-start | bytes 835592 | tf_op jit(solution)/shard_map/ppermute | solution.py:32
  43.1 9.6 %collective-permute-start.8 = (bf16[128,512]{1,0:T(8,128)(2,1)S(1)}, bf16[128,512]{1,0:T(8,128)(2,1)S(1)}, u32[]{:S(2)}, u32[]{:S(2)}) collective-permute-start(bf16[128,512]{1,0:T(8,128)(2,1)S(1)} %get-tuple-element.52), channel_id=1, source_target_pairs={{0,4},{1,5},{4,8},{5,9},{6,2},{8,12},{9,13},{10,6},{12,16},{13,17}... | collective-permute-start | bytes 393224 | tf_op jit(solution)/shard_map/ppermute | solution.py:26
  49.4 7.7 %collective-permute-start.9 = (bf16[128,512]{1,0:T(8,128)(2,1)S(1)}, bf16[128,512]{1,0:T(8,128)(2,1)S(1)}, u32[]{:S(2)}, u32[]{:S(2)}) collective-permute-start(bf16[128,512]{1,0:T(8,128)(2,1)S(1)} %get-tuple-element.58), channel_id=1, source_target_pairs={{0,1},{1,2},{2,3},{3,0},{4,5},{5,6},{6,7},{7,4},{8,9},{9,10},{10,1... | collective-permute-start | bytes 393224 | tf_op jit(solution)/shard_map/ppermute | solution.py:20
  49.5 7.6 %collective-permute-start.10 = (bf16[128,512]{1,0:T(8,128)(2,1)S(1)}, bf16[128,512]{1,0:T(8,128)(2,1)S(1)}, u32[]{:S(2)}, u32[]{:S(2)}) collective-permute-start(bf16[128,512]{1,0:T(8,128)(2,1)S(1)} %get-tuple-element.59), channel_id=1, source_target_pairs={{0,2},{1,3},{2,0},{3,1},{4,6},{5,7},{6,4},{7,5},{8,10},{9,11},{10,... | collective-permute-start | bytes 393224 | tf_op jit(solution)/shard_map/ppermute | solution.py:20
  53.7 5.0 %collective-permute-start.11 = (bf16[128,512]{1,0:T(8,128)(2,1)S(1)}, bf16[128,512]{1,0:T(8,128)(2,1)S(1)}, u32[]{:S(2)}, u32[]{:S(2)}) collective-permute-start(bf16[128,512]{1,0:T(8,128)(2,1)S(1)} %get-tuple-element.60), channel_id=1, source_target_pairs={{0,3},{1,0},{2,1},{3,2},{4,7},{5,4},{6,5},{7,6},{8,11},{9,8},{10,9... | collective-permute-start | bytes 393224 | tf_op jit(solution)/shard_map/ppermute | solution.py:20

commit v5 on v4

--- a/solution.py
+++ b/solution.py
@@ -234,8 +234,13 @@
     emit(out, attend(far, q, ext, docs))
 
 
+def far_is_ahead():
+    own, _, _, _, home = spots()
+    return (lax.rem(home, 2) == 1) & (own != 2)
+
+
 def ahead_body(ext_in, late_in, normed, wq, cosines, sines, docs, ext, late_out, out):
-    @pl.when(lax.rem(spots()[4], 2) == 1)
+    @pl.when(far_is_ahead())
     def _():
         far_tile(ext, normed, wq, cosines, sines, docs, out)
 
@@ -245,6 +250,9 @@
     def _():
         ext[0] = outer[0:CH]
         ext[1] = outer[CH : 2 * CH]
+
+    @pl.when(jnp.logical_not(far_is_ahead()))
+    def _():
         far_tile(ext, normed, wq, cosines, sines, docs, out)
 
 

time: 60 us -> 60 us (level)
  no operation moved by 1% of the time
where the time goes in v5:
time: 60 us; the launch traced here: 59.7 us
  waiting for transfers between devices  20.2 us (34%)
  starting transfers between devices  19 us (32%)
  Pallas kernels  16.9 us (28%)
  other arithmetic  1.69 us (3%)
  local copies, waits for them, and re-layouts  1.06 us (2%)
  between operations  0.99 us (2%)
    ppermute x9, waiting for transfers between devices, ring(): return lax.ppermute(array, 'tp', [(i, (i + by) % n) for i in range(n)])  17.7 us
    pallas_call x12, Pallas kernels, call(): pl.pallas_call(body, out_shape=[o if isinstance(o, jax.ShapeDtypeStruct)...  12.1 us
    ppermute x9, starting transfers between devices, ring(): return lax.ppermute(array, 'tp', [(i, (i + by) % n) for i in range(n)])  11.9 us
    pallas_call x2, Pallas kernels, mover(): pl.pallas_call(body, out_shape=[VM(s, bf) for s in outs], in_specs=[outsi...  4.73 us
    ppermute x2, starting transfers between devices, swap(): return lax.ppermute(array, 'seq', pairs)  4.39 us
    ppermute x1, starting transfers between devices, across(): return lax.ppermute(array, ('seq', 'tp'), pairs)  2.72 us
    ppermute x1, waiting for transfers between devices, across(): return lax.ppermute(array, ('seq', 'tp'), pairs)  1.57 us
  transfers between devices with their start and end apart: 12, of which 7 were waited for; matrix products, arithmetic and copies ran while one was open for 5% of the time, Pallas kernels for 25%

profile of v5, /device:TPU:128, one launch (start us, length us, event | category | flops | bytes accessed | tf_op | source)
XLA Modules:
  0.0 59.7 jit_solution(10585236073319348970)
XLA Ops:
  0.6 1.2 %shard_map.94 = (bf16[64,4096]{1,0:T(8,128)(2,1)S(1)}, bf16[64,4096]{1,0:T(8,128)(2,1)S(1)}) custom-call(bf16[128,4096]{1,0:T(8,128)(2,1)} %hidden.1), custom_call_target="tpu_custom_call" | custom-call | bytes 2097152 | tf_op jit(solution)/shard_map/pallas_call | solution.py:366
  1.9 3.1 %collective-permute-start.2 = (bf16[64,4096]{1,0:T(8,128)(2,1)S(1)}, bf16[64,4096]{1,0:T(8,128)(2,1)S(1)}, u32[]{:S(2)}, u32[]{:S(2)}) collective-permute-start(bf16[64,4096]{1,0:T(8,128)(2,1)S(1)} %get-tuple-element.33.xa), channel_id=1, source_target_pairs={{0,3},{1,0},{2,1},{3,2},{4,7},{5,4},{6,5},{7,6},{8,11},{9,8},{10,9... | collective-permute-start | bytes 1572872 | tf_op jit(solution)/shard_map/ppermute | solution.py:20
  5.0 0.6 collective-permute-start.3
  5.5 2.7 %collective-permute-start.1 = (bf16[64,4096]{1,0:T(8,128)(2,1)S(1)}, bf16[64,4096]{1,0:T(8,128)(2,1)S(1)}, u32[]{:S(2)}, u32[]{:S(2)}) collective-permute-start(bf16[64,4096]{1,0:T(8,128)(2,1)S(1)} %get-tuple-element.34.xb), channel_id=1, source_target_pairs={{0,3},{1,0},{2,1},{3,2},{4,7},{5,4},{6,5},{7,6},{8,11},{9,8},{10,9... | collective-permute-start | bytes 1572872 | tf_op jit(solution)/shard_map/ppermute | solution.py:20
  8.2 0.7 %broadcast_in_dim.32 = s32[16,32]{1,0:T(8,128)S(1)} broadcast(s32[16]{0:T(128)} %param.13), dimensions={0} | broadcast | bytes 2112 | tf_op jit(solution)/shard_map/broadcast_in_dim | solution.py:390
  9.0 0.7 %subtract_convert_fusion = (f32[512]{0:T(512)S(1)}, s32[512]{0:T(512)S(1)}) fusion(s32[512]{0:T(512)} %param.12, s32[]{:T(128)S(6)} %mul.35), kind=kLoop, calls=%fused_computation.5 | loop fusion | flops 2048 | bytes 6148 | tf_op jit(solution)/shard_map/convert_element_type | solution.py:387
  9.8 0.1 broadcast_in_dim.31.after.docs
  10.0 3.5 %shard_map.95 = (bf16[4096,512]{1,0:T(8,128)(2,1)S(1)}, bf16[4096,256]{1,0:T(8,128)(2,1)S(1)}, bf16[4096,256]{1,0:T(8,128)(2,1)S(1)}) custom-call(bf16[4096,512]{1,0:T(8,128)(2,1)} %wq.1, bf16[4096,256]{1,0:T(8,128)(2,1)} %wk.1, bf16[4096,256]{1,0:T(8,128)(2,1)} %wv.1, s32[512,128]{1,0:T(8,128)S(1)} %broadcast_in_dim.31.after.docs, ...), custom_call_target="tpu_custom_call" | custom-call | bytes 16777216 | tf_op jit(solution)/shard_map/pallas_call | solution.py:366
  13.5 1.0 %fusion = (f32[512,128]{1,0:T(8,128)S(1)}, f32[512,128]{1,0:T(8,128)S(1)}) fusion(f32[128]{0:T(128)S(1)} %get-tuple-element.67, f32[128]{0:T(128)S(1)} %get-tuple-element.68, f32[512]{0:T(512)S(1)} %get-tuple-element.65), kind=kLoop, calls=%fused_computation.2 | loop fusion | flops 131072 | bytes 527360 | tf_op jit(solution)/shard_map/mul | solution.py:388
  14.5 6.4 %collective-permute-done.la = bf16[64,4096]{1,0:T(8,128)(2,1)S(1)} collective-permute-done((bf16[64,4096]{1,0:T(8,128)(2,1)S(1)}, bf16[64,4096]{1,0:T(8,128)(2,1)S(1)}, u32[]{:S(2)}, u32[]{:S(2)}) %collective-permute-start) | collective-permute-done | bytes 524320 | tf_op jit(solution)/shard_map/ppermute | solution.py:20
  21.0 6.4 %collective-permute-done.1.rb = bf16[64,4096]{1,0:T(8,128)(2,1)S(1)} collective-permute-done((bf16[64,4096]{1,0:T(8,128)(2,1)S(1)}, bf16[64,4096]{1,0:T(8,128)(2,1)S(1)}, u32[]{:S(2)}, u32[]{:S(2)}) %collective-permute-start.1) | collective-permute-done | bytes 524320 | tf_op jit(solution)/shard_map/ppermute | solution.py:20
  27.4 3.7 %collective-permute-start.6 = (bf16[64,4096]{1,0:T(8,128)(2,1)S(1)}, bf16[64,4096]{1,0:T(8,128)(2,1)S(1)}, u32[]{:S(2)}, u32[]{:S(2)}) collective-permute-start(bf16[64,4096]{1,0:T(8,128)(2,1)S(1)} %collective-permute-done.1.rb), channel_id=1, source_target_pairs={{0,3},{1,0},{2,1},{3,2},{4,7},{5,4},{6,5},{7,6},{8,11},{9,8},{10,9... | collective-permute-start | bytes 1572872 | tf_op jit(solution)/shard_map/ppermute | solution.py:20
  31.1 1.6 %shard_map.96 = (bf16[6,128,512]{2,1,0:T(8,128)(2,1)S(1)}, bf16[128,512]{1,0:T(8,128)(2,1)S(1)}) custom-call(bf16[64,4096]{1,0:T(8,128)(2,1)S(1)} %get-tuple-element.33.xa, bf16[64,4096]{1,0:T(8,128)(2,1)S(1)} %get-tuple-element.34.xb, f32[1,4096]{1,0:T(1,128)S(1)} %bitcast.1, bf16[4096,512]{1,0:T(8,128)(2,1)S(1)} %get-tuple-element.35.wq, ...), custom_call_target="tpu_custom_call" | custom-call | flops 1073741824 | bytes 9977856 | tf_op jit(solution)/shard_map/pallas_call | solution.py:47
  32.7 1.6 %shard_map.97 = (bf16[6,128,512]{2,1,0:T(8,128)(2,1)S(1)}, bf16[128,512]{1,0:T(8,128)(2,1)S(1)}) custom-call(bf16[6,128,512]{2,1,0:T(8,128)(2,1)S(1)} %get-tuple-element.38.ext_in, bf16[64,4096]{1,0:T(8,128)(2,1)S(1)} %collective-permute-done.la, bf16[64,4096]{1,0:T(8,128)(2,1)S(1)} %collective-permute-done.1.rb, ...), custom_call_target="tpu_custom_call", output_to_operand_aliasing={{0}: (0, {})} | custom-call | flops 1073741824 | bytes 10764288 | tf_op jit(solution)/shard_map/pallas_call | solution.py:47
  34.3 1.1 %shard_map.98 = (bf16[6,128,512]{2,1,0:T(8,128)(2,1)S(1)}, bf16[128,4096]{1,0:T(8,128)(2,1)S(1)}, bf16[272,512]{1,0:T(8,128)(2,1)S(1)}, bf16[272,512]{1,0:T(8,128)(2,1)S(1)}) custom-call(bf16[6,128,512]{2,1,0:T(8,128)(2,1)S(1)} %get-tuple-element.39.ext_in, s32[512,128]{1,0:T(8,128)S(1)} %broadcast_in_dim.34.after_too.owners, ...), custom_call_target="tpu_custom_call", output_to_operand_aliasing={{0}: (0, {})} | custom-call | flops 536870912 | bytes 6832128 | tf_op jit(solution)/shard_map/pallas_call | solution.py:47
  35.6 4.3 %collective-permute-start.7 = (bf16[272,512]{1,0:T(8,128)(2,1)S(1)}, bf16[272,512]{1,0:T(8,128)(2,1)S(1)}, u32[]{:S(2)}, u32[]{:S(2)}) collective-permute-start(bf16[272,512]{1,0:T(8,128)(2,1)S(1)} %get-tuple-element.50), channel_id=1, source_target_pairs={{4,8},{8,4},{12,16},{16,12},{20,24},{24,20},{28,32},{32,28},{36,40... | collective-permute-start | bytes 835592 | tf_op jit(solution)/shard_map/ppermute | solution.py:32
  39.9 0.8 %shard_map.99.q_rest = bf16[128,512]{1,0:T(8,128)(2,1)S(1)} custom-call(bf16[128,4096]{1,0:T(8,128)(2,1)S(1)} %get-tuple-element.43.normed, bf16[4096,512]{1,0:T(8,128)(2,1)S(1)} %get-tuple-element.35.wq, f32[512,128]{1,0:T(8,128)S(1)} %get-tuple-element.64.cosines, f32[512,128]{1,0:T(8,128)S(1)} %get-tuple-element.63.sines), custom_call_target="tpu_custom_call" | custom-call | flops 536870912 | bytes 5767168 | tf_op jit(solution)/shard_map/pallas_call | solution.py:47
  40.7 0.2 shard_map.100
  40.9 1.1 %collective-permute-done.5.xa = bf16[64,4096]{1,0:T(8,128)(2,1)S(1)} collective-permute-done((bf16[64,4096]{1,0:T(8,128)(2,1)S(1)}, bf16[64,4096]{1,0:T(8,128)(2,1)S(1)}, u32[]{:S(2)}, u32[]{:S(2)}) %collective-permute-start.5) | collective-permute-done | bytes 524320 | tf_op jit(solution)/shard_map/ppermute | solution.py:20
  42.0 1.1 %shard_map.101 = (bf16[6,128,512]{2,1,0:T(8,128)(2,1)S(1)}, bf16[128,4096]{1,0:T(8,128)(2,1)S(1)}, bf16[128,512]{1,0:T(8,128)(2,1)S(1)}) custom-call(bf16[6,128,512]{2,1,0:T(8,128)(2,1)S(1)} %get-tuple-element.44.ext_in, s32[512,128]{1,0:T(8,128)S(1)} %broadcast_in_dim.34.after_too.owners, ...), custom_call_target="tpu_custom_call", output_to_operand_aliasing={{0}: (0, {})} | custom-call | flops 536870912 | bytes 6832128 | tf_op jit(solution)/shard_map/pallas_call | solution.py:47
  43.1 2.7 %collective-permute-start.8 = (bf16[128,512]{1,0:T(8,128)(2,1)S(1)}, bf16[128,512]{1,0:T(8,128)(2,1)S(1)}, u32[]{:S(2)}, u32[]{:S(2)}) collective-permute-start(bf16[128,512]{1,0:T(8,128)(2,1)S(1)} %get-tuple-element.52), channel_id=1, source_target_pairs={{0,4},{1,5},{4,8},{5,9},{6,2},{8,12},{9,13},{10,6},{12,16},{13,17}... | collective-permute-start | bytes 393224 | tf_op jit(solution)/shard_map/ppermute | solution.py:26
  45.9 0.9 %collective-permute-done.7.outer = bf16[272,512]{1,0:T(8,128)(2,1)S(1)} collective-permute-done((bf16[272,512]{1,0:T(8,128)(2,1)S(1)}, bf16[272,512]{1,0:T(8,128)(2,1)S(1)}, u32[]{:S(2)}, u32[]{:S(2)}) %collective-permute-start.7) | collective-permute-done | bytes 278560 | tf_op jit(solution)/shard_map/ppermute | solution.py:32
  46.7 1.7 %shard_map.103 = (bf16[6,128,512]{2,1,0:T(8,128)(2,1)S(1)}, bf16[128,512]{1,0:T(8,128)(2,1)S(1)}) custom-call(bf16[6,128,512]{2,1,0:T(8,128)(2,1)S(1)} %get-tuple-element.48.ext_in, bf16[128,512]{1,0:T(8,128)(2,1)S(1)} %get-tuple-element.49.out_in, bf16[272,512]{1,0:T(8,128)(2,1)S(1)} %collective-permute-done.7.outer, ...), custom_call_target="tpu_custom_call", output_to_operand_aliasing={{0}: (0, {}), {1}: (1, {})} | custom-call | flops 1073741824 | bytes 7225344 | tf_op jit(solution)/shard_map/pallas_call | solution.py:47
  48.5 1.0 %shard_map.106 = (bf16[128,512]{1,0:T(8,128)(2,1)S(1)}, bf16[128,512]{1,0:T(8,128)(2,1)S(1)}) custom-call(bf16[128,512]{1,0:T(8,128)(2,1)S(1)} %get-tuple-element.56.out_in, bf16[128,512]{1,0:T(8,128)(2,1)S(1)} %get-tuple-element.57.far_in, bf16[6,128,512]{2,1,0:T(8,128)(2,1)S(1)} %get-tuple-element.51.ext_in.ext, ...), custom_call_target="tpu_custom_call", output_to_operand_aliasing={{0}: (0, {}), {1}: (1, {})} | custom-call | flops 100663296 | bytes 1572864 | tf_op jit(solution)/shard_map/pallas_call | solution.py:47
  49.6 1.6 %collective-permute-start.10 = (bf16[128,512]{1,0:T(8,128)(2,1)S(1)}, bf16[128,512]{1,0:T(8,128)(2,1)S(1)}, u32[]{:S(2)}, u32[]{:S(2)}) collective-permute-start(bf16[128,512]{1,0:T(8,128)(2,1)S(1)} %get-tuple-element.59), channel_id=1, source_target_pairs={{0,2},{1,3},{2,0},{3,1},{4,6},{5,7},{6,4},{7,5},{8,10},{9,11},{10,... | collective-permute-start | bytes 393224 | tf_op jit(solution)/shard_map/ppermute | solution.py:20
  51.2 1.6 %collective-permute-done.8.late = bf16[128,512]{1,0:T(8,128)(2,1)S(1)} collective-permute-done((bf16[128,512]{1,0:T(8,128)(2,1)S(1)}, bf16[128,512]{1,0:T(8,128)(2,1)S(1)}, u32[]{:S(2)}, u32[]{:S(2)}) %collective-permute-start.8) | collective-permute-done | bytes 131104 | tf_op jit(solution)/shard_map/ppermute | solution.py:26
  52.7 1.0 %shard_map.104 = (bf16[6,128,512]{2,1,0:T(8,128)(2,1)S(1)}, bf16[128,512]{1,0:T(8,128)(2,1)S(1)}) custom-call(bf16[6,128,512]{2,1,0:T(8,128)(2,1)S(1)} %get-tuple-element.51.ext_in.ext, bf16[128,512]{1,0:T(8,128)(2,1)S(1)} %collective-permute-done.8.late, bf16[128,512]{1,0:T(8,128)(2,1)S(1)} %get-tuple-element.42.q_near, ...), custom_call_target="tpu_custom_call", output_to_operand_aliasing={{0}: (0, {})} | custom-call | flops 100663296 | bytes 1441792 | tf_op jit(solution)/shard_map/pallas_call | solution.py:47
  53.7 0.1 collective-permute-start.11
  53.9 1.1 %shard_map.105 = (bf16[128,512]{1,0:T(8,128)(2,1)S(1)}, bf16[768,256]{1,0:T(8,128)(2,1)}, bf16[768,256]{1,0:T(8,128)(2,1)}) custom-call(bf16[6,128,512]{2,1,0:T(8,128)(2,1)S(1)} %get-tuple-element.53.ext, s32[512,128]{1,0:T(8,128)S(1)} %broadcast_in_dim.34.after_too.owners, bf16[128,512]{1,0:T(8,128)(2,1)S(1)} %collective-permute-done.8.late, ...), custom_call_target="tpu_custom_call" | custom-call | flops 100663296 | bytes 2129920 | tf_op jit(solution)/shard_map/pallas_call | solution.py:47
  55.0 2.1 %collective-permute-done.9.r1 = bf16[128,512]{1,0:T(8,128)(2,1)S(1)} collective-permute-done((bf16[128,512]{1,0:T(8,128)(2,1)S(1)}, bf16[128,512]{1,0:T(8,128)(2,1)S(1)}, u32[]{:S(2)}, u32[]{:S(2)}) %collective-permute-start.9) | collective-permute-done | bytes 131104 | tf_op jit(solution)/shard_map/ppermute | solution.py:20
  57.1 1.6 %collective-permute-done.11.r3 = bf16[128,512]{1,0:T(8,128)(2,1)S(1)} collective-permute-done((bf16[128,512]{1,0:T(8,128)(2,1)S(1)}, bf16[128,512]{1,0:T(8,128)(2,1)S(1)}, u32[]{:S(2)}, u32[]{:S(2)}) %collective-permute-start.11) | collective-permute-done | bytes 131104 | tf_op jit(solution)/shard_map/ppermute | solution.py:20
  58.8 0.8 %shard_map.107 = bf16[128,2048]{1,0:T(8,128)(2,1)} custom-call(bf16[128,512]{1,0:T(8,128)(2,1)S(1)} %get-tuple-element.55.s0, bf16[128,512]{1,0:T(8,128)(2,1)S(1)} %collective-permute-done.9.r1, bf16[128,512]{1,0:T(8,128)(2,1)S(1)} %collective-permute-done.10.r2, bf16[128,512]{1,0:T(8,128)(2,1)S(1)} %collective-permute-done.11.r3), custom_call_target="tpu_custom_call" | custom-call | bytes 524288 | tf_op jit(solution)/shard_map/pallas_call | solution.py:47
  (15 shorter events, 0.4 us)
Async XLA Ops:
  1.9 32.5 %collective-permute-start.2 = (bf16[64,4096]{1,0:T(8,128)(2,1)S(1)}, bf16[64,4096]{1,0:T(8,128)(2,1)S(1)}, u32[]{:S(2)}, u32[]{:S(2)}) collective-permute-start(bf16[64,4096]{1,0:T(8,128)(2,1)S(1)} %get-tuple-element.33.xa), channel_id=1, source_target_pairs={{0,3},{1,0},{2,1},{3,2},{4,7},{5,4},{6,5},{7,6},{8,11},{9,8},{10,9... | collective-permute-start | bytes 1572872 | tf_op jit(solution)/shard_map/ppermute | solution.py:20
  4.9 16.0 %collective-permute-start = (bf16[64,4096]{1,0:T(8,128)(2,1)S(1)}, bf16[64,4096]{1,0:T(8,128)(2,1)S(1)}, u32[]{:S(2)}, u32[]{:S(2)}) collective-permute-start(bf16[64,4096]{1,0:T(8,128)(2,1)S(1)} %get-tuple-element.33.xa), channel_id=1, source_target_pairs={{0,1},{1,2},{2,3},{3,0},{4,5},{5,6},{6,7},{7,4},{8,9},{9,10},{10,1... | collective-permute-start | bytes 1572872 | tf_op jit(solution)/shard_map/ppermute | solution.py:20
  5.0 29.4 %collective-permute-start.3 = (bf16[64,4096]{1,0:T(8,128)(2,1)S(1)}, bf16[64,4096]{1,0:T(8,128)(2,1)S(1)}, u32[]{:S(2)}, u32[]{:S(2)}) collective-permute-start(bf16[64,4096]{1,0:T(8,128)(2,1)S(1)} %get-tuple-element.34.xb), channel_id=1, source_target_pairs={{0,1},{1,2},{2,3},{3,0},{4,5},{5,6},{6,7},{7,4},{8,9},{9,10},{10,1... | collective-permute-start | bytes 1572872 | tf_op jit(solution)/shard_map/ppermute | solution.py:20
  5.5 21.8 %collective-permute-start.1 = (bf16[64,4096]{1,0:T(8,128)(2,1)S(1)}, bf16[64,4096]{1,0:T(8,128)(2,1)S(1)}, u32[]{:S(2)}, u32[]{:S(2)}) collective-permute-start(bf16[64,4096]{1,0:T(8,128)(2,1)S(1)} %get-tuple-element.34.xb), channel_id=1, source_target_pairs={{0,3},{1,0},{2,1},{3,2},{4,7},{5,4},{6,5},{7,6},{8,11},{9,8},{10,9... | collective-permute-start | bytes 1572872 | tf_op jit(solution)/shard_map/ppermute | solution.py:20
  10.0 21.1 %copy-start = (f32[4096]{0:T(1024)S(1)}, f32[4096]{0:T(1024)}, u32[]{:S(2)}) copy-start(f32[4096]{0:T(1024)} %param.8) | copy-start | bytes 49156
  21.0 21.1 %collective-permute-start.5 = (bf16[64,4096]{1,0:T(8,128)(2,1)S(1)}, bf16[64,4096]{1,0:T(8,128)(2,1)S(1)}, u32[]{:S(2)}, u32[]{:S(2)}) collective-permute-start(bf16[64,4096]{1,0:T(8,128)(2,1)S(1)} %collective-permute-done.la), channel_id=1, source_target_pairs={{0,1},{1,2},{2,3},{3,0},{4,5},{5,6},{6,7},{7,4},{8,9},{9,10},{10,1... | collective-permute-start | bytes 1572872 | tf_op jit(solution)/shard_map/ppermute | solution.py:20
  27.4 14.7 %collective-permute-start.6 = (bf16[64,4096]{1,0:T(8,128)(2,1)S(1)}, bf16[64,4096]{1,0:T(8,128)(2,1)S(1)}, u32[]{:S(2)}, u32[]{:S(2)}) collective-permute-start(bf16[64,4096]{1,0:T(8,128)(2,1)S(1)} %collective-permute-done.1.rb), channel_id=1, source_target_pairs={{0,3},{1,0},{2,1},{3,2},{4,7},{5,4},{6,5},{7,6},{8,11},{9,8},{10,9... | collective-permute-start | bytes 1572872 | tf_op jit(solution)/shard_map/ppermute | solution.py:20
  35.5 5.2 %collective-permute-start.4 = (bf16[272,512]{1,0:T(8,128)(2,1)S(1)}, bf16[272,512]{1,0:T(8,128)(2,1)S(1)}, u32[]{:S(2)}, u32[]{:S(2)}) collective-permute-start(bf16[272,512]{1,0:T(8,128)(2,1)S(1)} %get-tuple-element.41), channel_id=1, source_target_pairs={{0,4},{4,0},{8,12},{12,8},{16,20},{20,16},{24,28},{28,24},{32,36},... | collective-permute-start | bytes 835592 | tf_op jit(solution)/shard_map/ppermute | solution.py:32
  35.6 11.2 %collective-permute-start.7 = (bf16[272,512]{1,0:T(8,128)(2,1)S(1)}, bf16[272,512]{1,0:T(8,128)(2,1)S(1)}, u32[]{:S(2)}, u32[]{:S(2)}) collective-permute-start(bf16[272,512]{1,0:T(8,128)(2,1)S(1)} %get-tuple-element.50), channel_id=1, source_target_pairs={{4,8},{8,4},{12,16},{16,12},{20,24},{24,20},{28,32},{32,28},{36,40... | collective-permute-start | bytes 835592 | tf_op jit(solution)/shard_map/ppermute | solution.py:32
  43.1 9.6 %collective-permute-start.8 = (bf16[128,512]{1,0:T(8,128)(2,1)S(1)}, bf16[128,512]{1,0:T(8,128)(2,1)S(1)}, u32[]{:S(2)}, u32[]{:S(2)}) collective-permute-start(bf16[128,512]{1,0:T(8,128)(2,1)S(1)} %get-tuple-element.52), channel_id=1, source_target_pairs={{0,4},{1,5},{4,8},{5,9},{6,2},{8,12},{9,13},{10,6},{12,16},{13,17}... | collective-permute-start | bytes 393224 | tf_op jit(solution)/shard_map/ppermute | solution.py:26
  49.5 7.7 %collective-permute-start.9 = (bf16[128,512]{1,0:T(8,128)(2,1)S(1)}, bf16[128,512]{1,0:T(8,128)(2,1)S(1)}, u32[]{:S(2)}, u32[]{:S(2)}) collective-permute-start(bf16[128,512]{1,0:T(8,128)(2,1)S(1)} %get-tuple-element.58), channel_id=1, source_target_pairs={{0,1},{1,2},{2,3},{3,0},{4,5},{5,6},{6,7},{7,4},{8,9},{9,10},{10,1... | collective-permute-start | bytes 393224 | tf_op jit(solution)/shard_map/ppermute | solution.py:20
  49.6 7.6 %collective-permute-start.10 = (bf16[128,512]{1,0:T(8,128)(2,1)S(1)}, bf16[128,512]{1,0:T(8,128)(2,1)S(1)}, u32[]{:S(2)}, u32[]{:S(2)}) collective-permute-start(bf16[128,512]{1,0:T(8,128)(2,1)S(1)} %get-tuple-element.59), channel_id=1, source_target_pairs={{0,2},{1,3},{2,0},{3,1},{4,6},{5,7},{6,4},{7,5},{8,10},{9,11},{10,... | collective-permute-start | bytes 393224 | tf_op jit(solution)/shard_map/ppermute | solution.py:20
  53.7 5.0 %collective-permute-start.11 = (bf16[128,512]{1,0:T(8,128)(2,1)S(1)}, bf16[128,512]{1,0:T(8,128)(2,1)S(1)}, u32[]{:S(2)}, u32[]{:S(2)}) collective-permute-start(bf16[128,512]{1,0:T(8,128)(2,1)S(1)} %get-tuple-element.60), channel_id=1, source_target_pairs={{0,3},{1,0},{2,1},{3,2},{4,7},{5,4},{6,5},{7,6},{8,11},{9,8},{10,9... | collective-permute-start | bytes 393224 | tf_op jit(solution)/shard_map/ppermute | solution.py:20

commit v6 on v3

--- a/solution.py
+++ b/solution.py
@@ -240,10 +240,14 @@
     emit(out, attend(far, q, ext, docs))
 
 
+def half_body(x, gain, out):
+    out[...] = normalize(x[...], gain[...])
+
+
 def last_body(ext_in, owners, xa, xb, gain, wk, wv, cosines, sines, ext, normed_out, late_out):
     _, _, _, far, home = spots()
     rows = chunk_rows(far)
-    normed = normalize_all((xa, xb), gain)
+    normed = jnp.concatenate([xa[...], normalize(xb[...], gain[...])], axis=0)
     normed_out[...] = normed
     parts = kv_parts(normed, wk, wv, cosines[rows], sines[rows])
     put(ext, 2 + far, slice(None), parts)
@@ -400,6 +404,7 @@
     inner = swap(inside_out, 0)
     (q_rest,) = call(rest_q_body, [piece], [normed, w_query, cosines, sines], flops // 2)
     ext, s1 = call(first_body, [slots, piece], [ext, inner, q_near, q_rest, docs], scores, alias=0)
+    (far_a,) = call(half_body, [(CH // 2, wide)], [far_a, gain])
     ext, normed, far = call(
         last_body,
         [slots, (CH, wide), piece],

time: 61 us -> 61.1 us (level)
    pallas_call x11 -> x12, Pallas kernels: 12.1 us -> 12.3 us  [call(): pl.pallas_call(body, out_shape=[o if isinstance(o, jax.ShapeDtypeStruct)...]
  transfers between devices with their start and end apart: 12 -> 12, of which waited for: 4 -> 4; matrix products, arithmetic and copies ran while one was open for 5% -> 4% of each run, Pallas kernels for 24% -> 25%
where the time goes in v6:
time: 61.1 us; the launch traced here: 61 us
  starting transfers between devices  22.6 us (37%)
  waiting for transfers between devices  17.6 us (29%)
  Pallas kernels  17 us (28%)
  other arithmetic  1.69 us (3%)
  local copies, waits for them, and re-layouts  1.06 us (2%)
  between operations  1.02 us (2%)
    ppermute x9, waiting for transfers between devices, ring(): return lax.ppermute(array, 'tp', [(i, (i + by) % n) for i in range(n)])  17.6 us
    pallas_call x12, Pallas kernels, call(): pl.pallas_call(body, out_shape=[o if isinstance(o, jax.ShapeDtypeStruct)...  12.3 us
    ppermute x9, starting transfers between devices, ring(): return lax.ppermute(array, 'tp', [(i, (i + by) % n) for i in range(n)])  11.7 us
    ppermute x2, starting transfers between devices, swap(): return lax.ppermute(array, 'seq', pairs)  6.47 us
    pallas_call x2, Pallas kernels, mover(): pl.pallas_call(body, out_shape=[VM(s, bf) for s in outs], in_specs=[outsi...  4.73 us
    ppermute x1, starting transfers between devices, across(): return lax.ppermute(array, ('seq', 'tp'), pairs)  4.39 us
  transfers between devices with their start and end apart: 12, of which 4 were waited for; matrix products, arithmetic and copies ran while one was open for 4% of the time, Pallas kernels for 25%

profile of v6, /device:TPU:103, one launch (start us, length us, event | category | flops | bytes accessed | tf_op | source)
XLA Modules:
  0.0 61.0 jit_solution(3943396060409261216)
XLA Ops:
  0.6 1.2 %shard_map.94 = (bf16[64,4096]{1,0:T(8,128)(2,1)S(1)}, bf16[64,4096]{1,0:T(8,128)(2,1)S(1)}) custom-call(bf16[128,4096]{1,0:T(8,128)(2,1)} %hidden.1), custom_call_target="tpu_custom_call" | custom-call | bytes 2097152 | tf_op jit(solution)/shard_map/pallas_call | solution.py:354
  1.9 2.8 %collective-permute-start.2 = (bf16[64,4096]{1,0:T(8,128)(2,1)S(1)}, bf16[64,4096]{1,0:T(8,128)(2,1)S(1)}, u32[]{:S(2)}, u32[]{:S(2)}) collective-permute-start(bf16[64,4096]{1,0:T(8,128)(2,1)S(1)} %get-tuple-element.30.xa), channel_id=1, source_target_pairs={{0,3},{1,0},{2,1},{3,2},{4,7},{5,4},{6,5},{7,6},{8,11},{9,8},{10,9... | collective-permute-start | bytes 1572872 | tf_op jit(solution)/shard_map/ppermute | solution.py:20
  4.7 2.7 %collective-permute-start.1 = (bf16[64,4096]{1,0:T(8,128)(2,1)S(1)}, bf16[64,4096]{1,0:T(8,128)(2,1)S(1)}, u32[]{:S(2)}, u32[]{:S(2)}) collective-permute-start(bf16[64,4096]{1,0:T(8,128)(2,1)S(1)} %get-tuple-element.31.xb), channel_id=1, source_target_pairs={{0,3},{1,0},{2,1},{3,2},{4,7},{5,4},{6,5},{7,6},{8,11},{9,8},{10,9... | collective-permute-start | bytes 1572872 | tf_op jit(solution)/shard_map/ppermute | solution.py:20
  7.4 0.7 %broadcast_in_dim.32 = s32[16,32]{1,0:T(8,128)S(1)} broadcast(s32[16]{0:T(128)} %param.13), dimensions={0} | broadcast | bytes 2112 | tf_op jit(solution)/shard_map/broadcast_in_dim | solution.py:378
  8.1 0.1 broadcast_in_dim.33
  8.2 0.7 %subtract_convert_fusion = (f32[512]{0:T(512)S(1)}, s32[512]{0:T(512)S(1)}) fusion(s32[512]{0:T(512)} %param.12, s32[]{:T(128)S(6)} %mul.35), kind=kLoop, calls=%fused_computation.5 | loop fusion | flops 2048 | bytes 6148 | tf_op jit(solution)/shard_map/convert_element_type | solution.py:375
  8.9 0.1 broadcast_in_dim.34.after_too.owners
  9.0 0.1 broadcast_in_dim.31.after.docs
  9.1 3.5 %shard_map.95 = (bf16[4096,512]{1,0:T(8,128)(2,1)S(1)}, bf16[4096,256]{1,0:T(8,128)(2,1)S(1)}, bf16[4096,256]{1,0:T(8,128)(2,1)S(1)}) custom-call(bf16[4096,512]{1,0:T(8,128)(2,1)} %wq.1, bf16[4096,256]{1,0:T(8,128)(2,1)} %wk.1, bf16[4096,256]{1,0:T(8,128)(2,1)} %wv.1, s32[512,128]{1,0:T(8,128)S(1)} %broadcast_in_dim.31.after.docs, ...), custom_call_target="tpu_custom_call" | custom-call | bytes 16777216 | tf_op jit(solution)/shard_map/pallas_call | solution.py:354
  12.7 1.0 %fusion = (f32[512,128]{1,0:T(8,128)S(1)}, f32[512,128]{1,0:T(8,128)S(1)}) fusion(f32[128]{0:T(128)S(1)} %get-tuple-element.61, f32[128]{0:T(128)S(1)} %get-tuple-element.62, f32[512]{0:T(512)S(1)} %get-tuple-element.59), kind=kLoop, calls=%fused_computation.2 | loop fusion | flops 131072 | bytes 527360 | tf_op jit(solution)/shard_map/mul | solution.py:376
  13.7 4.7 %collective-permute-done.la = bf16[64,4096]{1,0:T(8,128)(2,1)S(1)} collective-permute-done((bf16[64,4096]{1,0:T(8,128)(2,1)S(1)}, bf16[64,4096]{1,0:T(8,128)(2,1)S(1)}, u32[]{:S(2)}, u32[]{:S(2)}) %collective-permute-start) | collective-permute-done | bytes 524320 | tf_op jit(solution)/shard_map/ppermute | solution.py:20
  18.4 8.1 %collective-permute-done.1.rb = bf16[64,4096]{1,0:T(8,128)(2,1)S(1)} collective-permute-done((bf16[64,4096]{1,0:T(8,128)(2,1)S(1)}, bf16[64,4096]{1,0:T(8,128)(2,1)S(1)}, u32[]{:S(2)}, u32[]{:S(2)}) %collective-permute-start.1) | collective-permute-done | bytes 524320 | tf_op jit(solution)/shard_map/ppermute | solution.py:20
  26.5 3.4 %collective-permute-start.6 = (bf16[64,4096]{1,0:T(8,128)(2,1)S(1)}, bf16[64,4096]{1,0:T(8,128)(2,1)S(1)}, u32[]{:S(2)}, u32[]{:S(2)}) collective-permute-start(bf16[64,4096]{1,0:T(8,128)(2,1)S(1)} %collective-permute-done.1.rb), channel_id=1, source_target_pairs={{0,3},{1,0},{2,1},{3,2},{4,7},{5,4},{6,5},{7,6},{8,11},{9,8},{10,9... | collective-permute-start | bytes 1572872 | tf_op jit(solution)/shard_map/ppermute | solution.py:20
  29.9 1.6 %shard_map.96 = (bf16[6,128,512]{2,1,0:T(8,128)(2,1)S(1)}, bf16[128,512]{1,0:T(8,128)(2,1)S(1)}) custom-call(bf16[64,4096]{1,0:T(8,128)(2,1)S(1)} %get-tuple-element.30.xa, bf16[64,4096]{1,0:T(8,128)(2,1)S(1)} %get-tuple-element.31.xb, f32[1,4096]{1,0:T(1,128)S(1)} %bitcast.1, bf16[4096,512]{1,0:T(8,128)(2,1)S(1)} %get-tuple-element.32.wq, ...), custom_call_target="tpu_custom_call" | custom-call | flops 1073741824 | bytes 9977856 | tf_op jit(solution)/shard_map/pallas_call | solution.py:47
  31.5 1.6 %shard_map.97 = (bf16[6,128,512]{2,1,0:T(8,128)(2,1)S(1)}, bf16[128,512]{1,0:T(8,128)(2,1)S(1)}) custom-call(bf16[6,128,512]{2,1,0:T(8,128)(2,1)S(1)} %get-tuple-element.35.ext_in, bf16[64,4096]{1,0:T(8,128)(2,1)S(1)} %collective-permute-done.la, bf16[64,4096]{1,0:T(8,128)(2,1)S(1)} %collective-permute-done.1.rb, ...), custom_call_target="tpu_custom_call", output_to_operand_aliasing={{0}: (0, {})} | custom-call | flops 1073741824 | bytes 10764288 | tf_op jit(solution)/shard_map/pallas_call | solution.py:47
  33.2 1.1 %shard_map.98 = (bf16[6,128,512]{2,1,0:T(8,128)(2,1)S(1)}, bf16[128,4096]{1,0:T(8,128)(2,1)S(1)}, bf16[272,512]{1,0:T(8,128)(2,1)S(1)}, bf16[272,512]{1,0:T(8,128)(2,1)S(1)}) custom-call(bf16[6,128,512]{2,1,0:T(8,128)(2,1)S(1)} %get-tuple-element.36.ext_in, s32[512,128]{1,0:T(8,128)S(1)} %broadcast_in_dim.34.after_too.owners, ...), custom_call_target="tpu_custom_call", output_to_operand_aliasing={{0}: (0, {})} | custom-call | flops 536870912 | bytes 6832128 | tf_op jit(solution)/shard_map/pallas_call | solution.py:47
  34.3 1.9 %collective-permute-start.4 = (bf16[272,512]{1,0:T(8,128)(2,1)S(1)}, bf16[272,512]{1,0:T(8,128)(2,1)S(1)}, u32[]{:S(2)}, u32[]{:S(2)}) collective-permute-start(bf16[272,512]{1,0:T(8,128)(2,1)S(1)} %get-tuple-element.38), channel_id=1, source_target_pairs={{0,4},{4,0},{8,12},{12,8},{16,20},{20,16},{24,28},{28,24},{32,36},... | collective-permute-start | bytes 835592 | tf_op jit(solution)/shard_map/ppermute | solution.py:32
  36.2 4.6 %collective-permute-start.7 = (bf16[272,512]{1,0:T(8,128)(2,1)S(1)}, bf16[272,512]{1,0:T(8,128)(2,1)S(1)}, u32[]{:S(2)}, u32[]{:S(2)}) collective-permute-start(bf16[272,512]{1,0:T(8,128)(2,1)S(1)} %get-tuple-element.43), channel_id=1, source_target_pairs={{4,8},{8,4},{12,16},{16,12},{20,24},{24,20},{28,32},{32,28},{36,40... | collective-permute-start | bytes 835592 | tf_op jit(solution)/shard_map/ppermute | solution.py:32
  40.8 0.8 %shard_map.99.q_rest = bf16[128,512]{1,0:T(8,128)(2,1)S(1)} custom-call(bf16[128,4096]{1,0:T(8,128)(2,1)S(1)} %get-tuple-element.40.normed, bf16[4096,512]{1,0:T(8,128)(2,1)S(1)} %get-tuple-element.32.wq, f32[512,128]{1,0:T(8,128)S(1)} %get-tuple-element.58.cosines, f32[512,128]{1,0:T(8,128)S(1)} %get-tuple-element.57.sines), custom_call_target="tpu_custom_call" | custom-call | flops 536870912 | bytes 5767168 | tf_op jit(solution)/shard_map/pallas_call | solution.py:47
  41.6 1.2 %shard_map.100 = (bf16[6,128,512]{2,1,0:T(8,128)(2,1)S(1)}, bf16[128,512]{1,0:T(8,128)(2,1)S(1)}) custom-call(bf16[6,128,512]{2,1,0:T(8,128)(2,1)S(1)} %get-tuple-element.37.ext_in, bf16[272,512]{1,0:T(8,128)(2,1)S(1)} %collective-permute-done.4.inner, bf16[128,512]{1,0:T(8,128)(2,1)S(1)} %get-tuple-element.39.q_near, ...), custom_call_target="tpu_custom_call", output_to_operand_aliasing={{0}: (0, {})} | custom-call | flops 100663296 | bytes 1589248 | tf_op jit(solution)/shard_map/pallas_call | solution.py:47
  42.8 0.3 shard_map.101.xa
  43.1 1.0 %shard_map.102 = (bf16[6,128,512]{2,1,0:T(8,128)(2,1)S(1)}, bf16[128,4096]{1,0:T(8,128)(2,1)S(1)}, bf16[128,512]{1,0:T(8,128)(2,1)S(1)}) custom-call(bf16[6,128,512]{2,1,0:T(8,128)(2,1)S(1)} %get-tuple-element.41.ext_in, s32[512,128]{1,0:T(8,128)S(1)} %broadcast_in_dim.34.after_too.owners, ...), custom_call_target="tpu_custom_call", output_to_operand_aliasing={{0}: (0, {})} | custom-call | flops 536870912 | bytes 6832128 | tf_op jit(solution)/shard_map/pallas_call | solution.py:47
  44.1 4.4 %collective-permute-start.8 = (bf16[128,512]{1,0:T(8,128)(2,1)S(1)}, bf16[128,512]{1,0:T(8,128)(2,1)S(1)}, u32[]{:S(2)}, u32[]{:S(2)}) collective-permute-start(bf16[128,512]{1,0:T(8,128)(2,1)S(1)} %get-tuple-element.46), channel_id=1, source_target_pairs={{0,4},{1,5},{4,8},{5,9},{6,2},{8,12},{9,13},{10,6},{12,16},{13,17}... | collective-permute-start | bytes 393224 | tf_op jit(solution)/shard_map/ppermute | solution.py:26
  48.5 1.7 %shard_map.103 = (bf16[6,128,512]{2,1,0:T(8,128)(2,1)S(1)}, bf16[128,512]{1,0:T(8,128)(2,1)S(1)}) custom-call(bf16[6,128,512]{2,1,0:T(8,128)(2,1)S(1)} %get-tuple-element.42.ext_in, bf16[272,512]{1,0:T(8,128)(2,1)S(1)} %collective-permute-done.7.outer, bf16[128,4096]{1,0:T(8,128)(2,1)S(1)} %get-tuple-element.44.normed, ...), custom_call_target="tpu_custom_call", output_to_operand_aliasing={{0}: (0, {})} | custom-call | flops 1073741824 | bytes 7094272 | tf_op jit(solution)/shard_map/pallas_call | solution.py:47
  50.3 0.1 collective-permute-start.9
  50.4 0.1 collective-permute-start.10
  50.5 1.0 %shard_map.104 = (bf16[6,128,512]{2,1,0:T(8,128)(2,1)S(1)}, bf16[128,512]{1,0:T(8,128)(2,1)S(1)}) custom-call(bf16[6,128,512]{2,1,0:T(8,128)(2,1)S(1)} %get-tuple-element.45.ext_in.ext, bf16[128,512]{1,0:T(8,128)(2,1)S(1)} %collective-permute-done.8.late, bf16[128,512]{1,0:T(8,128)(2,1)S(1)} %get-tuple-element.39.q_near, ...), custom_call_target="tpu_custom_call", output_to_operand_aliasing={{0}: (0, {})} | custom-call | flops 100663296 | bytes 1441792 | tf_op jit(solution)/shard_map/pallas_call | solution.py:47
  51.5 2.6 %collective-permute-start.11 = (bf16[128,512]{1,0:T(8,128)(2,1)S(1)}, bf16[128,512]{1,0:T(8,128)(2,1)S(1)}, u32[]{:S(2)}, u32[]{:S(2)}) collective-permute-start(bf16[128,512]{1,0:T(8,128)(2,1)S(1)} %get-tuple-element.54), channel_id=1, source_target_pairs={{0,3},{1,0},{2,1},{3,2},{4,7},{5,4},{6,5},{7,6},{8,11},{9,8},{10,9... | collective-permute-start | bytes 393224 | tf_op jit(solution)/shard_map/ppermute | solution.py:20
  54.1 1.1 %shard_map.105 = (bf16[128,512]{1,0:T(8,128)(2,1)S(1)}, bf16[768,256]{1,0:T(8,128)(2,1)}, bf16[768,256]{1,0:T(8,128)(2,1)}) custom-call(bf16[6,128,512]{2,1,0:T(8,128)(2,1)S(1)} %get-tuple-element.47.ext, s32[512,128]{1,0:T(8,128)S(1)} %broadcast_in_dim.34.after_too.owners, bf16[128,512]{1,0:T(8,128)(2,1)S(1)} %collective-permute-done.8.late, ...), custom_call_target="tpu_custom_call" | custom-call | flops 100663296 | bytes 2129920 | tf_op jit(solution)/shard_map/pallas_call | solution.py:47
  55.2 3.8 %collective-permute-done.9.r1 = bf16[128,512]{1,0:T(8,128)(2,1)S(1)} collective-permute-done((bf16[128,512]{1,0:T(8,128)(2,1)S(1)}, bf16[128,512]{1,0:T(8,128)(2,1)S(1)}, u32[]{:S(2)}, u32[]{:S(2)}) %collective-permute-start.9) | collective-permute-done | bytes 131104 | tf_op jit(solution)/shard_map/ppermute | solution.py:20
  59.1 0.9 %collective-permute-done.11.r3 = bf16[128,512]{1,0:T(8,128)(2,1)S(1)} collective-permute-done((bf16[128,512]{1,0:T(8,128)(2,1)S(1)}, bf16[128,512]{1,0:T(8,128)(2,1)S(1)}, u32[]{:S(2)}, u32[]{:S(2)}) %collective-permute-start.11) | collective-permute-done | bytes 131104 | tf_op jit(solution)/shard_map/ppermute | solution.py:20
  60.0 0.8 %shard_map.107 = bf16[128,2048]{1,0:T(8,128)(2,1)} custom-call(bf16[128,512]{1,0:T(8,128)(2,1)S(1)} %get-tuple-element.49.s0, bf16[128,512]{1,0:T(8,128)(2,1)S(1)} %collective-permute-done.9.r1, bf16[128,512]{1,0:T(8,128)(2,1)S(1)} %collective-permute-done.10.r2, bf16[128,512]{1,0:T(8,128)(2,1)S(1)} %collective-permute-done.11.r3), custom_call_target="tpu_custom_call" | custom-call | bytes 524288 | tf_op jit(solution)/shard_map/pallas_call | solution.py:47
  (15 shorter events, 0.1 us)
Async XLA Ops:
  1.9 31.3 %collective-permute-start.2 = (bf16[64,4096]{1,0:T(8,128)(2,1)S(1)}, bf16[64,4096]{1,0:T(8,128)(2,1)S(1)}, u32[]{:S(2)}, u32[]{:S(2)}) collective-permute-start(bf16[64,4096]{1,0:T(8,128)(2,1)S(1)} %get-tuple-element.30.xa), channel_id=1, source_target_pairs={{0,3},{1,0},{2,1},{3,2},{4,7},{5,4},{6,5},{7,6},{8,11},{9,8},{10,9... | collective-permute-start | bytes 1572872 | tf_op jit(solution)/shard_map/ppermute | solution.py:20
  4.7 13.7 %collective-permute-start = (bf16[64,4096]{1,0:T(8,128)(2,1)S(1)}, bf16[64,4096]{1,0:T(8,128)(2,1)S(1)}, u32[]{:S(2)}, u32[]{:S(2)}) collective-permute-start(bf16[64,4096]{1,0:T(8,128)(2,1)S(1)} %get-tuple-element.30.xa), channel_id=1, source_target_pairs={{0,1},{1,2},{2,3},{3,0},{4,5},{5,6},{6,7},{7,4},{8,9},{9,10},{10,1... | collective-permute-start | bytes 1572872 | tf_op jit(solution)/shard_map/ppermute | solution.py:20
  4.7 28.5 %collective-permute-start.3 = (bf16[64,4096]{1,0:T(8,128)(2,1)S(1)}, bf16[64,4096]{1,0:T(8,128)(2,1)S(1)}, u32[]{:S(2)}, u32[]{:S(2)}) collective-permute-start(bf16[64,4096]{1,0:T(8,128)(2,1)S(1)} %get-tuple-element.31.xb), channel_id=1, source_target_pairs={{0,1},{1,2},{2,3},{3,0},{4,5},{5,6},{6,7},{7,4},{8,9},{9,10},{10,1... | collective-permute-start | bytes 1572872 | tf_op jit(solution)/shard_map/ppermute | solution.py:20
  4.7 21.8 %collective-permute-start.1 = (bf16[64,4096]{1,0:T(8,128)(2,1)S(1)}, bf16[64,4096]{1,0:T(8,128)(2,1)S(1)}, u32[]{:S(2)}, u32[]{:S(2)}) collective-permute-start(bf16[64,4096]{1,0:T(8,128)(2,1)S(1)} %get-tuple-element.31.xb), channel_id=1, source_target_pairs={{0,3},{1,0},{2,1},{3,2},{4,7},{5,4},{6,5},{7,6},{8,11},{9,8},{10,9... | collective-permute-start | bytes 1572872 | tf_op jit(solution)/shard_map/ppermute | solution.py:20
  9.1 20.8 %copy-start = (f32[4096]{0:T(1024)S(1)}, f32[4096]{0:T(1024)}, u32[]{:S(2)}) copy-start(f32[4096]{0:T(1024)} %param.8) | copy-start | bytes 49156
  18.4 24.4 %collective-permute-start.5 = (bf16[64,4096]{1,0:T(8,128)(2,1)S(1)}, bf16[64,4096]{1,0:T(8,128)(2,1)S(1)}, u32[]{:S(2)}, u32[]{:S(2)}) collective-permute-start(bf16[64,4096]{1,0:T(8,128)(2,1)S(1)} %collective-permute-done.la), channel_id=1, source_target_pairs={{0,1},{1,2},{2,3},{3,0},{4,5},{5,6},{6,7},{7,4},{8,9},{9,10},{10,1... | collective-permute-start | bytes 1572872 | tf_op jit(solution)/shard_map/ppermute | solution.py:20
  26.5 16.6 %collective-permute-start.6 = (bf16[64,4096]{1,0:T(8,128)(2,1)S(1)}, bf16[64,4096]{1,0:T(8,128)(2,1)S(1)}, u32[]{:S(2)}, u32[]{:S(2)}) collective-permute-start(bf16[64,4096]{1,0:T(8,128)(2,1)S(1)} %collective-permute-done.1.rb), channel_id=1, source_target_pairs={{0,3},{1,0},{2,1},{3,2},{4,7},{5,4},{6,5},{7,6},{8,11},{9,8},{10,9... | collective-permute-start | bytes 1572872 | tf_op jit(solution)/shard_map/ppermute | solution.py:20
  34.3 7.3 %collective-permute-start.4 = (bf16[272,512]{1,0:T(8,128)(2,1)S(1)}, bf16[272,512]{1,0:T(8,128)(2,1)S(1)}, u32[]{:S(2)}, u32[]{:S(2)}) collective-permute-start(bf16[272,512]{1,0:T(8,128)(2,1)S(1)} %get-tuple-element.38), channel_id=1, source_target_pairs={{0,4},{4,0},{8,12},{12,8},{16,20},{20,16},{24,28},{28,24},{32,36},... | collective-permute-start | bytes 835592 | tf_op jit(solution)/shard_map/ppermute | solution.py:32
  36.2 12.3 %collective-permute-start.7 = (bf16[272,512]{1,0:T(8,128)(2,1)S(1)}, bf16[272,512]{1,0:T(8,128)(2,1)S(1)}, u32[]{:S(2)}, u32[]{:S(2)}) collective-permute-start(bf16[272,512]{1,0:T(8,128)(2,1)S(1)} %get-tuple-element.43), channel_id=1, source_target_pairs={{4,8},{8,4},{12,16},{16,12},{20,24},{24,20},{28,32},{32,28},{36,40... | collective-permute-start | bytes 835592 | tf_op jit(solution)/shard_map/ppermute | solution.py:32
  44.1 6.4 %collective-permute-start.8 = (bf16[128,512]{1,0:T(8,128)(2,1)S(1)}, bf16[128,512]{1,0:T(8,128)(2,1)S(1)}, u32[]{:S(2)}, u32[]{:S(2)}) collective-permute-start(bf16[128,512]{1,0:T(8,128)(2,1)S(1)} %get-tuple-element.46), channel_id=1, source_target_pairs={{0,4},{1,5},{4,8},{5,9},{6,2},{8,12},{9,13},{10,6},{12,16},{13,17}... | collective-permute-start | bytes 393224 | tf_op jit(solution)/shard_map/ppermute | solution.py:26
  50.3 8.8 %collective-permute-start.9 = (bf16[128,512]{1,0:T(8,128)(2,1)S(1)}, bf16[128,512]{1,0:T(8,128)(2,1)S(1)}, u32[]{:S(2)}, u32[]{:S(2)}) collective-permute-start(bf16[128,512]{1,0:T(8,128)(2,1)S(1)} %get-tuple-element.52), channel_id=1, source_target_pairs={{0,1},{1,2},{2,3},{3,0},{4,5},{5,6},{6,7},{7,4},{8,9},{9,10},{10,1... | collective-permute-start | bytes 393224 | tf_op jit(solution)/shard_map/ppermute | solution.py:20
  50.4 8.7 %collective-permute-start.10 = (bf16[128,512]{1,0:T(8,128)(2,1)S(1)}, bf16[128,512]{1,0:T(8,128)(2,1)S(1)}, u32[]{:S(2)}, u32[]{:S(2)}) collective-permute-start(bf16[128,512]{1,0:T(8,128)(2,1)S(1)} %get-tuple-element.53), channel_id=1, source_target_pairs={{0,2},{1,3},{2,0},{3,1},{4,6},{5,7},{6,4},{7,5},{8,10},{9,11},{10,... | collective-permute-start | bytes 393224 | tf_op jit(solution)/shard_map/ppermute | solution.py:20
  51.5 8.5 %collective-permute-start.11 = (bf16[128,512]{1,0:T(8,128)(2,1)S(1)}, bf16[128,512]{1,0:T(8,128)(2,1)S(1)}, u32[]{:S(2)}, u32[]{:S(2)}) collective-permute-start(bf16[128,512]{1,0:T(8,128)(2,1)S(1)} %get-tuple-element.54), channel_id=1, source_target_pairs={{0,3},{1,0},{2,1},{3,2},{4,7},{5,4},{6,5},{7,6},{8,11},{9,8},{10,9... | collective-permute-start | bytes 393224 | tf_op jit(solution)/shard_map/ppermute | solution.py:20
